TPU v7x, 32 devices: a whole 2x2x4 slice. The times are simulated.
32 devices in a mesh: seq: 2 (over y), dp: 16 (over z, x, core).
Axes of the slice: x: 2, y: 2, z: 4, core: 2. Of those that a mesh axis runs over, the one named last changes fastest.
Arguments:
- incoming_activations: bfloat16 [16, 2048, 768], P('dp', 'seq'), may hold values from -6 to 6
- upstream_derivative: bfloat16 [16, 2048, 768], P('dp', 'seq'), may hold values from -6 to 6
- grid_coordinates: int32 [16, 2048], P('dp'), may hold values from 0 to 511, as said below
- word_segment_ids: int32 [16, 2048], P('dp'), may hold values from 0 to 7, never falling along the last dimension, each value on 1 to 384 neighbouring positions
- asking_matrix: bfloat16 [768, 768], P(('seq', 'dp')), may hold values from -0.21875 to 0.21875
- asking_shift: bfloat16 [768], P(('seq', 'dp')), may hold values from -4 to 4
- lookup_matrix: bfloat16 [768, 768], P(('seq', 'dp')), may hold values from -0.21875 to 0.21875
- content_matrix: bfloat16 [768, 768], P(('seq', 'dp')), may hold values from -0.21875 to 0.21875
- content_shift: bfloat16 [768], P(('seq', 'dp')), may hold values from -4 to 4
- mixing_result_matrix: bfloat16 [768, 768], P(('seq', 'dp')), may hold values from -3.5 to 3.5
- mixing_result_shift: bfloat16 [768], P(('seq', 'dp')), may hold values from -4 to 4
- post_mixing_scaling: bfloat16 [768], P(('seq', 'dp')), may hold values from 0.5 to 1.5
- post_mixing_offset: bfloat16 [768], P(('seq', 'dp')), may hold values from -4 to 4
- expand_matrix: bfloat16 [768, 3072], P(('seq', 'dp')), may hold values from -0.21875 to 0.21875
- expand_shift: bfloat16 [3072], P(('seq', 'dp')), may hold values from -4 to 4
- contract_matrix: bfloat16 [3072, 768], P(('seq', 'dp')), may hold values from -0.109375 to 0.109375
- contract_shift: bfloat16 [768], P(('seq', 'dp')), may hold values from -4 to 4
- post_perceptron_scaling: bfloat16 [768], P(('seq', 'dp')), may hold values from 0.5 to 1.5
- post_perceptron_offset: bfloat16 [768], P(('seq', 'dp')), may hold values from -4 to 4
- pair_gate_scores: float32 [12, 512, 512], P(None, ('seq', 'dp')), may hold values from -6 to 6
- gate_random_jitter: float32 [12, 512, 512], P(None, ('seq', 'dp')), may hold values from -6 to 6
- softening_scale: float32 [12], replicated, may hold values from 0.5 to 2
Outputs:
- layer_out: bfloat16 [16, 2048, 768], P('dp', 'seq')
- input_grad: float32 [16, 2048, 768], P('dp', 'seq')
- grad_query_weight: float32 [768, 768], P(('seq', 'dp'))
- grad_query_bias: float32 [768], P(('seq', 'dp'))
- grad_key_weight: float32 [768, 768], P(('seq', 'dp'))
- grad_value_weight: float32 [768, 768], P(('seq', 'dp'))
- grad_value_bias: float32 [768], P(('seq', 'dp'))
- grad_output_weight: float32 [768, 768], P(('seq', 'dp'))
- grad_output_bias: float32 [768], P(('seq', 'dp'))
- grad_first_gain: float32 [768], P(('seq', 'dp'))
- grad_first_shift: float32 [768], P(('seq', 'dp'))
- grad_inner_weight: float32 [768, 3072], P(('seq', 'dp'))
- grad_inner_bias: float32 [3072], P(('seq', 'dp'))
- grad_outer_weight: float32 [3072, 768], P(('seq', 'dp'))
- grad_outer_bias: float32 [768], P(('seq', 'dp'))
- grad_second_gain: float32 [768], P(('seq', 'dp'))
- grad_second_shift: float32 [768], P(('seq', 'dp'))
- mask_logits_gradient: float32 [12, 512, 512], P(None, ('seq', 'dp'))
Inputs may be any that keep to these rules, and one draw needn't show every extreme that they name: `grid_coordinates`: in each sequence the positions count up by one from a start of the sequence's own, modulo 512. `word_segment_ids`: in each sequence the numbers never fall and every number appears on consecutive positions, at most 384 of them, one on exactly that many.
All inputs are finite; a program needn't handle non-finite values.
Results may differ from a plain program's by a relative error of at most 0.015.
Values may be sent and summed in bfloat16 or wider, within the bound.
No kernel may reach another device: no remote copies, remote signals or barrier semaphores. Data moves between devices by JAX's collectives and lax.ppermute only.
A program may use at most 320 MiB of HBM per device.

v0:
```python
import math

import jax
import jax.numpy as jnp
from jax import lax
from jax.sharding import PartitionSpec as P

EPSILON = 1e-06
NEGATIVE = -1e30


def matmul(left_side, right_side):
    return jnp.dot(left_side, right_side, preferred_element_type=jnp.float32)


def contract_rows(left_side, right_side):
    return jnp.einsum("rd,re->de", left_side, right_side, preferred_element_type=jnp.float32)


def times_transpose(left_side, right_side):
    return jnp.einsum("re,de->rd", left_side, right_side, preferred_element_type=jnp.float32)


def norm_forward(values, norm_gain, norm_shift):
    center = values - jnp.mean(values, axis=-1, keepdims=True)
    rstdev = lax.rsqrt(jnp.mean(center * center, axis=-1, keepdims=True) + EPSILON)
    normed = center * rstdev
    return (normed * norm_gain + norm_shift, normed, rstdev)


def norm_backward(gradient, normed, rstdev, norm_gain):
    scaled = gradient * norm_gain
    back = rstdev * (
        scaled
        - jnp.mean(scaled, axis=-1, keepdims=True)
        - normed * jnp.mean(scaled * normed, axis=-1, keepdims=True)
    )
    return (back, jnp.sum(gradient * normed, axis=0), jnp.sum(gradient, axis=0))


def split_groups(matrix, group_count, group_size):
    row_count = matrix.shape[0]
    head_size = matrix.shape[1] // (group_count * group_size)
    return matrix.reshape(row_count, group_count, group_size, head_size).transpose(1, 0, 2, 3)


def join_groups(stacked):
    row_count = stacked.shape[1]
    return stacked.transpose(1, 0, 2, 3).reshape(row_count, -1)


def tiled_table(table_group, row_shift, col_shift, row_count, col_count):
    table_size = table_group.shape[1]
    rolled = jnp.roll(jnp.roll(table_group, -row_shift, axis=1), -col_shift, axis=2)
    return jnp.tile(rolled, (1, row_count // table_size, col_count // table_size))


def folded_table(grad_scores, row_shift, col_shift, table_size):
    group_width, row_count, col_count = grad_scores.shape
    folded = (
        grad_scores.astype(jnp.float32)
        .reshape(
            group_width, row_count // table_size, table_size, col_count // table_size, table_size
        )
        .sum(axis=(1, 3))
    )
    return jnp.roll(jnp.roll(folded, row_shift, axis=1), col_shift, axis=2)


def group_scores(query_group, keys_group, table_group, row_shift, col_shift, allowed, score_scale):
    logits = (
        jnp.einsum("qgd,kgd->gqk", query_group, keys_group, preferred_element_type=jnp.float32)
        * score_scale
    )
    picked = tiled_table(
        table_group, row_shift, col_shift, query_group.shape[0], keys_group.shape[0]
    )
    logits = logits + 4.0 * picked.astype(jnp.float32)
    return jnp.where(allowed[None], logits, NEGATIVE)


def body(
    incoming_activations,
    upstream_derivative,
    grid_coordinates,
    word_segment_ids,
    asking_matrix,
    asking_shift,
    lookup_matrix,
    content_matrix,
    content_shift,
    mixing_result_matrix,
    mixing_result_shift,
    post_mixing_scaling,
    post_mixing_offset,
    expand_matrix,
    expand_shift,
    contract_matrix,
    contract_shift,
    post_perceptron_scaling,
    post_perceptron_offset,
    pair_gate_scores,
    gate_random_jitter,
    softening_scale,
):
    focus_tally = softening_scale.shape[0]
    model_width = incoming_activations.shape[2]
    local_rows = incoming_activations.shape[1]
    table_size = pair_gate_scores.shape[2]
    head_size = model_width // focus_tally
    score_scale = 1.0 / math.sqrt(head_size)
    group_size = 2
    group_count = focus_tally // group_size
    row_start = lax.axis_index("seq") * local_rows
    pos_cols = grid_coordinates[0]
    blocks_cols = word_segment_ids[0]
    col_shift = pos_cols[0]
    row_shift = lax.dynamic_slice_in_dim(pos_cols, row_start, 1, 0)[0]
    blocks_rows = lax.dynamic_slice_in_dim(blocks_cols, row_start, local_rows, 0)
    allowed = blocks_cols[None, :] <= blocks_rows[:, None]
    inputs = incoming_activations[0]
    smoothed_gate = jax.nn.sigmoid(
        (pair_gate_scores + gate_random_jitter) / softening_scale[:, None, None]
    )
    mask_low = smoothed_gate.astype(jnp.bfloat16)
    forward_full = (
        lax.all_gather(asking_matrix, ("seq", "dp"), axis=0, tiled=True),
        lax.all_gather(lookup_matrix, ("seq", "dp"), axis=0, tiled=True),
        lax.all_gather(content_matrix, ("seq", "dp"), axis=0, tiled=True),
        lax.all_gather(mixing_result_matrix, ("seq", "dp"), axis=0, tiled=True),
        lax.all_gather(expand_matrix, ("seq", "dp"), axis=0, tiled=True),
        lax.all_gather(contract_matrix, ("seq", "dp"), axis=0, tiled=True),
        lax.all_gather(asking_shift, ("seq", "dp"), axis=0, tiled=True),
        lax.all_gather(content_shift, ("seq", "dp"), axis=0, tiled=True),
        lax.all_gather(mixing_result_shift, ("seq", "dp"), axis=0, tiled=True),
        lax.all_gather(post_mixing_scaling, ("seq", "dp"), axis=0, tiled=True),
        lax.all_gather(post_mixing_offset, ("seq", "dp"), axis=0, tiled=True),
        lax.all_gather(expand_shift, ("seq", "dp"), axis=0, tiled=True),
        lax.all_gather(contract_shift, ("seq", "dp"), axis=0, tiled=True),
        lax.all_gather(post_perceptron_scaling, ("seq", "dp"), axis=0, tiled=True),
        lax.all_gather(post_perceptron_offset, ("seq", "dp"), axis=0, tiled=True),
        lax.all_gather(mask_low, ("seq", "dp"), axis=1, tiled=True),
    )
    (
        query_matrix,
        key_matrix,
        value_matrix,
        output_matrix,
        inner_matrix,
        outer_matrix,
        query_offset,
        value_offset,
        output_offset,
        first_scale,
        first_offset,
        inner_offset,
        outer_offset,
        second_scale,
        second_offset,
        location_gate_grid,
    ) = forward_full
    queries = (matmul(inputs, query_matrix) + query_offset.astype(jnp.float32)).astype(jnp.bfloat16)
    keys_local = matmul(inputs, key_matrix).astype(jnp.bfloat16)
    values_local = (matmul(inputs, value_matrix) + value_offset.astype(jnp.float32)).astype(
        jnp.bfloat16
    )
    keys_all, values_all = (
        lax.all_gather(keys_local, "seq", axis=0, tiled=True),
        lax.all_gather(values_local, "seq", axis=0, tiled=True),
    )
    query_groups = split_groups(queries, group_count, group_size)
    key_groups = split_groups(keys_all, group_count, group_size)
    value_groups = split_groups(values_all, group_count, group_size)
    mask_groups = location_gate_grid.reshape(group_count, group_size, table_size, table_size)

    def attend(unused_state, members):
        query_group, keys_group, values_group, table_group = members
        logits = group_scores(
            query_group, keys_group, table_group, row_shift, col_shift, allowed, score_scale
        )
        row_peak = jnp.max(logits, axis=-1, keepdims=True)
        exponent = jnp.exp(logits - row_peak)
        row_total = jnp.sum(exponent, axis=-1, keepdims=True)
        softmax_low = (exponent / row_total).astype(jnp.bfloat16)
        mixture = jnp.einsum(
            "gqk,kgd->qgd", softmax_low, values_group, preferred_element_type=jnp.float32
        ).astype(jnp.bfloat16)
        return (unused_state, (mixture, (row_peak + jnp.log(row_total))[..., 0]))

    unused_state, (attended_groups, logsum) = lax.scan(
        attend, jnp.zeros((), jnp.float32), (query_groups, key_groups, value_groups, mask_groups)
    )
    attended = join_groups(attended_groups)
    projected = matmul(attended, output_matrix) + output_offset.astype(jnp.float32)
    first_out, first_normed, first_rstdev = norm_forward(
        inputs.astype(jnp.float32) + projected,
        first_scale.astype(jnp.float32),
        first_offset.astype(jnp.float32),
    )
    first_low = first_out.astype(jnp.bfloat16)
    inner_pre = matmul(first_low, inner_matrix) + inner_offset.astype(jnp.float32)
    active_low = jax.nn.gelu(inner_pre).astype(jnp.bfloat16)
    outer_pre = matmul(active_low, outer_matrix) + outer_offset.astype(jnp.float32)
    second, second_normed, second_rstdev = norm_forward(
        first_out + outer_pre, second_scale.astype(jnp.float32), second_offset.astype(jnp.float32)
    )
    layer_out = second.astype(jnp.bfloat16)
    backward_full = (
        lax.all_gather(asking_matrix, ("seq", "dp"), axis=0, tiled=True),
        lax.all_gather(lookup_matrix, ("seq", "dp"), axis=0, tiled=True),
        lax.all_gather(content_matrix, ("seq", "dp"), axis=0, tiled=True),
        lax.all_gather(mixing_result_matrix, ("seq", "dp"), axis=0, tiled=True),
        lax.all_gather(expand_matrix, ("seq", "dp"), axis=0, tiled=True),
        lax.all_gather(contract_matrix, ("seq", "dp"), axis=0, tiled=True),
        lax.all_gather(asking_shift, ("seq", "dp"), axis=0, tiled=True),
        lax.all_gather(content_shift, ("seq", "dp"), axis=0, tiled=True),
        lax.all_gather(mixing_result_shift, ("seq", "dp"), axis=0, tiled=True),
        lax.all_gather(post_mixing_scaling, ("seq", "dp"), axis=0, tiled=True),
        lax.all_gather(post_mixing_offset, ("seq", "dp"), axis=0, tiled=True),
        lax.all_gather(expand_shift, ("seq", "dp"), axis=0, tiled=True),
        lax.all_gather(contract_shift, ("seq", "dp"), axis=0, tiled=True),
        lax.all_gather(post_perceptron_scaling, ("seq", "dp"), axis=0, tiled=True),
        lax.all_gather(post_perceptron_offset, ("seq", "dp"), axis=0, tiled=True),
        lax.all_gather(mask_low, ("seq", "dp"), axis=1, tiled=True),
    )
    (
        query_matrix,
        key_matrix,
        value_matrix,
        output_matrix,
        inner_matrix,
        outer_matrix,
        query_offset,
        value_offset,
        output_offset,
        first_scale,
        first_offset,
        inner_offset,
        outer_offset,
        second_scale,
        second_offset,
        location_gate_grid,
    ) = backward_full
    mask_groups = location_gate_grid.reshape(group_count, group_size, table_size, table_size)
    grad_out = upstream_derivative[0].astype(jnp.float32)
    grad_sum, grad_second_gain, grad_second_shift = norm_backward(
        grad_out, second_normed, second_rstdev, second_scale.astype(jnp.float32)
    )
    grad_outer_low = grad_sum.astype(jnp.bfloat16)
    grad_outer_weight = contract_rows(active_low, grad_outer_low)
    grad_outer_bias = jnp.sum(grad_outer_low.astype(jnp.float32), axis=0)
    grad_active = times_transpose(grad_outer_low, outer_matrix)
    unused_value, gelu_pull = jax.vjp(jax.nn.gelu, inner_pre)
    grad_inner_low = gelu_pull(grad_active)[0].astype(jnp.bfloat16)
    grad_inner_weight = contract_rows(first_low, grad_inner_low)
    grad_inner_bias = jnp.sum(grad_inner_low.astype(jnp.float32), axis=0)
    grad_first = grad_sum + times_transpose(grad_inner_low, inner_matrix)
    grad_summed, grad_first_gain, grad_first_shift = norm_backward(
        grad_first, first_normed, first_rstdev, first_scale.astype(jnp.float32)
    )
    grad_proj_low = grad_summed.astype(jnp.bfloat16)
    grad_output_weight = contract_rows(attended, grad_proj_low)
    grad_output_bias = jnp.sum(grad_proj_low.astype(jnp.float32), axis=0)
    grad_attended = times_transpose(grad_proj_low, output_matrix).astype(jnp.bfloat16)

    def attend_back(unused_state, members):
        query_group, keys_group, values_group, table_group, logsum_group, grad_group = members
        logits = group_scores(
            query_group, keys_group, table_group, row_shift, col_shift, allowed, score_scale
        )
        softmax = jnp.exp(logits - logsum_group[..., None])
        grad_probs = jnp.einsum(
            "qgd,kgd->gqk", grad_group, values_group, preferred_element_type=jnp.float32
        )
        row_inner = jnp.sum(softmax * grad_probs, axis=-1, keepdims=True)
        grad_scores = (softmax * (grad_probs - row_inner)).astype(jnp.bfloat16)
        grad_query = (
            jnp.einsum("gqk,kgd->qgd", grad_scores, keys_group, preferred_element_type=jnp.float32)
            * score_scale
        )
        grad_keys = (
            jnp.einsum("gqk,qgd->kgd", grad_scores, query_group, preferred_element_type=jnp.float32)
            * score_scale
        )
        grad_values = jnp.einsum(
            "gqk,qgd->kgd",
            softmax.astype(jnp.bfloat16),
            grad_group,
            preferred_element_type=jnp.float32,
        )
        grad_table = 4.0 * folded_table(grad_scores, row_shift, col_shift, table_group.shape[1])
        return (unused_state, (grad_query.astype(jnp.bfloat16), grad_keys, grad_values, grad_table))

    unused_state, (grad_query_groups, grad_key_groups, grad_value_groups, grad_tables) = lax.scan(
        attend_back,
        jnp.zeros((), jnp.float32),
        (
            query_groups,
            key_groups,
            value_groups,
            mask_groups,
            logsum,
            split_groups(grad_attended, group_count, group_size),
        ),
    )
    key_sums, value_sums = (
        lax.psum_scatter(join_groups(grad_key_groups), "seq", scatter_dimension=0, tiled=True),
        lax.psum_scatter(join_groups(grad_value_groups), "seq", scatter_dimension=0, tiled=True),
    )
    grad_keys_low = key_sums.astype(jnp.bfloat16)
    grad_values_low = value_sums.astype(jnp.bfloat16)
    grad_queries_low = join_groups(grad_query_groups)
    gate_derivative_rule = grad_tables.reshape(focus_tally, table_size, table_size)
    grad_query_weight = contract_rows(inputs, grad_queries_low)
    grad_query_bias = jnp.sum(grad_queries_low.astype(jnp.float32), axis=0)
    grad_key_weight = contract_rows(inputs, grad_keys_low)
    grad_value_weight = contract_rows(inputs, grad_values_low)
    grad_value_bias = jnp.sum(grad_values_low.astype(jnp.float32), axis=0)
    input_grad = (
        grad_summed
        + times_transpose(grad_queries_low, query_matrix)
        + times_transpose(grad_keys_low, key_matrix)
        + times_transpose(grad_values_low, value_matrix)
    )
    (
        grad_query_weight,
        grad_query_bias,
        grad_key_weight,
        grad_value_weight,
        grad_value_bias,
        grad_output_weight,
        grad_output_bias,
        grad_first_gain,
        grad_first_shift,
        grad_inner_weight,
        grad_inner_bias,
        grad_outer_weight,
        grad_outer_bias,
        grad_second_gain,
        grad_second_shift,
        gate_derivative_rule,
    ) = (
        lax.psum_scatter(grad_query_weight, ("seq", "dp"), scatter_dimension=0, tiled=True),
        lax.psum_scatter(grad_query_bias, ("seq", "dp"), scatter_dimension=0, tiled=True),
        lax.psum_scatter(grad_key_weight, ("seq", "dp"), scatter_dimension=0, tiled=True),
        lax.psum_scatter(grad_value_weight, ("seq", "dp"), scatter_dimension=0, tiled=True),
        lax.psum_scatter(grad_value_bias, ("seq", "dp"), scatter_dimension=0, tiled=True),
        lax.psum_scatter(grad_output_weight, ("seq", "dp"), scatter_dimension=0, tiled=True),
        lax.psum_scatter(grad_output_bias, ("seq", "dp"), scatter_dimension=0, tiled=True),
        lax.psum_scatter(grad_first_gain, ("seq", "dp"), scatter_dimension=0, tiled=True),
        lax.psum_scatter(grad_first_shift, ("seq", "dp"), scatter_dimension=0, tiled=True),
        lax.psum_scatter(grad_inner_weight, ("seq", "dp"), scatter_dimension=0, tiled=True),
        lax.psum_scatter(grad_inner_bias, ("seq", "dp"), scatter_dimension=0, tiled=True),
        lax.psum_scatter(grad_outer_weight, ("seq", "dp"), scatter_dimension=0, tiled=True),
        lax.psum_scatter(grad_outer_bias, ("seq", "dp"), scatter_dimension=0, tiled=True),
        lax.psum_scatter(grad_second_gain, ("seq", "dp"), scatter_dimension=0, tiled=True),
        lax.psum_scatter(grad_second_shift, ("seq", "dp"), scatter_dimension=0, tiled=True),
        lax.psum_scatter(gate_derivative_rule, ("seq", "dp"), scatter_dimension=1, tiled=True),
    )
    mask_logits_gradient = (
        gate_derivative_rule
        * smoothed_gate
        * (1.0 - smoothed_gate)
        / softening_scale[:, None, None]
    )
    return (
        layer_out[None],
        input_grad[None],
        grad_query_weight,
        grad_query_bias,
        grad_key_weight,
        grad_value_weight,
        grad_value_bias,
        grad_output_weight,
        grad_output_bias,
        grad_first_gain,
        grad_first_shift,
        grad_inner_weight,
        grad_inner_bias,
        grad_outer_weight,
        grad_outer_bias,
        grad_second_gain,
        grad_second_shift,
        mask_logits_gradient,
    )


def solution(mesh):
    return jax.shard_map(
        body,
        mesh=mesh,
        in_specs=(
            P("dp", "seq", None),
            P("dp", "seq", None),
            P("dp", None),
            P("dp", None),
            P(("seq", "dp"), None),
            P(("seq", "dp")),
            P(("seq", "dp"), None),
            P(("seq", "dp"), None),
            P(("seq", "dp")),
            P(("seq", "dp"), None),
            P(("seq", "dp")),
            P(("seq", "dp")),
            P(("seq", "dp")),
            P(("seq", "dp"), None),
            P(("seq", "dp")),
            P(("seq", "dp"), None),
            P(("seq", "dp")),
            P(("seq", "dp")),
            P(("seq", "dp")),
            P(None, ("seq", "dp"), None),
            P(None, ("seq", "dp"), None),
            P(),
        ),
        out_specs=(
            P("dp", "seq", None),
            P("dp", "seq", None),
            P(("seq", "dp"), None),
            P(("seq", "dp")),
            P(("seq", "dp"), None),
            P(("seq", "dp"), None),
            P(("seq", "dp")),
            P(("seq", "dp"), None),
            P(("seq", "dp")),
            P(("seq", "dp")),
            P(("seq", "dp")),
            P(("seq", "dp"), None),
            P(("seq", "dp")),
            P(("seq", "dp"), None),
            P(("seq", "dp")),
            P(("seq", "dp")),
            P(("seq", "dp")),
            P(None, ("seq", "dp"), None),
        ),
        check_vma=False,
    )
```

profile of v0, /device:TPU:0, one launch (start us, length us, event | category | flops | bytes accessed | tf_op | source)
XLA Modules:
  0.0 2531.0 jit_solution(9380549809217622605)
XLA Ops:
  17.0 42.7 %all-reduce.19 = (bf16[768]{0:T(1024)(128)(2,1)S(1)}, bf16[768]{0:T(1024)(128)(2,1)}, bf16[768]{0:T(1024)(128)(2,1)}, bf16[768]{0:T(1024)(128)(2,1)}, bf16[768]{...) all-reduce(bf16[768]{0:T(1024)(128)(2,1)S(1)} %dynamic-update-slice, ...), channel_id=1, replica_groups=mesh['seq'=2,'dp'=16] {'seq','dp'}, use_global_device_ids=true, to_apply=%add | all-reduce | flops 9216 | bytes 36864
  72.4 51.2 %all-gather.16.cloned.1.call-done = bf16[768,768]{1,0:T(8,128)(2,1)} async-done(((bf16[24,768]{1,0:T(8,128)(2,1)}), bf16[768,768]{1,0:T(8,128)(2,1)}) %all-gather.16.cloned.1.call-update) | async-done | bytes 1179664 | tf_op jit(solution)/shard_map/all_gather | solution.py:128
  149.4 30.1 %all-gather.14.cloned.1.call-done = bf16[768,768]{1,0:T(8,128)(2,1)} async-done(((bf16[24,768]{1,0:T(8,128)(2,1)}), bf16[768,768]{1,0:T(8,128)(2,1)}) %all-gather.14.cloned.1.call-update) | async-done | bytes 1179664 | tf_op jit(solution)/shard_map/all_gather | solution.py:127
  183.3 42.0 %all-gather.12.cloned.1.call-done = bf16[2048,768]{1,0:T(8,128)(2,1)} async-done(((bf16[1024,768]{1,0:T(8,128)(2,1)}), bf16[2048,768]{1,0:T(8,128)(2,1)}) %all-gather.12.cloned.1.call-update) | async-done | bytes 3145744 | tf_op jit(solution)/shard_map/all_gather | solution.py:169
  230.0 41.7 %all-gather.18.cloned.1.call-done = bf16[2048,768]{1,0:T(8,128)(2,1)} async-done(((bf16[1024,768]{1,0:T(8,128)(2,1)}), bf16[2048,768]{1,0:T(8,128)(2,1)}) %all-gather.18.cloned.1.call-update) | async-done | bytes 3145744 | tf_op jit(solution)/shard_map/all_gather | solution.py:168
  276.4 68.0 %all-gather.20.cloned.1.call-done = bf16[12,512,512]{2,1,0:T(8,128)(2,1)} async-done(((bf16[12,16,512]{2,1,0:T(8,128)(2,1)}), bf16[12,512,512]{2,1,0:T(8,128)(2,1)}) %all-gather.20.cloned.1.call-update) | async-done | bytes 6291472 | tf_op jit(solution)/shard_map/all_gather | solution.py:142
  345.7 367.2 %while.35 = (s32[]{:T(128)}, bf16[6,1024,2,64]{1,3,2,0:T(8,128)(2,1)}, f32[6,2,1024]{2,1,0:T(2,128)S(1)}, bf16[6,2048,2,64]{1,3,2,0:T(8,128)(2,1)}, bf16[6,1024,...) while((s32[]{:T(128)}, ...), condition=%wide.region_3.6_spmd.clone, body=%wide.region_0.5_spmd.clone.sunk | while | flops 1118435328 | bytes 132725224 | solution.py:190
  358.4 20.5 mul.485
  378.9 11.7 fusion.148
  419.4 20.6 mul.485
  439.9 11.7 fusion.148
  480.8 20.6 mul.485
  501.4 12.0 fusion.148
  542.2 20.5 mul.485
  562.7 11.7 fusion.148
  603.1 20.5 mul.485
  664.0 20.5 mul.485
  746.4 17.7 convert_reduce_fusion
  779.3 727.4 %while.36 = (s32[]{:T(128)}, bf16[6,1024,2,64]{1,3,2,0:T(8,128)(2,1)}, f32[6,2048,2,64]{1,3,2,0:T(8,128)}, f32[6,2048,2,64]{1,3,2,0:T(8,128)}, f32[6,2,512,512]{...) while((s32[]{:T(128)}, ...), condition=%wide.region_15.18_spmd.clone, body=%wide.region_12.17_spmd.clone.sunk | while | flops 2738878464 | bytes 364701760 | solution.py:294
  791.7 20.5 mul.492
  821.5 18.4 multiply_reduce_fusion.7
  866.9 19.8 reshape.220
  912.9 20.5 mul.492
  942.6 18.4 multiply_reduce_fusion.7
  988.0 19.8 reshape.220
  1034.0 20.5 mul.492
  1063.8 18.3 multiply_reduce_fusion.7
  1109.2 19.8 reshape.220
  1155.1 20.5 mul.492
  1184.9 18.3 multiply_reduce_fusion.7
  1230.3 19.8 reshape.220
  1276.3 20.5 mul.492
  1306.1 18.3 multiply_reduce_fusion.7
  1351.5 19.8 reshape.220
  1397.4 20.5 mul.492
  1427.2 18.3 multiply_reduce_fusion.7
  1472.5 19.8 reshape.220
  1519.1 14.2 fusion.96
  1545.8 37.2 %reduce-scatter.16.cloned.1.call-done = f32[1024,768]{0,1:T(8,128)} async-done(((f32[2048,768]{0,1:T(8,128)}), f32[1024,768]{0,1:T(8,128)}) %reduce-scatter.16.cloned.1.call-update) | async-done | bytes 3145744 | tf_op jit(solution)/shard_map/reduce_scatter | solution.py:307
  1588.8 73.7 %reduce-scatter.18.cloned.1.call-done = f32[1024,768]{0,1:T(8,128)} async-done(((f32[2048,768]{0,1:T(8,128)}), f32[1024,768]{0,1:T(8,128)}) %reduce-scatter.18.cloned.1.call-update) | async-done | bytes 3145744 | tf_op jit(solution)/shard_map/reduce_scatter | solution.py:308
  1681.6 40.4 %all-reduce.18 = (f32[768]{0:T(1024)S(1)}, f32[768]{0:T(1024)S(1)}, f32[768]{0:T(1024)S(1)}, f32[768]{0:T(1024)S(1)}, f32[768]{0:T(1024)S(1)}, /*index=5*/f32[30...) all-reduce(f32[768]{0:T(1024)S(1)} %reduce_sum.199, ...), channel_id=5, replica_groups=mesh['seq'=2,'dp'=16] {'seq','dp'}, use_global_device_ids=true, to_apply=%region_20.23.clone | all-reduce | flops 9216 | bytes 73728
  1738.4 85.5 %reduce-scatter.26.cloned.1.call-done = f32[12,16,512]{2,1,0:T(8,128)} async-done(((f32[12,512,512]{2,1,0:T(8,128)}), f32[12,16,512]{2,1,0:T(8,128)}) %reduce-scatter.26.cloned.1.call-update) | async-done | bytes 393232 | tf_op jit(solution)/shard_map/reduce_scatter | solution.py:358
  1825.8 103.1 %reduce-scatter.20.cloned.1.call-done = f32[24,768]{1,0:T(8,128)} async-done(((f32[768,768]{1,0:T(8,128)}), f32[24,768]{1,0:T(8,128)}) %reduce-scatter.20.cloned.1.call-update) | async-done | bytes 73744 | tf_op jit(solution)/shard_map/reduce_scatter | solution.py:348
  1928.9 103.8 %reduce-scatter.28.cloned.1.call-done = f32[24,768]{1,0:T(8,128)} async-done(((f32[768,768]{1,0:T(8,128)}), f32[24,768]{1,0:T(8,128)}) %reduce-scatter.28.cloned.1.call-update) | async-done | bytes 73744
  2032.7 141.9 %reduce-scatter.24.cloned.1.call-done = f32[96,768]{1,0:T(8,128)} async-done(((f32[3072,768]{1,0:T(8,128)}), f32[96,768]{1,0:T(8,128)}) %reduce-scatter.24.cloned.1.call-update) | async-done | bytes 294928 | tf_op jit(solution)/shard_map/reduce_scatter | solution.py:354
  2174.6 141.0 %reduce-scatter.22.cloned.1.call-done = f32[24,3072]{1,0:T(8,128)} async-done(((f32[768,3072]{1,0:T(8,128)}), f32[24,3072]{1,0:T(8,128)}) %reduce-scatter.22.cloned.1.call-update) | async-done | bytes 294928 | tf_op jit(solution)/shard_map/reduce_scatter | solution.py:352
  2315.6 104.7 %reduce-scatter.30.cloned.1.call-done = f32[24,768]{1,0:T(8,128)} async-done(((f32[768,768]{1,0:T(8,128)}), f32[24,768]{1,0:T(8,128)}) %reduce-scatter.30.cloned.1.call-update) | async-done | bytes 73744
  2420.2 103.7 %reduce-scatter.32.cloned.1.call-done = f32[24,768]{1,0:T(8,128)} async-done(((f32[768,768]{1,0:T(8,128)}), f32[24,768]{1,0:T(8,128)}) %reduce-scatter.32.cloned.1.call-update) | async-done | bytes 73744
  (370 shorter events, 745.4 us)
Async XLA Ops:
  7.2 60.8 %all-gather.10.cloned.1.call-start = ((), (), s32[]{:S(2)}) async-start(), calls=%async_computation.9 | async-start | bytes 1216512 | tf_op jit(solution)/shard_map/all_gather | solution.py:129
  7.9 115.7 %all-gather.16.cloned.1.call-start = ((), (), s32[]{:S(2)}) async-start(), calls=%async_computation.12 | async-start | bytes 1216512 | tf_op jit(solution)/shard_map/all_gather | solution.py:128
  8.7 170.8 %all-gather.14.cloned.1.call-start = ((), (), s32[]{:S(2)}) async-start(), calls=%async_computation.11 | async-start | bytes 1216512 | tf_op jit(solution)/shard_map/all_gather | solution.py:127
  9.4 215.9 %all-gather.12.cloned.1.call-start = ((), (), s32[]{:S(2)}) async-start(), calls=%async_computation.10 | async-start | bytes 4718592 | tf_op jit(solution)/shard_map/all_gather | solution.py:169
  59.7 63.9 %copy-start.13 = (bf16[1,1024,768]{2,1,0:T(8,128)(2,1)S(1)}, bf16[1,1024,768]{2,1,0:T(8,128)(2,1)}, u32[]{:S(2)}) copy-start(bf16[1,1024,768]{2,1,0:T(8,128)(2,1)} %param.30) | copy-start | bytes 4718596
  72.3 55.2 %copy-start.24 = (f32[12,16,512]{2,1,0:T(8,128)S(1)}, f32[12,16,512]{2,1,0:T(8,128)}, u32[]{:S(2)}) copy-start(f32[12,16,512]{2,1,0:T(8,128)} %param.49) | copy-start | bytes 1179652
  72.3 199.4 %all-gather.18.cloned.1.call-start = ((), (), s32[]{:S(2)}) async-start(), calls=%async_computation.13 | async-start | bytes 4718592 | tf_op jit(solution)/shard_map/all_gather | solution.py:168
  127.4 11.4 copy-start.17
  127.4 20.3 copy-start.12
  127.5 216.9 %all-gather.20.cloned.1.call-start = ((), (), s32[]{:S(2)}) async-start(), calls=%async_computation.14 | async-start | bytes 6488064 | tf_op jit(solution)/shard_map/all_gather | solution.py:142
  129.7 583.2 %all-gather.22.cloned.1.call-start = ((), (), s32[]{:S(2)}) async-start(), calls=%async_computation.15 | async-start | bytes 1216512 | tf_op jit(solution)/shard_map/all_gather | solution.py:130
  130.4 586.8 %all-gather.24.cloned.1.call-start = ((), (), s32[]{:S(2)}) async-start(), calls=%async_computation.16 | async-start | bytes 4866048 | tf_op jit(solution)/shard_map/all_gather | solution.py:131
  131.2 597.3 %all-gather.26.cloned.1.call-start = ((), (), s32[]{:S(2)}) async-start(), calls=%async_computation.17 | async-start | bytes 4866048 | tf_op jit(solution)/shard_map/all_gather | solution.py:132
  131.9 1451.1 %reduce-scatter.16.cloned.1.call-start = ((), (), s32[]{:S(2)}) async-start(), calls=%async_computation.18 | async-start | bytes 9437184 | tf_op jit(solution)/shard_map/reduce_scatter | solution.py:307
  345.7 367.2 %copy-start.36 = (f32[768]{0:T(1024)S(1)}, f32[768]{0:T(1024)}, u32[]{:S(2)}) copy-start(f32[768]{0:T(1024)} %convert_element_type.153) | copy-start | bytes 9220
  716.7 56.9 %copy-start.2 = (f32[1024,768]{0,1:T(8,128)}, f32[1024,768]{0,1:T(8,128)S(1)}, u32[]{:S(2)}) copy-start(f32[1024,768]{0,1:T(8,128)S(1)} %get-tuple-element.636) | copy-start | bytes 9437188
  716.8 56.8 %copy-start.18 = (f32[1024]{0:T(1024)}, f32[1024]{0:T(1024)S(1)}, u32[]{:S(2)}) copy-start(f32[1024]{0:T(1024)S(1)} %broadcast_multiply_fusion.5) | copy-start | bytes 12292
  717.2 56.4 %copy-start.22 = (f32[1024]{0:T(1024)}, f32[1024]{0:T(1024)S(1)}, u32[]{:S(2)}) copy-start(f32[1024]{0:T(1024)S(1)} %add_rsqrt_fusion.1) | copy-start | bytes 12292
  717.2 11.2 copy-start.32
  717.2 11.2 copy-start.35
  741.3 5.1 copy-start.40
  743.2 21.0 slice-start
  746.4 17.7 copy-start.14
  746.4 17.7 slice-start.1
  839.9 15.4 copy-start.1
  855.2 8.1 copy-start
  961.0 15.4 copy-start.1
  976.4 8.1 copy-start
  1082.0 15.4 copy-start.1
  1097.4 8.2 copy-start
  1203.2 15.4 copy-start.1
  1218.6 8.1 copy-start
  1324.4 15.4 copy-start.1
  1339.8 8.1 copy-start
  1445.4 15.4 copy-start.1
  1460.8 8.1 copy-start
  1506.7 155.8 %reduce-scatter.18.cloned.1.call-start = ((), (), s32[]{:S(2)}) async-start(), calls=%async_computation.19 | async-start | bytes 9437184 | tf_op jit(solution)/shard_map/reduce_scatter | solution.py:308
  1507.5 316.5 %reduce-scatter.26.cloned.1.call-start = ((), (), s32[]{:S(2)}) async-start(), calls=%async_computation.23 | async-start | bytes 12976128 | tf_op jit(solution)/shard_map/reduce_scatter | solution.py:358
  1508.0 420.8 %reduce-scatter.20.cloned.1.call-start = ((), (), s32[]{:S(2)}) async-start(), calls=%async_computation.20 | async-start | bytes 2433024 | tf_op jit(solution)/shard_map/reduce_scatter | solution.py:348
  1513.7 519.0 %reduce-scatter.28.cloned.1.call-start = ((), (), s32[]{:S(2)}) async-start(), calls=%async_computation.24 | async-start | bytes 2433024
  1519.0 655.6 %reduce-scatter.24.cloned.1.call-start = ((), (), s32[]{:S(2)}) async-start(), calls=%async_computation.22 | async-start | bytes 9732096 | tf_op jit(solution)/shard_map/reduce_scatter | solution.py:354
  1533.4 782.2 %reduce-scatter.22.cloned.1.call-start = ((), (), s32[]{:S(2)}) async-start(), calls=%async_computation.21 | async-start | bytes 9732096 | tf_op jit(solution)/shard_map/reduce_scatter | solution.py:352
  1545.8 874.5 %reduce-scatter.30.cloned.1.call-start = ((), (), s32[]{:S(2)}) async-start(), calls=%async_computation.25 | async-start | bytes 2433024
  1588.8 935.2 %reduce-scatter.32.cloned.1.call-start = ((), (), s32[]{:S(2)}) async-start(), calls=%async_computation.26 | async-start | bytes 2433024
  1675.7 5.2 copy-start.6
  1726.7 4.4 copy-start.16
  1734.2 89.7 %copy-start.15 = (f32[12,16,512]{2,1,0:T(8,128)S(1)}, f32[12,16,512]{2,1,0:T(8,128)}, u32[]{:S(2)}) copy-start(f32[12,16,512]{2,1,0:T(8,128)} %get-tuple-element.627) | copy-start | bytes 1179652
  1734.2 89.7 %copy-start.39 = (f32[12]{0:T(128)S(1)}, f32[12]{0:T(128)}, u32[]{:S(2)}) copy-start(f32[12]{0:T(128)} %param.51) | copy-start | bytes 148
  (24 other events, 42.0 us)
Sparse Core Ops, SparseCore 0:
  10.9 57.0 all-gather.9
  70.9 52.6 all-gather.15
  126.5 52.9 all-gather.13
  181.4 43.8 all-gather.11
  226.7 44.9 all-gather.17
  275.0 69.3 all-gather.19
  347.3 52.9 all-gather.21
  403.1 62.5 all-gather.23
  468.6 62.4 all-gather.25
  1506.9 76.1 reduce-scatter.15
  1585.4 77.0 reduce-scatter.17
  1668.4 155.5 reduce-scatter.25
  1830.7 98.1 reduce-scatter.19
  1934.6 98.0 reduce-scatter.27
  2040.0 134.5 reduce-scatter.23
  2181.0 134.5 reduce-scatter.21
  2322.1 98.0 reduce-scatter.29
  2426.0 97.9 reduce-scatter.31
where the time goes:
time: 2550 us; the launch traced here: 2530 us
  waiting for transfers between devices  1140 us (45%)
  local copies, waits for them, and re-layouts  538 us (21%)
  matrix products  477 us (19%)
  other arithmetic  269 us (11%)
  blocking collectives  83 us (3%)
    unnamed x21, waiting for transfers between devices  318 us
    mul x12, local copies, waits for them, and re-layouts, group_scores(): logits = logits + 4.0 * picked.astype(jnp.float32)  247 us
    dot_general x12, matrix products, group_scores(): jnp.einsum('qgd,kgd->gqk', query_group, keys_group, preferred_element_typ...  180 us
    reduce_scatter x1, waiting for transfers between devices, body(): lax.psum_scatter(grad_outer_weight, ('seq', 'dp'), scatter_dimension=0, t...  142 us
    reduce_scatter x1, waiting for transfers between devices, body(): lax.psum_scatter(grad_inner_weight, ('seq', 'dp'), scatter_dimension=0, t...  141 us
    reshape x6, local copies, waits for them, and re-layouts, folded_table(): folded = grad_scores.astype(jnp.float32).reshape(group_width, row_count /...  119 us
    reduce_scatter x1, waiting for transfers between devices, body(): lax.psum_scatter(grad_output_weight, ('seq', 'dp'), scatter_dimension=0,...  103 us
    another operation x12, local copies, waits for them, and re-layouts, tiled_table(): jnp.tile(rolled, (1, row_count // table_size, col_count // table_size))  85.6 us
  transfers between devices with their start and end apart: 18, of which 15 were waited for; matrix products, arithmetic and copies ran while one was open for 20% of the time, Pallas kernels for 0%

commit v1 on v0

v1 whole, which is shorter than its diff:
```python
import functools
import math

import jax
import jax.numpy as jnp
from jax import lax
from jax.experimental import pallas as pl
from jax.experimental.pallas import tpu as pltpu
from jax.sharding import PartitionSpec as P

EPSILON = 1e-06
LOG2E = math.log2(math.e)
MASKED = -1e30
TILE = 256
NT = (((1,), (1,)), ((), ()))
NN = (((1,), (0,)), ((), ()))


def dot(a, b, dims=NN):
    return lax.dot_general(a, b, dims, preferred_element_type=jnp.float32)


def local_row(block, seq_index, half_blocks):
    return ((block // half_blocks) ^ seq_index) * (half_blocks * TILE) + (block % half_blocks) * TILE


def split_pair(rows):
    lane = lax.broadcasted_iota(jnp.int32, rows.shape, 1)
    zero = jnp.zeros_like(rows)
    return jnp.where(lane < 64, rows, zero), jnp.where(lane < 64, zero, rows)


def attend_kernel(half_blocks, scale, s_ref, nk_ref, qkv_ref, tab_ref, end_ref, att_ref, o32_ref, lse_ref, vt_ref, st_ref, acc_ref):
    block = pl.program_id(1)
    seq_index = s_ref[0]
    table_blocks = tab_ref.shape[1] // TILE

    @pl.when(block == 0)
    def _():
        vt = qkv_ref[:, 256:384].astype(jnp.float32).T
        sub = lax.broadcasted_iota(jnp.int32, vt.shape, 0)
        vt_ref[0] = jnp.where(sub < 64, vt, 1.0).astype(jnp.bfloat16)
        vt_ref[1] = jnp.where(sub < 64, 1.0, vt).astype(jnp.bfloat16)

    here = pl.multiple_of(local_row(block, seq_index, half_blocks), TILE)
    queries = split_pair(qkv_ref[pl.ds(here, TILE), 0:128])
    row_end = end_ref[0:1, :]
    sub = lax.broadcasted_iota(jnp.int32, (TILE, TILE), 0)
    count = nk_ref[block]

    def score(j, peaks):
        there = pl.multiple_of(local_row(j, seq_index, half_blocks), TILE)
        keys = qkv_ref[pl.ds(there, TILE), 128:256]
        allowed = sub < row_end - j * TILE
        out = []
        for h in range(2):
            part = tab_ref[h, pl.ds(pl.multiple_of((j % table_blocks) * TILE, TILE), TILE), :]
            x = jnp.where(allowed, dot(keys, queries[h], NT) * scale + part, MASKED)
            st_ref[h, pl.ds(pl.multiple_of(j * TILE, TILE), TILE), :] = x
            out.append(jnp.maximum(peaks[h], jnp.max(x.reshape(TILE // 8, 8, TILE), axis=0)))
        return tuple(out)

    start = jnp.full((8, TILE), MASKED, jnp.float32)
    peaks = lax.fori_loop(0, count, score, (start, start))
    peak = [jnp.max(p, axis=0, keepdims=True) for p in peaks]
    acc_ref[...] = jnp.zeros_like(acc_ref)

    def mix(j, carry):
        there = pl.multiple_of(local_row(j, seq_index, half_blocks), TILE)
        for h in range(2):
            x = st_ref[h, pl.ds(pl.multiple_of(j * TILE, TILE), TILE), :]
            p = jnp.exp2(x - peak[h]).astype(jnp.bfloat16)
            acc_ref[h] += dot(vt_ref[h, :, pl.ds(there, TILE)], p)
        return carry

    lax.fori_loop(0, count, mix, 0)
    out0 = acc_ref[0, 0:64, :] / acc_ref[0, 64:128, :]
    out1 = acc_ref[1, 64:128, :] / acc_ref[1, 0:64, :]
    out = jnp.concatenate([out0, out1], axis=0).T
    o32_ref[...] = out
    att_ref[...] = out.astype(jnp.bfloat16)
    lse0 = peak[0] + jnp.log2(acc_ref[0, 64:65, :])
    lse1 = peak[1] + jnp.log2(acc_ref[1, 0:1, :])
    lse_ref[0] = jnp.concatenate([lse0, lse1, jnp.zeros((6, TILE), jnp.float32)], axis=0)


def attend(qkv, tables, row_end, counts, seq_index, score_scale):
    rows = qkv.shape[0]
    pairs = qkv.shape[1] // 384
    blocks = rows // TILE
    half = blocks // 2
    tsize = tables.shape[1]
    spec = pltpu.PrefetchScalarGridSpec(
        num_scalar_prefetch=2,
        grid=(pairs, blocks),
        in_specs=[
            pl.BlockSpec((rows, 384), lambda p, g, s, n: (0, p)),
            pl.BlockSpec((2, tsize, TILE), lambda p, g, s, n: (p, 0, g % (tsize // TILE))),
            pl.BlockSpec((1, TILE), lambda p, g, s, n: (0, g)),
        ],
        out_specs=[
            pl.BlockSpec((TILE, 128), lambda p, g, s, n: (((g // half) ^ s[0]) * half + g % half, p)),
            pl.BlockSpec((TILE, 128), lambda p, g, s, n: (((g // half) ^ s[0]) * half + g % half, p)),
            pl.BlockSpec((1, 8, TILE), lambda p, g, s, n: (p, 0, g)),
        ],
        scratch_shapes=[
            pltpu.VMEM((2, 128, rows), jnp.bfloat16),
            pltpu.VMEM((2, rows, TILE), jnp.float32),
            pltpu.VMEM((2, 128, TILE), jnp.float32),
        ],
    )
    return pl.pallas_call(
        functools.partial(attend_kernel, half, score_scale * LOG2E),
        grid_spec=spec,
        out_shape=[
            jax.ShapeDtypeStruct((rows, pairs * 128), jnp.bfloat16),
            jax.ShapeDtypeStruct((rows, pairs * 128), jnp.float32),
            jax.ShapeDtypeStruct((pairs, 8, rows), jnp.float32),
        ],
        compiler_params=pltpu.CompilerParams(dimension_semantics=("arbitrary", "arbitrary"), vmem_limit_bytes=40 << 20),
        name="attend",
    )(seq_index, counts, qkv, tables, row_end)


def attend_back_kernel(half_blocks, scale, score_scale, s_ref, nk_ref, qkv_ref, grad_ref, o32_ref, tab_ref, end_ref, lse_ref,
                       dqkv_ref, gtab_ref, kt_ref, dk_ref, dv_ref, dq_ref):
    block = pl.program_id(1)
    seq_index = s_ref[0]
    table_blocks = tab_ref.shape[1] // TILE

    @pl.when(block == 0)
    def _():
        kt = qkv_ref[:, 128:256].astype(jnp.float32).T
        sub = lax.broadcasted_iota(jnp.int32, kt.shape, 0)
        kt_ref[0] = jnp.where(sub < 64, kt, 0.0).astype(jnp.bfloat16)
        kt_ref[1] = jnp.where(sub < 64, 0.0, kt).astype(jnp.bfloat16)
        dk_ref[...] = jnp.zeros_like(dk_ref)
        dv_ref[...] = jnp.zeros_like(dv_ref)
        gtab_ref[...] = jnp.zeros_like(gtab_ref)

    here = pl.multiple_of(local_row(block, seq_index, half_blocks), TILE)
    queries = split_pair(qkv_ref[pl.ds(here, TILE), 0:128])
    grads = split_pair(grad_ref[...])
    row_end = end_ref[0:1, :]
    inner = (grad_ref[...].astype(jnp.float32) * o32_ref[...]).T
    delta = [jnp.sum(inner[0:64], axis=0, keepdims=True), jnp.sum(inner[64:128], axis=0, keepdims=True)]
    lse = [lse_ref[0, 0:1, :], lse_ref[0, 1:2, :]]
    q_stack = jnp.concatenate(queries, axis=0)
    g_stack = jnp.concatenate(grads, axis=0)
    sub = lax.broadcasted_iota(jnp.int32, (TILE, TILE), 0)
    dq_ref[...] = jnp.zeros_like(dq_ref)
    lane0 = pl.multiple_of((block % table_blocks) * TILE, TILE)

    def step(j, carry):
        there = pl.multiple_of(local_row(j, seq_index, half_blocks), TILE)
        keys = qkv_ref[pl.ds(there, TILE), 128:256]
        values = qkv_ref[pl.ds(there, TILE), 256:384]
        allowed = sub < row_end - j * TILE
        trow = pl.multiple_of((j % table_blocks) * TILE, TILE)
        probs, scores = [], []
        for h in range(2):
            part = tab_ref[h, pl.ds(trow, TILE), :]
            x = dot(keys, queries[h], NT) * scale + part - lse[h]
            p = jnp.exp2(jnp.where(allowed, x, MASKED))
            d = p * (dot(values, grads[h], NT) - delta[h])
            gtab_ref[h, pl.ds(trow, TILE), pl.ds(lane0, TILE)] += d
            probs.append(p.astype(jnp.bfloat16))
            scores.append(d.astype(jnp.bfloat16))
        dv_ref[pl.ds(there, TILE), :] += dot(jnp.concatenate(probs, axis=1), g_stack)
        dk_ref[pl.ds(there, TILE), :] += dot(jnp.concatenate(scores, axis=1), q_stack)
        kt = jnp.concatenate([kt_ref[0, :, pl.ds(there, TILE)], kt_ref[1, :, pl.ds(there, TILE)]], axis=1)
        dq_ref[...] += dot(kt, jnp.concatenate(scores, axis=0))
        return carry

    lax.fori_loop(0, nk_ref[block], step, 0)
    dqkv_ref[pl.ds(here, TILE), 0:128] = (dq_ref[...] * score_scale).T.astype(jnp.bfloat16)

    @pl.when(block == pl.num_programs(1) - 1)
    def _():
        dqkv_ref[:, 128:256] = (dk_ref[...] * score_scale).astype(jnp.bfloat16)
        dqkv_ref[:, 256:384] = dv_ref[...].astype(jnp.bfloat16)


def attend_back(qkv, grads, o32, tables, row_end, lse, counts, seq_index, score_scale):
    rows = qkv.shape[0]
    pairs = qkv.shape[1] // 384
    blocks = rows // TILE
    half = blocks // 2
    tsize = tables.shape[1]
    row_map = lambda p, g, s, n: (((g // half) ^ s[0]) * half + g % half, p)
    spec = pltpu.PrefetchScalarGridSpec(
        num_scalar_prefetch=2,
        grid=(pairs, blocks),
        in_specs=[
            pl.BlockSpec((rows, 384), lambda p, g, s, n: (0, p)),
            pl.BlockSpec((TILE, 128), row_map),
            pl.BlockSpec((TILE, 128), row_map),
            pl.BlockSpec((2, tsize, TILE), lambda p, g, s, n: (p, 0, g % (tsize // TILE))),
            pl.BlockSpec((1, TILE), lambda p, g, s, n: (0, g)),
            pl.BlockSpec((1, 8, TILE), lambda p, g, s, n: (p, 0, g)),
        ],
        out_specs=[
            pl.BlockSpec((rows, 384), lambda p, g, s, n: (0, p)),
            pl.BlockSpec((2, tsize, tsize), lambda p, g, s, n: (p, 0, 0)),
        ],
        scratch_shapes=[
            pltpu.VMEM((2, 128, rows), jnp.bfloat16),
            pltpu.VMEM((rows, 128), jnp.float32),
            pltpu.VMEM((rows, 128), jnp.float32),
            pltpu.VMEM((128, TILE), jnp.float32),
        ],
    )
    return pl.pallas_call(
        functools.partial(attend_back_kernel, half, score_scale * LOG2E, score_scale),
        grid_spec=spec,
        out_shape=[
            jax.ShapeDtypeStruct((rows, pairs * 384), jnp.bfloat16),
            jax.ShapeDtypeStruct((2 * pairs, tsize, tsize), jnp.float32),
        ],
        compiler_params=pltpu.CompilerParams(dimension_semantics=("arbitrary", "arbitrary"), vmem_limit_bytes=40 << 20),
        name="attend_back",
    )(seq_index, counts, qkv, grads, o32, tables, row_end, lse)


def matmul(left_side, right_side):
    return jnp.dot(left_side, right_side, preferred_element_type=jnp.float32)


def contract_rows(left_side, right_side):
    return jnp.einsum("rd,re->de", left_side, right_side, preferred_element_type=jnp.float32)


def times_transpose(left_side, right_side):
    return jnp.einsum("re,de->rd", left_side, right_side, preferred_element_type=jnp.float32)


def norm_forward(values, norm_gain, norm_shift):
    center = values - jnp.mean(values, axis=-1, keepdims=True)
    rstdev = lax.rsqrt(jnp.mean(center * center, axis=-1, keepdims=True) + EPSILON)
    normed = center * rstdev
    return (normed * norm_gain + norm_shift, normed, rstdev)


def norm_backward(gradient, normed, rstdev, norm_gain):
    scaled = gradient * norm_gain
    back = rstdev * (
        scaled
        - jnp.mean(scaled, axis=-1, keepdims=True)
        - normed * jnp.mean(scaled * normed, axis=-1, keepdims=True)
    )
    return (back, jnp.sum(gradient * normed, axis=0), jnp.sum(gradient, axis=0))

def swap_seq(value):
    return lax.ppermute(value, "seq", [(0, 1), (1, 0)])


def pair_up(mine, theirs, seq_index):
    first = seq_index == 0
    return jnp.stack([jnp.where(first, mine, theirs), jnp.where(first, theirs, mine)])


def flip_bit(value, axis, bit):
    count = lax.axis_size(axis)
    return lax.ppermute(value, axis, [(i, i ^ bit) for i in range(count)])


def gather_small(value):
    gathered = value[None]
    bit = 1
    for axis in ("dp", "seq"):
        bit = 1
        while bit < lax.axis_size(axis):
            other = flip_bit(gathered, axis, bit)
            low = (lax.axis_index(axis) & bit) == 0
            gathered = jnp.concatenate(
                [jnp.where(low, gathered, other), jnp.where(low, other, gathered)], axis=0
            )
            bit *= 2
    return gathered


def sum_small(value):
    for axis in ("dp", "seq"):
        bit = 1
        while bit < lax.axis_size(axis):
            value = value + flip_bit(value, axis, bit)
            bit *= 2
    return value


def body(
    incoming_activations,
    upstream_derivative,
    grid_coordinates,
    word_segment_ids,
    asking_matrix,
    asking_shift,
    lookup_matrix,
    content_matrix,
    content_shift,
    mixing_result_matrix,
    mixing_result_shift,
    post_mixing_scaling,
    post_mixing_offset,
    expand_matrix,
    expand_shift,
    contract_matrix,
    contract_shift,
    post_perceptron_scaling,
    post_perceptron_offset,
    pair_gate_scores,
    gate_random_jitter,
    softening_scale,
):
    f32, bf16 = jnp.float32, jnp.bfloat16
    heads = softening_scale.shape[0]
    width = incoming_activations.shape[2]
    rows = incoming_activations.shape[1]
    inner = expand_matrix.shape[1]
    tsize = pair_gate_scores.shape[2]
    head_size = width // heads
    score_scale = 1.0 / math.sqrt(head_size)
    half_width, half_heads = width // 2, heads // 2
    pairs = half_heads // 2
    seq_index = lax.axis_index("seq")
    dp_index = lax.axis_index("dp")
    dp_size = lax.axis_size("dp")
    inputs = incoming_activations[0]
    share = asking_matrix.shape[0]

    other_inputs = swap_seq(inputs)
    vectors = gather_small(
        jnp.concatenate(
            [
                asking_shift,
                content_shift,
                mixing_result_shift,
                post_mixing_scaling,
                post_mixing_offset,
                contract_shift,
                post_perceptron_scaling,
                post_perceptron_offset,
                expand_shift,
            ]
        )
    )

    def vector(index, size=share):
        return vectors[:, index * share : index * share + size].reshape(-1).astype(f32)

    def pack_heads(parts):
        return jnp.stack([part.reshape(share, 2, pairs, 128) for part in parts], axis=3).reshape(
            share, 2, 3 * half_width
        )

    packed = pack_heads((asking_matrix, lookup_matrix, content_matrix))
    kept = lax.dynamic_index_in_dim(packed, seq_index, 1, keepdims=False)
    sent = lax.dynamic_index_in_dim(packed, 1 - seq_index, 1, keepdims=False)
    heads_matrix = lax.all_gather(
        pair_up(kept, swap_seq(sent), seq_index), "dp", axis=1, tiled=True
    ).reshape(width, 3 * half_width)

    smoothed_gate = jax.nn.sigmoid(
        (pair_gate_scores + gate_random_jitter) / softening_scale[:, None, None]
    )
    mask_rows = tsize // (2 * dp_size)
    mask_low = smoothed_gate.astype(bf16).reshape(2, half_heads, mask_rows, tsize)
    kept = lax.dynamic_index_in_dim(mask_low, seq_index, 0, keepdims=False)
    sent = lax.dynamic_index_in_dim(mask_low, 1 - seq_index, 0, keepdims=False)
    own_mask = lax.all_gather(
        pair_up(kept, swap_seq(sent), seq_index).transpose(1, 0, 2, 3), "dp", axis=2, tiled=True
    ).reshape(half_heads, tsize, tsize)

    layer_matrix = lax.all_gather(
        jnp.concatenate(
            [mixing_result_matrix, expand_matrix, contract_matrix.reshape(share, inner)], axis=1
        ),
        ("seq", "dp"),
        axis=0,
        tiled=True,
    )
    output_matrix = layer_matrix[:, :width]
    inner_matrix = layer_matrix[:, width : width + inner]
    outer_matrix = layer_matrix[:, width + inner :].reshape(inner, width)

    segments = word_segment_ids[0]
    values_range = jnp.arange(8, dtype=jnp.int32)[:, None]
    segment_ends = jnp.sum((segments[None, :] <= values_range).astype(jnp.int32), axis=1)
    row_end = jnp.sum(
        jnp.where(segments[None, :] == values_range, segment_ends[:, None], 0), axis=0
    )
    counts = (row_end.reshape(-1, TILE)[:, -1] + (TILE - 1)) // TILE
    row_end = row_end[None]
    seq_scalar = seq_index[None].astype(jnp.int32)
    start = grid_coordinates[0, 0]
    turned = (jnp.arange(tsize, dtype=jnp.int32) + start) % tsize
    turn = (turned[:, None] == jnp.arange(tsize, dtype=jnp.int32)[None, :]).astype(bf16)
    tables = jnp.einsum("hab,cb->hca", own_mask, turn, preferred_element_type=f32).astype(bf16)
    tables = jnp.einsum("hca,da->hcd", tables, turn, preferred_element_type=f32) * (4.0 * LOG2E)

    own_columns = lambda index: lax.dynamic_slice_in_dim(
        vector(index), seq_index * half_width, half_width
    ).reshape(pairs, 128)
    query_shift, value_shift = own_columns(0), own_columns(1)
    heads_shift = jnp.stack([query_shift, jnp.zeros_like(query_shift), value_shift], axis=1)
    both_inputs = jnp.concatenate([inputs, other_inputs], axis=0)
    heads_rows = (matmul(both_inputs, heads_matrix) + heads_shift.reshape(-1)).astype(bf16)
    own_attended, own_attended_wide, logsum = attend(
        heads_rows, tables, row_end, counts, seq_scalar, score_scale
    )
    their_attended = swap_seq(own_attended[rows:])
    attended = pair_up(own_attended[:rows], their_attended, seq_index)
    attended = jnp.concatenate([attended[0], attended[1]], axis=1)

    first_scale, first_offset = vector(3), vector(4)
    second_scale, second_offset = vector(6), vector(7)
    projected = matmul(attended, output_matrix) + vector(2)
    first_out, first_normed, first_rstdev = norm_forward(
        inputs.astype(f32) + projected, first_scale, first_offset
    )
    first_low = first_out.astype(bf16)
    inner_pre = matmul(first_low, inner_matrix) + vector(8, expand_shift.shape[0])
    active_low = jax.nn.gelu(inner_pre).astype(bf16)
    outer_pre = matmul(active_low, outer_matrix) + vector(5)
    second, second_normed, second_rstdev = norm_forward(
        first_out + outer_pre, second_scale, second_offset
    )
    layer_out = second.astype(bf16)

    grad_out = upstream_derivative[0].astype(f32)
    grad_sum, grad_second_gain, grad_second_shift = norm_backward(
        grad_out, second_normed, second_rstdev, second_scale
    )
    grad_outer_low = grad_sum.astype(bf16)
    grad_active = times_transpose(grad_outer_low, outer_matrix)
    unused_value, gelu_pull = jax.vjp(jax.nn.gelu, inner_pre)
    grad_inner_low = gelu_pull(grad_active)[0].astype(bf16)
    grad_first = grad_sum + times_transpose(grad_inner_low, inner_matrix)
    grad_summed, grad_first_gain, grad_first_shift = norm_backward(
        grad_first, first_normed, first_rstdev, first_scale
    )
    grad_proj_low = grad_summed.astype(bf16)
    grad_attended = times_transpose(grad_proj_low, output_matrix).astype(bf16)
    grad_halves = grad_attended.reshape(rows, 2, half_width)
    own_grad = lax.dynamic_index_in_dim(grad_halves, seq_index, 1, keepdims=False)
    sent_grad = lax.dynamic_index_in_dim(grad_halves, 1 - seq_index, 1, keepdims=False)
    grads_all = jnp.concatenate([own_grad, swap_seq(sent_grad)], axis=0)

    grad_outer_weight = contract_rows(active_low, grad_outer_low).astype(bf16)
    grad_inner_weight = contract_rows(first_low, grad_inner_low).astype(bf16)
    grad_output_weight = contract_rows(attended, grad_proj_low).astype(bf16)
    layer_grad = lax.psum_scatter(
        jnp.concatenate(
            [grad_output_weight, grad_inner_weight, grad_outer_weight.reshape(width, inner)], axis=1
        ),
        ("seq", "dp"),
        scatter_dimension=0,
        tiled=True,
    ).astype(f32)

    grad_heads, grad_tables = attend_back(
        heads_rows, grads_all, own_attended_wide, tables, row_end, logsum, counts, seq_scalar, score_scale
    )
    grad_input_parts = times_transpose(grad_heads, heads_matrix)
    their_part = swap_seq(grad_input_parts[rows:].astype(bf16))
    input_grad = grad_summed + grad_input_parts[:rows] + their_part.astype(f32)
    grad_heads_weight = contract_rows(both_inputs, grad_heads).astype(bf16)

    grad_tables = jnp.einsum(
        "da,hcd->hac", turn, grad_tables.astype(bf16), preferred_element_type=f32
    ).astype(bf16)
    grad_mask = jnp.einsum("hac,cb->hab", grad_tables, turn, preferred_element_type=f32).astype(bf16)
    mask_sum = lax.psum_scatter(
        grad_mask.reshape(half_heads, 2, tsize // 2, tsize), "dp", scatter_dimension=2, tiled=True
    ).astype(f32)
    heads_sum = lax.psum_scatter(
        grad_heads_weight.reshape(2, half_width, 3 * half_width), "dp", scatter_dimension=1, tiled=True
    ).astype(f32)
    kept = lax.dynamic_index_in_dim(mask_sum, seq_index, 1, keepdims=False)
    sent = lax.dynamic_index_in_dim(mask_sum, 1 - seq_index, 1, keepdims=False)
    mask_grad = pair_up(kept, swap_seq(sent), seq_index).reshape(heads, mask_rows, tsize)
    mask_logits_gradient = (
        4.0 * mask_grad * smoothed_gate * (1.0 - smoothed_gate) / softening_scale[:, None, None]
    )
    kept = lax.dynamic_index_in_dim(heads_sum, seq_index, 0, keepdims=False)
    sent = lax.dynamic_index_in_dim(heads_sum, 1 - seq_index, 0, keepdims=False)
    heads_grad = pair_up(kept, swap_seq(sent), seq_index).reshape(2, share, pairs, 3, 128)
    heads_grad = heads_grad.transpose(3, 1, 0, 2, 4).reshape(3, share, width)

    head_bias = jnp.sum(grad_heads.astype(f32), axis=0).reshape(pairs, 3, 128)

    def spread(part):
        return lax.dynamic_update_slice_in_dim(
            jnp.zeros((width,), f32), part.reshape(half_width), seq_index * half_width, 0
        )

    sums = sum_small(
        jnp.concatenate(
            [
                spread(head_bias[:, 0]),
                spread(head_bias[:, 2]),
                jnp.sum(grad_proj_low.astype(f32), axis=0),
                grad_first_gain,
                grad_first_shift,
                jnp.sum(grad_outer_low.astype(f32), axis=0),
                grad_second_gain,
                grad_second_shift,
                jnp.sum(grad_inner_low.astype(f32), axis=0),
            ]
        )
    )
    owner = seq_index * dp_size + dp_index

    def piece(index, size=share):
        return lax.dynamic_slice_in_dim(sums, index * width + owner * size, size)

    return (
        layer_out[None],
        input_grad[None],
        heads_grad[0],
        piece(0),
        heads_grad[1],
        heads_grad[2],
        piece(1),
        layer_grad[:, :width],
        piece(2),
        piece(3),
        piece(4),
        layer_grad[:, width : width + inner],
        piece(8, expand_shift.shape[0]),
        layer_grad[:, width + inner :].reshape(contract_matrix.shape),
        piece(5),
        piece(6),
        piece(7),
        mask_logits_gradient,
    )


def solution(mesh):
    return jax.shard_map(
        body,
        mesh=mesh,
        in_specs=(
            P("dp", "seq", None),
            P("dp", "seq", None),
            P("dp", None),
            P("dp", None),
            P(("seq", "dp"), None),
            P(("seq", "dp")),
            P(("seq", "dp"), None),
            P(("seq", "dp"), None),
            P(("seq", "dp")),
            P(("seq", "dp"), None),
            P(("seq", "dp")),
            P(("seq", "dp")),
            P(("seq", "dp")),
            P(("seq", "dp"), None),
            P(("seq", "dp")),
            P(("seq", "dp"), None),
            P(("seq", "dp")),
            P(("seq", "dp")),
            P(("seq", "dp")),
            P(None, ("seq", "dp"), None),
            P(None, ("seq", "dp"), None),
            P(),
        ),
        out_specs=(
            P("dp", "seq", None),
            P("dp", "seq", None),
            P(("seq", "dp"), None),
            P(("seq", "dp")),
            P(("seq", "dp"), None),
            P(("seq", "dp"), None),
            P(("seq", "dp")),
            P(("seq", "dp"), None),
            P(("seq", "dp")),
            P(("seq", "dp")),
            P(("seq", "dp")),
            P(("seq", "dp"), None),
            P(("seq", "dp")),
            P(("seq", "dp"), None),
            P(("seq", "dp")),
            P(("seq", "dp")),
            P(("seq", "dp")),
            P(None, ("seq", "dp"), None),
        ),
        check_vma=False,
    )
```

time: 2550 us -> 712 us (0.28)
  waiting for transfers between devices: 1140 us -> 282 us
  local copies, waits for them, and re-layouts: 538 us -> 72.2 us
  matrix products: 477 us -> 120 us
  other arithmetic: 269 us -> 30.7 us
  Pallas kernels: 0 us -> 160 us
  blocking collectives: 83 us -> 0 us
    reduce_scatter x6 -> x2, waiting for transfers between devices: 582 us -> 152 us  [the longest x1 139 us: body(): lax.psum_scatter(jnp.concatenate([grad_output_weight, grad_inner_weight,...]
    dot_general x42 -> x2, matrix products: 356 us -> 16.3 us  [the longest x1 8.28 us: body(): jnp.einsum('hac,cb->hab', grad_tables, turn, preferred_element_type=f32)]
    unnamed x21 -> x7, waiting for transfers between devices: 318 us -> 0.1 us
    mul x12 -> x0, local copies, waits for them, and re-layouts: 247 us -> none  [group_scores(): logits = logits + 4.0 * picked.astype(jnp.float32)]
    all_gather x9 -> x3, waiting for transfers between devices: 241 us -> 33.3 us  [the longest x1 33.3 us: body(): lax.all_gather(pair_up(kept, swap_seq(sent), seq_index).transpose(1, 0, 2...]
    pallas_call x0 -> x2, Pallas kernels: none -> 160 us  [the longest x1 88.2 us: attend_back(): pl.pallas_call(functools.partial(attend_back_kernel, half, score_scale *...]
    reduce_sum x16 -> x5, other arithmetic: 121 us -> 7.58 us  [the longest x1 3.2 us: body(): head_bias = jnp.sum(grad_heads.astype(f32), axis=0).reshape(pairs, 3, 128)]
    reshape x6 -> x7, local copies, waits for them, and re-layouts: 119 us -> 18.1 us  [the longest x1 8.64 us: body(): grad_outer_weight.reshape(width, inner)]
  transfers between devices with their start and end apart: 18 -> 24, of which waited for: 15 -> 17; matrix products, arithmetic and copies ran while one was open for 20% -> 15% of each run, Pallas kernels for 0% -> 10%
where the time goes in v1:
time: 712 us; the launch traced here: 703 us
  waiting for transfers between devices  282 us (40%)
  Pallas kernels  160 us (22%)
  matrix products  120 us (17%)
  local copies, waits for them, and re-layouts  72.2 us (10%)
  other arithmetic  30.7 us (4%)
  starting transfers between devices  23.2 us (3%)
  between operations  15.5 us (2%)
    reduce_scatter x1, waiting for transfers between devices, body(): lax.psum_scatter(jnp.concatenate([grad_output_weight, grad_inner_weight,...  139 us
    pallas_call x1, Pallas kernels, attend_back(): pl.pallas_call(functools.partial(attend_back_kernel, half, score_scale *...  88.2 us
    pallas_call x1, Pallas kernels, attend(): pl.pallas_call(functools.partial(attend_kernel, half, score_scale * LOG2E...  72 us
    ppermute x10, waiting for transfers between devices, flip_bit(): return lax.ppermute(value, axis, [(i, i ^ bit) for i in range(count)])  58.5 us
    ppermute x8, waiting for transfers between devices, swap_seq(): return lax.ppermute(value, 'seq', [(0, 1), (1, 0)])  38.2 us
    dot_general x4, matrix products, times_transpose(): jnp.einsum('re,de->rd', left_side, right_side, preferred_element_type=jnp...  37.3 us
    dot_general x4, matrix products, matmul(): return jnp.dot(left_side, right_side, preferred_element_type=jnp.float32)  33.7 us
    all_gather x1, waiting for transfers between devices, body(): lax.all_gather(pair_up(kept, swap_seq(sent), seq_index).transpose(1, 0, 2...  33.3 us
  transfers between devices with their start and end apart: 24, of which 17 were waited for; matrix products, arithmetic and copies ran while one was open for 15% of the time, Pallas kernels for 10%

profile of v1, /device:TPU:0, one launch (start us, length us, event | category | flops | bytes accessed | tf_op | source)
XLA Modules:
  0.0 703.2 jit_solution(376945908197122108)
XLA Ops:
  10.3 3.0 collective-permute-start.1
  13.3 2.1 collective-permute-done.1
  18.3 2.1 collective-permute-start.7
  20.4 2.6 collective-permute-done.7
  25.8 2.1 collective-permute-start
  35.5 2.6 collective-permute-start.5
  41.1 22.1 %collective-permute-done.6 = bf16[16,288]{1,0:T(8,128)(2,1)S(1)} collective-permute-done((bf16[16,288]{1,0:T(8,128)(2,1)S(1)}, bf16[16,288]{1,0:T(8,128)(2,1)S(1)}, u32[]{:S(2)}, u32[]{:S(2)}) %collective-permute-start.6) | collective-permute-done | bytes 9248 | tf_op jit(solution)/shard_map/ppermute | solution.py:264
  63.8 8.4 %add_convert_fusion.qkv_ref = bf16[2048,1152]{1,0:T(8,128)(2,1)} fusion(bf16[768,1152]{1,0:T(8,128)(2,1)} %bitcast.155, f32[1152]{0:T(1024)S(1)} %add.224, bf16[1024,768]{0,1:T(8,128)(2,1)} %collective-permute-done, bf16[1024,768]{0,1:T(8,128)(2,1)S(1)} %bitcast.145), kind=kOutput, calls=%fused_computation.13 | convolution fusion | flops 3634888704 | bytes 9638400 | tf_op jit(solution)/shard_map/dot_general | solution.py:226
  72.2 33.3 %all-gather.6.cloned.1.call-done = bf16[6,2,256,512]{3,2,1,0:T(8,128)(2,1)} async-done(((bf16[6,2,16,512]{3,2,1,0:T(8,128)(2,1)}), bf16[6,2,256,512]{3,2,1,0:T(8,128)(2,1)}) %all-gather.6.cloned.1.call-update) | async-done | bytes 3145744 | tf_op jit(solution)/shard_map/all_gather | solution.py:370
  105.5 8.0 %broadcast_multiply_fusion.tab_ref = f32[6,512,512]{2,1,0:T(8,128)} fusion(bf16[6,512,512]{2,1,0:T(8,128)(2,1)} %bitcast.154, s32[512]{0:T(512)S(1)} %add_select_fusion), kind=kOutput, calls=%fused_computation.55 | convolution fusion | flops 3224895488 | bytes 9439232 | tf_op jit(solution)/shard_map/hca,da->hcd/dot_general | solution.py:399
  113.5 2.5 copy-done
  116.0 72.0 %attend.1 = (bf16[2048,384]{1,0:T(8,128)(2,1)S(1)}, f32[2048,384]{1,0:T(8,128)S(1)}, f32[3,8,2048]{2,1,0:T(8,128)S(1)}) custom-call(s32[1]{0:T(128)} %bitcast.1.s_ref, s32[8]{0:T(128)S(1)} %and_select_fusion.nk_ref, bf16[2048,1152]{1,0:T(8,128)(2,1)S(1)} %copy-done, f32[6,512,512]{2,1,0:T(8,128)} %broadcast_multiply_fusion.tab_ref, s32[1,2048]{1,0:T(1,128)S(1)} %bitcast.137), custom_call_target="tpu_custom_call" | custom-call | tf_op jit(solution)/shard_map/attend/pallas_call | solution.py:112
  191.6 2.9 copy.105
  195.2 14.9 %collective-permute-done.8 = bf16[1024,384]{1,0:T(8,128)(2,1)} collective-permute-done((bf16[1024,384]{1,0:T(8,128)(2,1)}, bf16[1024,384]{1,0:T(8,128)(2,1)}, u32[]{:S(2)}, u32[]{:S(2)}) %collective-permute-start.8) | collective-permute-done | bytes 786464 | tf_op jit(solution)/shard_map/ppermute | solution.py:254
  210.1 2.7 broadcast_select_fusion.1
  212.7 3.9 fusion.98
  218.7 4.8 slice.123
  223.5 8.5 %reshape.219 = bf16[3072,768]{1,0:T(8,128)(2,1)} reshape(bf16[768,3072]{1,0:T(8,128)(2,1)} %slice.123) | data formatting | bytes 9437184 | tf_op jit(solution)/shard_map/reshape | solution.py:384
  232.0 11.2 %fusion.9 = f32[1024,3072]{1,0:T(8,128)} fusion(bf16[768,6912]{1,0:T(8,128)(2,1)} %all-gather.8.cloned.1.call-done, f32[1024,768]{0,1:T(8,128)} %copy-done.7, f32[768]{0:T(1024)S(1)} %reshape.230, f32[768]{0:T(1024)S(1)} %reshape.229, f32[1024]{0:T(1024)S(1)} %add_rsqrt_fusion.1, f32[1024]{0:T(1024)S(1)} %broadcast_multiply_fusion.6), kind=kOutput, calls=%fused_computation.18 | convolution fusion | flops 4835770368 | bytes 20461568 | tf_op jit(solution)/shard_map/dot_general | solution.py:226
  243.2 10.1 %fusion.99 = (f32[1024]{0:T(1024)S(1)}, f32[1024,768]{0,1:T(8,128)S(1)}) fusion(f32[768]{0:T(1024)S(1)} %reshape.232, bf16[3072,768]{1,0:T(8,128)(2,1)S(1)} %copy-done.13, f32[1024,3072]{1,0:T(8,128)} %fusion.9, f32[3072]{0:T(1024)S(1)} %reshape.231, f32[768]{0:T(1024)S(1)} %reshape.230, f32[768]{0:T(1024)S(1)} %reshape.229, ...), kind=kOutput, calls=%fused_computation.204 | convolution fusion | flops 4868799488 | bytes 23626752 | tf_op jit(solution)/shard_map/dot_general | solution.py:226
  256.1 3.0 convert_reduce_fusion.3
  259.1 17.0 %convert_reduce_fusion = (f32[3072]{0:T(1024)S(1)}, bf16[1024,3072]{1,0:T(8,128)(2,1)}) fusion(f32[1024,3072]{1,0:T(8,128)} %fusion.9, f32[3072]{0:T(1024)S(1)} %reshape.231, bf16[1024,768]{0,1:T(8,128)(2,1)S(1)} %get-tuple-element.128, bf16[3072,768]{1,0:T(8,128)(2,1)S(1)} %copy-done.13), kind=kOutput, calls=%fused_computation.9 | convolution fusion | flops 4904186880 | bytes 25190400 | tf_op jit(solution)/shard_map/re,de->rd/dot_general | solution.py:234
  276.1 10.6 %multiply_reduce_fusion = (f32[768]{0:T(1024)S(1)}, f32[1024]{0:T(1024)S(1)}, f32[1024]{0:T(1024)S(1)}, f32[768]{0:T(1024)S(1)}, f32[1024,768]{0,1:T(8,128)S(1)}) fusion(f32[1024,768]{0,1:T(8,128)S(1)} %copy-done.8, f32[1024]{0:T(1024)S(1)} %add_rsqrt_fusion.1, f32[1024]{0:T(1024)S(1)} %broadcast_multiply_fusion.6, f32[768]{0:T(1024)S(1)} %reshape.229, ...), kind=kOutput, calls=%fused_computation.45 | convolution fusion | flops 4845989888 | bytes 22065152 | tf_op jit(solution)/shard_map/re,de->rd/dot_general | solution.py:234
  287.9 3.5 convolution_convert_fusion.3
  292.8 2.3 copy.125
  296.5 2.3 copy.124
  298.8 16.6 %collective-permute-done.9 = bf16[1024,384]{1,0:T(8,128)(2,1)} collective-permute-done((bf16[1024,384]{1,0:T(8,128)(2,1)}, bf16[1024,384]{1,0:T(8,128)(2,1)}, u32[]{:S(2)}, u32[]{:S(2)}) %collective-permute-start.9) | collective-permute-done | bytes 786464 | tf_op jit(solution)/shard_map/ppermute | solution.py:254
  317.0 2.3 copy-done.1
  319.3 88.2 %attend_back.1 = (bf16[2048,1152]{1,0:T(8,128)(2,1)S(1)}, f32[6,512,512]{2,1,0:T(8,128)}) custom-call(s32[1]{0:T(128)} %bitcast.1.s_ref, s32[8]{0:T(128)S(1)} %and_select_fusion.nk_ref, bf16[2048,1152]{1,0:T(8,128)(2,1)S(1)} %copy-done.1, bf16[2048,384]{1,0:T(8,128)(2,1)S(1)} %pad_maximum_fusion.5.grad_ref, f32[2048,384]{1,0:T(8,128)S(1)} %get-tuple-element.24.o32_ref, ...), custom_call_target="tpu_custom_call" | custom-call | tf_op jit(solution)/shard_map/attend_back/pallas_call | solution.py:213
  407.5 6.8 convolution_convert_fusion.2
  418.7 3.8 convolution_convert_fusion.4
  422.5 2.4 copy.114
  424.9 8.3 %fusion.33 = bf16[6,512,512]{2,1,0:T(8,128)(2,1)} fusion(f32[6,512,512]{2,1,0:T(8,128)} %get-tuple-element.27, s32[512]{0:T(512)S(1)} %add_select_fusion), kind=kOutput, calls=%fused_computation.61 | convolution fusion | flops 3226468352 | bytes 9439232 | tf_op jit(solution)/shard_map/hac,cb->hab/dot_general | solution.py:472
  434.6 13.2 %convolution_convert_fusion = bf16[3072,768]{1,0:T(8,128)(2,1)} fusion(bf16[1024,768]{0,1:T(8,128)(2,1)S(1)} %copy-done.20, f32[1024,3072]{1,0:T(8,128)} %fusion.9, f32[3072]{0:T(1024)S(1)} %reshape.231), kind=kOutput, calls=%fused_computation.14 | convolution fusion | flops 4865654784 | bytes 18886656 | tf_op jit(solution)/shard_map/rd,re->de/dot_general | solution.py:230
  447.8 8.6 %reshape.223 = bf16[768,3072]{1,0:T(8,128)(2,1)} reshape(bf16[3072,768]{1,0:T(8,128)(2,1)} %convolution_convert_fusion) | data formatting | bytes 9437184 | tf_op jit(solution)/shard_map/reshape | solution.py:454
  456.5 8.5 %convolution_convert_fusion.1 = bf16[768,3072]{1,0:T(8,128)(2,1)S(1)} fusion(bf16[1024,3072]{1,0:T(8,128)(2,1)} %get-tuple-element.183, f32[1024,768]{0,1:T(8,128)S(1)} %copy-done.9, f32[768]{0:T(1024)S(1)} %reshape.230, f32[768]{0:T(1024)S(1)} %reshape.229, f32[1024]{0:T(1024)S(1)} %add_rsqrt_fusion.1, f32[1024]{0:T(1024)S(1)} %broadcast_multiply_fusion.6), kind=kOutput, calls=%fused_computation.15 | convolution fusion | flops 4838129664 | bytes 14170112 | tf_op jit(solution)/shard_map/rd,re->de/dot_general | solution.py:230
  465.0 4.7 pad_maximum_fusion
  471.4 3.2 convert_reduce_fusion.1
  474.6 6.2 fusion.100
  480.8 2.6 copy-done.15
  487.8 4.0 collective-permute-done.13
  491.9 3.8 collective-permute-done.14
  495.7 4.9 collective-permute-done.15
  503.0 18.4 %collective-permute-done.16 = f32[9216]{0:T(1024)S(1)} collective-permute-done((f32[9216]{0:T(1024)S(1)}, f32[9216]{0:T(1024)S(1)}, u32[]{:S(2)}, u32[]{:S(2)}) %collective-permute-start.16) | collective-permute-done | bytes 36896 | tf_op jit(solution)/shard_map/ppermute | solution.py:264
  525.6 4.2 fusion.21
  529.9 2.4 copy.117
  532.4 12.7 %reduce-scatter.8.cloned.1.call-done = bf16[6,2,16,512]{3,2,1,0:T(8,128)(2,1)} async-done(((bf16[6,2,256,512]{3,2,1,0:T(8,128)(2,1)}), bf16[6,2,16,512]{3,2,1,0:T(8,128)(2,1)}) %reduce-scatter.8.cloned.1.call-update) | async-done | bytes 196624 | tf_op jit(solution)/shard_map/reduce_scatter | solution.py:473
  552.9 139.1 %reduce-scatter.6.cloned.1.call-done = bf16[24,6912]{1,0:T(8,128)(2,1)} async-done(((bf16[768,6912]{1,0:T(8,128)(2,1)}), bf16[24,6912]{1,0:T(8,128)(2,1)}) %reduce-scatter.6.cloned.1.call-update) | async-done | bytes 331792 | tf_op jit(solution)/shard_map/reduce_scatter | solution.py:452
  (225 shorter events, 64.2 us)
Async XLA Ops:
  7.2 16.6 %copy-start.22 = (bf16[96,768]{1,0:T(8,128)(2,1)S(1)}, bf16[96,768]{1,0:T(8,128)(2,1)}, u32[]{:S(2)}) copy-start(bf16[96,768]{1,0:T(8,128)(2,1)} %param.37) | copy-start | bytes 442372
  7.2 16.7 %copy-start.24 = (bf16[24,768]{1,0:T(8,128)(2,1)S(1)}, bf16[24,768]{1,0:T(8,128)(2,1)}, u32[]{:S(2)}) copy-start(bf16[24,768]{1,0:T(8,128)(2,1)} %param.31) | copy-start | bytes 110596
  7.2 16.7 %copy-start.23 = (bf16[24,3072]{1,0:T(8,128)(2,1)S(1)}, bf16[24,3072]{1,0:T(8,128)(2,1)}, u32[]{:S(2)}) copy-start(bf16[24,3072]{1,0:T(8,128)(2,1)} %param.35) | copy-start | bytes 442372
  7.2 17.5 %copy-start.27 = (bf16[24]{0:T(256)(128)(2,1)S(1)}, bf16[24]{0:T(256)(128)(2,1)}, u32[]{:S(2)}) copy-start(bf16[24]{0:T(256)(128)(2,1)} %param.27) | copy-start | bytes 148
  7.2 17.5 %copy-start.28 = (bf16[24]{0:T(256)(128)(2,1)S(1)}, bf16[24]{0:T(256)(128)(2,1)}, u32[]{:S(2)}) copy-start(bf16[24]{0:T(256)(128)(2,1)} %param.30) | copy-start | bytes 148
  7.2 17.5 %copy-start.29 = (bf16[24]{0:T(256)(128)(2,1)S(1)}, bf16[24]{0:T(256)(128)(2,1)}, u32[]{:S(2)}) copy-start(bf16[24]{0:T(256)(128)(2,1)} %param.32) | copy-start | bytes 148
  7.3 17.5 %copy-start.30 = (bf16[24]{0:T(256)(128)(2,1)S(1)}, bf16[24]{0:T(256)(128)(2,1)}, u32[]{:S(2)}) copy-start(bf16[24]{0:T(256)(128)(2,1)} %param.33) | copy-start | bytes 148
  7.3 17.5 %copy-start.31 = (bf16[24]{0:T(256)(128)(2,1)S(1)}, bf16[24]{0:T(256)(128)(2,1)}, u32[]{:S(2)}) copy-start(bf16[24]{0:T(256)(128)(2,1)} %param.34) | copy-start | bytes 148
  7.3 17.5 %copy-start.35 = (bf16[96]{0:T(256)(128)(2,1)S(1)}, bf16[96]{0:T(256)(128)(2,1)}, u32[]{:S(2)}) copy-start(bf16[96]{0:T(256)(128)(2,1)} %param.36) | copy-start | bytes 580
  7.3 17.5 %copy-start.32 = (bf16[24]{0:T(256)(128)(2,1)S(1)}, bf16[24]{0:T(256)(128)(2,1)}, u32[]{:S(2)}) copy-start(bf16[24]{0:T(256)(128)(2,1)} %param.38) | copy-start | bytes 148
  7.3 17.5 %copy-start.33 = (bf16[24]{0:T(256)(128)(2,1)S(1)}, bf16[24]{0:T(256)(128)(2,1)}, u32[]{:S(2)}) copy-start(bf16[24]{0:T(256)(128)(2,1)} %param.39) | copy-start | bytes 148
  7.3 17.5 %copy-start.34 = (bf16[24]{0:T(256)(128)(2,1)S(1)}, bf16[24]{0:T(256)(128)(2,1)}, u32[]{:S(2)}) copy-start(bf16[24]{0:T(256)(128)(2,1)} %param.40) | copy-start | bytes 148
  7.3 17.7 %copy-start.16 = (bf16[1,1024,768]{2,1,0:T(8,128)(2,1)S(1)}, bf16[1,1024,768]{2,1,0:T(8,128)(2,1)}, u32[]{:S(2)}) copy-start(bf16[1,1024,768]{2,1,0:T(8,128)(2,1)} %param.22) | copy-start | bytes 4718596
  7.3 56.5 %all-gather.4.cloned.1.call-start = ((), (), s32[]{:S(2)}) async-start(), calls=%async_computation.3 | async-start | bytes 1880064 | tf_op jit(solution)/shard_map/all_gather | solution.py:359
  10.3 5.2 collective-permute-start.1
  16.2 89.3 %all-gather.6.cloned.1.call-start = ((), (), s32[]{:S(2)}) async-start(), calls=%async_computation.4 | async-start | bytes 3342336 | tf_op jit(solution)/shard_map/all_gather | solution.py:370
  18.3 9.6 %copy-start.25 = (s32[1,2048]{1,0:T(1,128)S(1)}, s32[1,2048]{1,0:T(1,128)}, u32[]{:S(2)}) copy-start(s32[1,2048]{1,0:T(1,128)} %param.25) | copy-start | bytes 24580
  18.3 4.7 collective-permute-start.7
  23.7 189.0 %all-gather.8.cloned.1.call-start = ((), (), s32[]{:S(2)}) async-start(), calls=%async_computation.5 | async-start | bytes 10948608 | tf_op jit(solution)/shard_map/all_gather | solution.py:374
  24.7 497.8 %reduce-scatter.10.cloned.1.call-start = ((), (), s32[]{:S(2)}) async-start(), calls=%async_computation.8 | async-start | bytes 1880064
  25.0 3.1 collective-permute-start.2
  25.8 46.4 %copy-start.17 = (bf16[1,1024,768]{1,2,0:T(8,128)(2,1)}, bf16[1,1024,768]{1,2,0:T(8,128)(2,1)S(1)}, u32[]{:S(2)}) copy-start(bf16[1,1024,768]{1,2,0:T(8,128)(2,1)S(1)} %copy.101) | copy-start | bytes 4718596
  25.8 38.0 %collective-permute-start = (bf16[1024,768]{0,1:T(8,128)(2,1)S(1)}, bf16[1024,768]{0,1:T(8,128)(2,1)}, u32[]{:S(2)}, u32[]{:S(2)}) collective-permute-start(bf16[1024,768]{0,1:T(8,128)(2,1)S(1)} %bitcast.144), channel_id=1, source_target_pairs={{0,16},{16,0},{1,17},{17,1},{2,18},{18,2},{3,19},{19,3},{4,20},{20... | collective-permute-start | bytes 4718600 | tf_op jit(solution)/shard_map/ppermute | solution.py:254
  28.1 3.6 collective-permute-start.3
  31.8 3.7 collective-permute-start.4
  35.5 4.6 collective-permute-start.5
  40.1 23.1 %collective-permute-start.6 = (bf16[16,288]{1,0:T(8,128)(2,1)S(1)}, bf16[16,288]{1,0:T(8,128)(2,1)S(1)}, u32[]{:S(2)}, u32[]{:S(2)}) collective-permute-start(bf16[16,288]{1,0:T(8,128)(2,1)S(1)} %pad_maximum_fusion.11), channel_id=1, source_target_pairs={{0,16},{16,0},{1,17},{17,1},{2,18},{18,2},{3,19},{19,3},{4,20},{20... | collective-permute-start | bytes 27656 | tf_op jit(solution)/shard_map/ppermute | solution.py:264
  190.2 19.9 %collective-permute-start.8 = (bf16[1024,384]{1,0:T(8,128)(2,1)}, bf16[1024,384]{1,0:T(8,128)(2,1)}, u32[]{:S(2)}, u32[]{:S(2)}) collective-permute-start(bf16[1024,384]{1,0:T(8,128)(2,1)} %slice.87), channel_id=1, source_target_pairs={{0,16},{16,0},{1,17},{17,1},{2,18},{18,2},{3,19},{19,3},{4,20},{20... | collective-permute-start | bytes 2359304 | tf_op jit(solution)/shard_map/ppermute | solution.py:254
  232.0 11.2 %copy-start.8 = (f32[1024,768]{0,1:T(8,128)S(1)}, f32[1024,768]{0,1:T(8,128)}, u32[]{:S(2)}) copy-start(f32[1024,768]{0,1:T(8,128)} %copy-done.7) | copy-start | bytes 9437188
  232.0 11.2 %copy-start.13 = (bf16[3072,768]{1,0:T(8,128)(2,1)S(1)}, bf16[3072,768]{1,0:T(8,128)(2,1)}, u32[]{:S(2)}) copy-start(bf16[3072,768]{1,0:T(8,128)(2,1)} %reshape.219) | copy-start | bytes 14155780
  259.1 17.0 %copy-start.19 = (bf16[1024,768]{0,1:T(8,128)(2,1)}, bf16[1024,768]{0,1:T(8,128)(2,1)S(1)}, u32[]{:S(2)}) copy-start(bf16[1024,768]{0,1:T(8,128)(2,1)S(1)} %get-tuple-element.128) | copy-start | bytes 4718596
  295.1 20.4 %collective-permute-start.9 = (bf16[1024,384]{1,0:T(8,128)(2,1)}, bf16[1024,384]{1,0:T(8,128)(2,1)}, u32[]{:S(2)}, u32[]{:S(2)}) collective-permute-start(bf16[1024,384]{1,0:T(8,128)(2,1)} %bitcast.148), channel_id=1, source_target_pairs={{0,16},{16,0},{1,17},{17,1},{2,18},{18,2},{3,19},{19,3},{4,20},{20... | collective-permute-start | bytes 2359304 | tf_op jit(solution)/shard_map/ppermute | solution.py:254
  319.3 88.2 %copy-start.18 = (bf16[1,1024,768]{1,2,0:T(8,128)(2,1)S(1)}, bf16[1,1024,768]{1,2,0:T(8,128)(2,1)}, u32[]{:S(2)}) copy-start(bf16[1,1024,768]{1,2,0:T(8,128)(2,1)} %copy-done.17) | copy-start | bytes 4718596
  417.6 127.5 %reduce-scatter.8.cloned.1.call-start = ((), (), s32[]{:S(2)}) async-start(), calls=%async_computation.7 | async-start | bytes 3342336 | tf_op jit(solution)/shard_map/reduce_scatter | solution.py:473
  433.2 258.7 %reduce-scatter.6.cloned.1.call-start = ((), (), s32[]{:S(2)}) async-start(), calls=%async_computation.6 | async-start | bytes 10948608 | tf_op jit(solution)/shard_map/reduce_scatter | solution.py:452
  447.8 8.6 %copy-start.9 = (f32[1024,768]{0,1:T(8,128)S(1)}, f32[1024,768]{0,1:T(8,128)}, u32[]{:S(2)}) copy-start(f32[1024,768]{0,1:T(8,128)} %copy-done.7) | copy-start | bytes 9437188
  456.4 8.6 %copy-start.14 = (bf16[768,768]{1,0:T(8,128)(2,1)S(1)}, bf16[768,768]{1,0:T(8,128)(2,1)}, u32[]{:S(2)}) copy-start(bf16[768,768]{1,0:T(8,128)(2,1)} %copy.114) | copy-start | bytes 3538948
  483.4 17.7 %copy-start.12 = (bf16[1,1024,768]{1,2,0:T(8,128)(2,1)S(1)}, bf16[1,1024,768]{1,2,0:T(8,128)(2,1)}, u32[]{:S(2)}) copy-start(bf16[1,1024,768]{1,2,0:T(8,128)(2,1)} %get-tuple-element.133) | copy-start | bytes 4718596
  483.7 41.9 %collective-permute-start.10 = (bf16[1024,768]{0,1:T(8,128)(2,1)S(1)}, bf16[1024,768]{0,1:T(8,128)(2,1)}, u32[]{:S(2)}, u32[]{:S(2)}) collective-permute-start(bf16[1024,768]{0,1:T(8,128)(2,1)S(1)} %slice.225), channel_id=1, source_target_pairs={{0,16},{16,0},{1,17},{17,1},{2,18},{18,2},{3,19},{19,3},{4,20},{20... | collective-permute-start | bytes 4718600 | tf_op jit(solution)/shard_map/ppermute | solution.py:254
  485.6 2.2 collective-permute-start.12
  487.8 4.0 collective-permute-start.13
  491.8 4.0 collective-permute-start.14
  495.7 4.9 collective-permute-start.15
  500.6 20.7 %collective-permute-start.16 = (f32[9216]{0:T(1024)S(1)}, f32[9216]{0:T(1024)S(1)}, u32[]{:S(2)}, u32[]{:S(2)}) collective-permute-start(f32[9216]{0:T(1024)S(1)} %add.254), channel_id=1, source_target_pairs={{0,16},{16,0},{1,17},{17,1},{2,18},{18,2},{3,19},{19,3},{4,20},{20... | collective-permute-start | bytes 110600 | tf_op jit(solution)/shard_map/ppermute | solution.py:264
  524.2 8.1 %collective-permute-start.11 = (f32[24,1152]{1,0:T(8,128)}, f32[24,1152]{1,0:T(8,128)S(1)}, u32[]{:S(2)}, u32[]{:S(2)}) collective-permute-start(f32[24,1152]{1,0:T(8,128)} %dynamic-slice_bitcast_fusion.1), channel_id=1, source_target_pairs={{0,16},{16,0},{1,17},{17,1},{2,18},{18,2},{3,19},{19,3},{4,20},{20... | collective-permute-start | bytes 331784 | tf_op jit(solution)/shard_map/ppermute | solution.py:254
  532.2 19.8 %copy-start.21 = (f32[12,16,512]{2,1,0:T(8,128)S(1)}, f32[12,16,512]{2,1,0:T(8,128)}, u32[]{:S(2)}) copy-start(f32[12,16,512]{2,1,0:T(8,128)} %get-tuple-element.132) | copy-start | bytes 1179652
  532.2 19.8 %copy-start.26 = (f32[12]{0:T(128)S(1)}, f32[12]{0:T(128)}, u32[]{:S(2)}) copy-start(f32[12]{0:T(128)} %param.43) | copy-start | bytes 148
  546.2 5.7 collective-permute-start.17
  (13 other events, 39.2 us)
Sparse Core Ops, SparseCore 0:
  16.3 42.1 all-gather.3
  61.3 44.1 all-gather.5
  108.3 86.1 all-gather.7
  417.8 58.5 reduce-scatter.9
  480.0 65.0 reduce-scatter.7
  551.1 140.7 reduce-scatter.5

commit v2 on v1

v2 whole, which is shorter than its diff:
```python
import functools
import math

import jax
import jax.numpy as jnp
from jax import lax
from jax.experimental import pallas as pl
from jax.experimental.pallas import tpu as pltpu
from jax.sharding import PartitionSpec as P

EPSILON = 1e-06
LOG2E = math.log2(math.e)
MASKED = -1e30
TILE = 256
NT = (((1,), (1,)), ((), ()))
NN = (((1,), (0,)), ((), ()))
TN = (((0,), (0,)), ((), ()))


def dot(a, b, dims=NN):
    return lax.dot_general(a, b, dims, preferred_element_type=jnp.float32)


def local_row(block, seq_index, half_blocks):
    return ((block // half_blocks) ^ seq_index) * (half_blocks * TILE) + (block % half_blocks) * TILE


def split_pair(rows):
    lane = lax.broadcasted_iota(jnp.int32, rows.shape, 1)
    zero = jnp.zeros_like(rows)
    return jnp.where(lane < 64, rows, zero), jnp.where(lane < 64, zero, rows)


CHUNK = 512
BACK = 512


def chunk_row(block, seq_index, half_blocks):
    return pl.multiple_of(local_row(block, seq_index, half_blocks), TILE)


def attend_kernel(half_blocks, scale, s_ref, nk_ref, full_ref, qkv_ref, tab_ref, end_ref, att_ref, o32_ref, lse_ref, vt_ref, st_ref, acc_ref):
    seq_index = s_ref[0]
    table_size = tab_ref.shape[1]
    per = CHUNK // TILE
    pick = split_pair(jnp.ones((128, 128), jnp.bfloat16))
    reach = jnp.zeros((1, 1), jnp.float32)
    for half in pick:
        longest = []
        for at in (0, 128):
            part = qkv_ref[:, at : at + 128].astype(jnp.float32)
            squares = dot((part * part).astype(jnp.bfloat16), half, NT)
            longest.append(jnp.max(squares, keepdims=True))
        reach = jnp.maximum(reach, jnp.sqrt(longest[0]) * jnp.sqrt(longest[1]) * scale)
    small = reach[0, 0] < 80.0
    vt = qkv_ref[:, 256:384].astype(jnp.float32).T
    sub = lax.broadcasted_iota(jnp.int32, vt.shape, 0)
    vt_ref[0, 0:128] = jnp.where(sub < 64, vt, 0.0).astype(jnp.bfloat16)
    vt_ref[1, 0:128] = jnp.where(sub < 64, 0.0, vt).astype(jnp.bfloat16)
    sub = lax.broadcasted_iota(jnp.int32, (16, vt.shape[1]), 0)
    vt_ref[0, 128:144] = jnp.where(sub < 8, 1.0, 0.0).astype(jnp.bfloat16)
    vt_ref[1, 128:144] = jnp.where(sub < 8, 0.0, 1.0).astype(jnp.bfloat16)
    sub = lax.broadcasted_iota(jnp.int32, (CHUNK, TILE), 0)

    def query_block(block, carry):
        here = chunk_row(block, seq_index, half_blocks)
        queries = split_pair(qkv_ref[pl.ds(here, TILE), 0:128])
        at = pl.multiple_of(block * TILE, TILE)
        row_end = end_ref[0:1, pl.ds(at, TILE)]
        count = (nk_ref[block] + per - 1) // per
        full = full_ref[block] // CHUNK
        lane0 = pl.multiple_of((block * TILE) % table_size, TILE)

        def logits(j, masked):
            keys = qkv_ref[pl.ds(chunk_row(j * per, seq_index, half_blocks), CHUNK), 128:256]
            trow = pl.multiple_of((j * CHUNK) % table_size, CHUNK)
            out = []
            for h in range(2):
                x = dot(keys, queries[h], NT) * scale + tab_ref[h, pl.ds(trow, CHUNK), pl.ds(lane0, TILE)]
                if masked:
                    x = jnp.where(sub < row_end - j * CHUNK, x, MASKED)
                out.append(x)
            return out

        def accumulate(j, probs):
            there = chunk_row(j * per, seq_index, half_blocks)
            values = jnp.concatenate([vt_ref[h, :, pl.ds(there, CHUNK)] for h in range(2)], axis=1)
            acc_ref[...] += dot(values, jnp.concatenate([p.astype(jnp.bfloat16) for p in probs], axis=0))

        def finish(peak):
            acc = acc_ref[...]
            sums = [acc[128:129], acc[136:137]]
            out = jnp.concatenate([acc[0:64] / sums[0], acc[64:128] / sums[1]], axis=0).T
            o32_ref[pl.ds(here, TILE), :] = out
            att_ref[pl.ds(here, TILE), :] = out.astype(jnp.bfloat16)
            for h in range(2):
                lse_ref[0, h : h + 1, pl.ds(at, TILE)] = peak[h] + jnp.log2(sums[h])

        acc_ref[...] = jnp.zeros_like(acc_ref)

        @pl.when(small)
        def _():
            def step(masked, j, carry):
                accumulate(j, [jnp.exp2(x) for x in logits(j, masked)])
                return carry

            lax.fori_loop(0, full, functools.partial(step, False), 0)
            lax.fori_loop(full, count, functools.partial(step, True), 0)
            finish([0.0, 0.0])

        @pl.when(jnp.logical_not(small))
        def _():
            def score(j, peaks):
                out = []
                for h, x in enumerate(logits(j, True)):
                    st_ref[h, pl.ds(pl.multiple_of(j * CHUNK, CHUNK), CHUNK), :] = x
                    out.append(jnp.maximum(peaks[h], jnp.max(x.reshape(CHUNK // 8, 8, TILE), axis=0)))
                return tuple(out)

            start = jnp.full((8, TILE), MASKED, jnp.float32)
            peaks = lax.fori_loop(0, count, score, (start, start))
            peak = [jnp.max(p, axis=0, keepdims=True) for p in peaks]

            def mix(j, carry):
                at_chunk = pl.ds(pl.multiple_of(j * CHUNK, CHUNK), CHUNK)
                accumulate(j, [jnp.exp2(st_ref[h, at_chunk, :] - peak[h]) for h in range(2)])
                return carry

            lax.fori_loop(0, count, mix, 0)
            finish(peak)

        return carry

    lax.fori_loop(0, nk_ref.shape[0], query_block, 0)


def attend(qkv, tables, row_end, scalars, score_scale):
    rows = qkv.shape[0]
    pairs = qkv.shape[1] // 384
    tsize = tables.shape[1]
    spec = pltpu.PrefetchScalarGridSpec(
        num_scalar_prefetch=len(scalars),
        grid=(pairs,),
        in_specs=[
            pl.BlockSpec((rows, 384), lambda p, *_: (0, p)),
            pl.BlockSpec((2, tsize, tsize), lambda p, *_: (p, 0, 0)),
            pl.BlockSpec((1, rows), lambda p, *_: (0, 0)),
        ],
        out_specs=[
            pl.BlockSpec((rows, 128), lambda p, *_: (0, p)),
            pl.BlockSpec((rows, 128), lambda p, *_: (0, p)),
            pl.BlockSpec((1, 8, rows), lambda p, *_: (p, 0, 0)),
        ],
        scratch_shapes=[
            pltpu.VMEM((2, 144, rows), jnp.bfloat16),
            pltpu.VMEM((2, rows, TILE), jnp.float32),
            pltpu.VMEM((144, TILE), jnp.float32),
        ],
    )
    return pl.pallas_call(
        functools.partial(attend_kernel, rows // TILE // 2, score_scale * LOG2E),
        grid_spec=spec,
        out_shape=[
            jax.ShapeDtypeStruct((rows, pairs * 128), jnp.bfloat16),
            jax.ShapeDtypeStruct((rows, pairs * 128), jnp.float32),
            jax.ShapeDtypeStruct((pairs, 8, rows), jnp.float32),
        ],
        compiler_params=pltpu.CompilerParams(dimension_semantics=("arbitrary",), vmem_limit_bytes=40 << 20),
        cost_estimate=pl.CostEstimate(flops=8 * rows * rows * 128, transcendentals=2 * rows * rows, bytes_accessed=8 << 20),
        name="attend",
    )(*scalars, qkv, tables, row_end)


def attend_back_kernel(half_blocks, scale, score_scale, s_ref, nk_ref, full_ref, qkv_ref, grad_ref, o32_ref, tab_ref, end_ref, lse_ref,
                       turned_ref, back_ref, turn_ref, dqkv_ref, table_ref, weight_ref, bias_ref, gtab_ref, kt_ref, dk_ref, dv_ref, dq_ref):
    seq_index = s_ref[0]
    table_size = tab_ref.shape[1]
    per = BACK // TILE
    kt = qkv_ref[:, 128:256].astype(jnp.float32).T
    sub = lax.broadcasted_iota(jnp.int32, kt.shape, 0)
    kt_ref[0] = jnp.where(sub < 64, kt, 0.0).astype(jnp.bfloat16)
    kt_ref[1] = jnp.where(sub < 64, 0.0, kt).astype(jnp.bfloat16)
    dk_ref[...] = jnp.zeros_like(dk_ref)
    dv_ref[...] = jnp.zeros_like(dv_ref)
    gtab_ref[...] = jnp.zeros_like(gtab_ref)
    sub = lax.broadcasted_iota(jnp.int32, (BACK, TILE), 0)

    def query_block(block, carry):
        here = chunk_row(block, seq_index, half_blocks)
        queries = split_pair(qkv_ref[pl.ds(here, TILE), 0:128])
        grad_rows = grad_ref[pl.ds(here, TILE), :]
        grads = split_pair(grad_rows)
        at = pl.multiple_of(block * TILE, TILE)
        row_end = end_ref[0:1, pl.ds(at, TILE)]
        inner = (grad_rows.astype(jnp.float32) * o32_ref[pl.ds(here, TILE), :]).T
        delta = [jnp.sum(inner[0:64], axis=0, keepdims=True), jnp.sum(inner[64:128], axis=0, keepdims=True)]
        lse = [lse_ref[0, h : h + 1, pl.ds(at, TILE)] for h in range(2)]
        q_stack = jnp.concatenate(queries, axis=0)
        g_stack = jnp.concatenate(grads, axis=0)
        lane0 = pl.multiple_of((block * TILE) % table_size, TILE)
        count = (nk_ref[block] + per - 1) // per
        full = full_ref[block] // BACK
        dq_ref[...] = jnp.zeros_like(dq_ref)

        def step(masked, j, carry):
            rows_at = pl.ds(chunk_row(j * per, seq_index, half_blocks), BACK)
            keys = qkv_ref[rows_at, 128:256]
            values = qkv_ref[rows_at, 256:384]
            trow = pl.ds(pl.multiple_of((j * BACK) % table_size, BACK), BACK)
            probs, scores = [], []
            for h in range(2):
                x = dot(keys, queries[h], NT) * scale + tab_ref[h, trow, pl.ds(lane0, TILE)] - lse[h]
                if masked:
                    x = jnp.where(sub < row_end - j * BACK, x, MASKED)
                p = jnp.exp2(x)
                d = p * (dot(values, grads[h], NT) - delta[h])
                gtab_ref[h, trow, pl.ds(lane0, TILE)] += d
                probs.append(p.astype(jnp.bfloat16))
                scores.append(d.astype(jnp.bfloat16))
            dv_ref[rows_at, :] += dot(jnp.concatenate(probs, axis=1), g_stack)
            dk_ref[rows_at, :] += dot(jnp.concatenate(scores, axis=1), q_stack)
            kt = jnp.concatenate([kt_ref[h, :, rows_at] for h in range(2)], axis=1)
            dq_ref[...] += dot(kt, jnp.concatenate(scores, axis=0))
            return carry

        lax.fori_loop(0, full, functools.partial(step, False), 0)
        lax.fori_loop(full, count, functools.partial(step, True), 0)
        dqkv_ref[pl.ds(here, TILE), 0:128] = (dq_ref[...] * score_scale).T.astype(jnp.bfloat16)
        return carry

    lax.fori_loop(0, nk_ref.shape[0], query_block, 0)
    dqkv_ref[:, 128:256] = (dk_ref[...] * score_scale).astype(jnp.bfloat16)
    dqkv_ref[:, 256:384] = dv_ref[...].astype(jnp.bfloat16)
    bias_ref[...] = jnp.broadcast_to(
        jnp.sum(dqkv_ref[...].astype(jnp.float32), axis=0, keepdims=True), bias_ref.shape
    )
    for h in range(2):
        rows = dot(back_ref[...], gtab_ref[h].astype(jnp.bfloat16), NT).astype(jnp.bfloat16)
        table_ref[h] = dot(rows, turn_ref[...]).astype(jnp.bfloat16)

    def weights(i, carry):
        at = pl.ds(pl.multiple_of(i * 128, 128), 128)
        weight_ref[at, :] = dot(turned_ref[:, at], dqkv_ref[...], TN).astype(jnp.bfloat16)
        return carry

    lax.fori_loop(0, weight_ref.shape[0] // 128, weights, 0)


def attend_back(pair, qkv, grads, o32, tables, row_end, lse, turned, back, turn, scalars, score_scale):
    rows = qkv.shape[0]
    tsize = tables.shape[1]
    width = turned.shape[1]
    spec = pltpu.PrefetchScalarGridSpec(
        num_scalar_prefetch=len(scalars),
        grid=(1,),
        in_specs=[
            pl.BlockSpec((rows, 384), lambda p, *_: (0, pair)),
            pl.BlockSpec((rows, 128), lambda p, *_: (0, 0)),
            pl.BlockSpec((rows, 128), lambda p, *_: (0, pair)),
            pl.BlockSpec((2, tsize, tsize), lambda p, *_: (pair, 0, 0)),
            pl.BlockSpec((1, rows), lambda p, *_: (0, 0)),
            pl.BlockSpec((1, 8, rows), lambda p, *_: (pair, 0, 0)),
            pl.BlockSpec((rows, width), lambda p, *_: (0, 0)),
            pl.BlockSpec((tsize, tsize), lambda p, *_: (0, 0)),
            pl.BlockSpec((tsize, tsize), lambda p, *_: (0, 0)),
        ],
        out_specs=[
            pl.BlockSpec((rows, 384), lambda p, *_: (0, 0)),
            pl.BlockSpec((2, tsize, tsize), lambda p, *_: (0, 0, 0)),
            pl.BlockSpec((width, 384), lambda p, *_: (0, 0)),
            pl.BlockSpec((8, 384), lambda p, *_: (0, 0)),
        ],
        scratch_shapes=[
            pltpu.VMEM((2, tsize, tsize), jnp.float32),
            pltpu.VMEM((2, 128, rows), jnp.bfloat16),
            pltpu.VMEM((rows, 128), jnp.float32),
            pltpu.VMEM((rows, 128), jnp.float32),
            pltpu.VMEM((128, TILE), jnp.float32),
        ],
    )
    return pl.pallas_call(
        functools.partial(attend_back_kernel, rows // TILE // 2, score_scale * LOG2E, score_scale),
        grid_spec=spec,
        out_shape=[
            jax.ShapeDtypeStruct((rows, 384), jnp.bfloat16),
            jax.ShapeDtypeStruct((2, tsize, tsize), jnp.bfloat16),
            jax.ShapeDtypeStruct((width, 384), jnp.bfloat16),
            jax.ShapeDtypeStruct((8, 384), jnp.float32),
        ],
        compiler_params=pltpu.CompilerParams(dimension_semantics=("arbitrary",), vmem_limit_bytes=56 << 20),
        cost_estimate=pl.CostEstimate(flops=20 * rows * rows * 128, transcendentals=2 * rows * rows, bytes_accessed=12 << 20),
        name="attend_back",
    )(*scalars, qkv, grads, o32, tables, row_end, lse, turned, back, turn)

GELU_A = math.sqrt(2.0 / math.pi)
GELU_B = 0.044715


def row_stats(values):
    center = values - jnp.mean(values, axis=-1, keepdims=True)
    rstdev = lax.rsqrt(jnp.mean(center * center, axis=-1, keepdims=True) + EPSILON)
    return center * rstdev, rstdev


def row_back(gradient, normed, rstdev, gain):
    scaled = gradient * gain
    return rstdev * (
        scaled
        - jnp.mean(scaled, axis=-1, keepdims=True)
        - normed * jnp.mean(scaled * normed, axis=-1, keepdims=True)
    )


def layer_kernel(s_ref, *refs):
    f32, bf16 = jnp.float32, jnp.bfloat16
    (own_ref, their_ref, x_ref, up_ref, wide_ref, vec_ref, bias_ref,
     out_ref, gsum_ref, gatt_ref, att_ref, first_ref, active_ref, ginner_ref, gouter_ref, gproj_ref,
     vsum_ref, bsum_ref, slope_ref, acc_ref, n1_ref, f1_ref) = refs
    width = x_ref.shape[1]
    inner = active_ref.shape[1]
    step = width
    vec = lambda i: vec_ref[i : i + 1, :]
    total = lambda value: jnp.sum(value, axis=0, keepdims=True)

    def outer_rows(c):
        return wide_ref[:, pl.ds(pl.multiple_of(width + inner + c * step, 128), width)]

    @pl.when(pl.program_id(0) == 0)
    def _():
        vsum_ref[...] = jnp.zeros_like(vsum_ref)
        bsum_ref[...] = jnp.zeros_like(bsum_ref)

    first_seq = s_ref[0] == 0
    mine, others = own_ref[...], their_ref[...]

    @pl.when(first_seq)
    def _():
        att_ref[:, : width // 2] = mine
        att_ref[:, width // 2 :] = others

    @pl.when(jnp.logical_not(first_seq))
    def _():
        att_ref[:, : width // 2] = others
        att_ref[:, width // 2 :] = mine

    summed = x_ref[...].astype(f32) + (dot(att_ref[...], wide_ref[:, :width]) + vec(0))
    normed, rstdev1 = row_stats(summed)
    n1_ref[...] = normed
    first = normed * vec(1) + vec(2)
    f1_ref[...] = first
    first_ref[...] = first.astype(bf16)
    acc_ref[...] = jnp.zeros_like(acc_ref)

    def up(c, carry):
        at = pl.ds(pl.multiple_of(c * step, 128), step)
        w_at = pl.ds(pl.multiple_of(width + c * step, 128), step)
        u = dot(first_ref[...], wide_ref[:, w_at]) + bias_ref[0:1, at]
        square = u * u
        t = jnp.tanh(GELU_A * (u + GELU_B * (square * u)))
        half = 0.5 * (1.0 + t)
        slope_ref[:, at] = half + 0.5 * u * (1.0 - t * t) * (GELU_A * (1.0 + 3.0 * GELU_B * square))
        active = (u * half).astype(bf16)
        active_ref[:, at] = active
        acc_ref[...] += dot(active, outer_rows(c))
        return carry

    lax.fori_loop(0, inner // step, up, 0)
    normed, rstdev = row_stats(f1_ref[...] + (acc_ref[...] + vec(3)))
    out_ref[...] = (normed * vec(4) + vec(5)).astype(bf16)
    gradient = up_ref[...].astype(f32)
    vsum_ref[4:5, :] += total(gradient * normed)
    vsum_ref[5:6, :] += total(gradient)
    grad_sum = row_back(gradient, normed, rstdev, vec(4))
    grad_low = grad_sum.astype(bf16)
    gouter_ref[...] = grad_low
    vsum_ref[3:4, :] += total(grad_low.astype(f32))
    acc_ref[...] = grad_sum

    def down(c, carry):
        at = pl.ds(pl.multiple_of(c * step, 128), step)
        w_at = pl.ds(pl.multiple_of(width + c * step, 128), step)
        g = (dot(gouter_ref[...], outer_rows(c), NT) * slope_ref[:, at]).astype(bf16)
        ginner_ref[:, at] = g
        bsum_ref[0:1, at] += total(g.astype(f32))
        acc_ref[...] += dot(g, wide_ref[:, w_at], NT)
        return carry

    lax.fori_loop(0, inner // step, down, 0)
    grad_first = acc_ref[...]
    normed = n1_ref[...]
    vsum_ref[1:2, :] += total(grad_first * normed)
    vsum_ref[2:3, :] += total(grad_first)
    grad_summed = row_back(grad_first, normed, rstdev1, vec(1))
    gsum_ref[...] = grad_summed
    grad_low = grad_summed.astype(bf16)
    gproj_ref[...] = grad_low
    vsum_ref[0:1, :] += total(grad_low.astype(f32))
    gatt_ref[...] = dot(grad_low, wide_ref[:, :width], NT).astype(bf16)


def layer(seq_index, own, their, x, upstream, wide, vectors, bias):
    rows, width = x.shape
    inner = bias.shape[1]
    block = 256
    by_rows = lambda size: pl.BlockSpec((block, size), lambda i, *_: (i, 0))
    whole = lambda shape: pl.BlockSpec(shape, lambda i, *_: (0,) * len(shape), pipeline_mode=pl.Buffered(1))
    once = lambda shape: pl.BlockSpec(shape, lambda i, *_: (0, 0))
    spec = pltpu.PrefetchScalarGridSpec(
        num_scalar_prefetch=1,
        grid=(rows // block,),
        in_specs=[by_rows(width // 2)] * 2
        + [by_rows(width), by_rows(width), whole(wide.shape), whole(vectors.shape), whole(bias.shape)],
        out_specs=[by_rows(width)] * 5
        + [by_rows(inner)] * 2
        + [by_rows(width)] * 2
        + [once((8, width)), once((8, inner))],
        scratch_shapes=[pltpu.VMEM((block, inner), jnp.float32)] + [pltpu.VMEM((block, width), jnp.float32)] * 3,
    )
    shape = lambda size, dtype: jax.ShapeDtypeStruct((rows, size), dtype)
    low = jnp.bfloat16
    return pl.pallas_call(
        layer_kernel,
        grid_spec=spec,
        out_shape=[shape(width, low), shape(width, jnp.float32), shape(width, low), shape(width, low), shape(width, low)]
        + [shape(inner, low)] * 2
        + [shape(width, low)] * 2
        + [jax.ShapeDtypeStruct((8, width), jnp.float32), jax.ShapeDtypeStruct((8, inner), jnp.float32)],
        compiler_params=pltpu.CompilerParams(dimension_semantics=("arbitrary",), vmem_limit_bytes=56 << 20),
        cost_estimate=pl.CostEstimate(
            flops=8 * rows * width * (width // 2 + inner), transcendentals=rows * inner, bytes_accessed=36 << 20
        ),
        name="layer",
    )(seq_index, own, their, x, upstream, wide, vectors, bias)


def weights_kernel(att_ref, first_ref, active_ref, gproj_ref, gouter_ref, ginner_ref, wide_ref):
    bf16 = jnp.bfloat16
    c = pl.program_id(1)
    width = gproj_ref.shape[1]
    inner = width * pl.num_programs(1)

    @pl.when(c == 0)
    def _():
        wide_ref[:, :width] = dot(att_ref[...], gproj_ref[...], TN).astype(bf16)

    at = pl.ds(pl.multiple_of(width * (c + 1), 128), width)
    wide_ref[:, at] = dot(first_ref[...], ginner_ref[...], TN).astype(bf16)
    at = pl.ds(pl.multiple_of(inner + width * (c + 1), 128), width)
    wide_ref[:, at] = dot(active_ref[...], gouter_ref[...], TN).astype(bf16)


def layer_weights(attended, first, active, gproj, gouter, ginner):
    rows, width = gproj.shape
    inner = ginner.shape[1]
    half = width // 2
    steps = inner // width
    spec = pltpu.PrefetchScalarGridSpec(
        num_scalar_prefetch=0,
        grid=(2, steps),
        in_specs=[
            pl.BlockSpec((rows, half), lambda i, c: (0, i)),
            pl.BlockSpec((rows, half), lambda i, c: (0, i)),
            pl.BlockSpec((rows, half), lambda i, c: (0, 2 * c + i)),
            pl.BlockSpec((rows, width), lambda i, c: (0, 0)),
            pl.BlockSpec((rows, width), lambda i, c: (0, 0)),
            pl.BlockSpec((rows, width), lambda i, c: (0, c)),
        ],
        out_specs=pl.BlockSpec((half, width + 2 * inner), lambda i, c: (i, 0)),
    )
    return pl.pallas_call(
        weights_kernel,
        grid_spec=spec,
        out_shape=jax.ShapeDtypeStruct((width, width + 2 * inner), jnp.bfloat16),
        compiler_params=pltpu.CompilerParams(dimension_semantics=("arbitrary", "arbitrary"), vmem_limit_bytes=56 << 20),
        cost_estimate=pl.CostEstimate(
            flops=4 * rows * width * (width // 2 + inner), transcendentals=0, bytes_accessed=32 << 20
        ),
        name="layer_weights",
    )(attended, first, active, gproj, gouter, ginner)


def matmul(left_side, right_side):
    return jnp.dot(left_side, right_side, preferred_element_type=jnp.float32)


def contract_rows(left_side, right_side):
    return jnp.einsum("rd,re->de", left_side, right_side, preferred_element_type=jnp.float32)


def times_transpose(left_side, right_side):
    return jnp.einsum("re,de->rd", left_side, right_side, preferred_element_type=jnp.float32)


def norm_forward(values, norm_gain, norm_shift):
    center = values - jnp.mean(values, axis=-1, keepdims=True)
    rstdev = lax.rsqrt(jnp.mean(center * center, axis=-1, keepdims=True) + EPSILON)
    normed = center * rstdev
    return (normed * norm_gain + norm_shift, normed, rstdev)


def norm_backward(gradient, normed, rstdev, norm_gain):
    scaled = gradient * norm_gain
    back = rstdev * (
        scaled
        - jnp.mean(scaled, axis=-1, keepdims=True)
        - normed * jnp.mean(scaled * normed, axis=-1, keepdims=True)
    )
    return (back, jnp.sum(gradient * normed, axis=0), jnp.sum(gradient, axis=0))


def swap_seq(value):
    return lax.ppermute(value, "seq", [(0, 1), (1, 0)])


def flip(value, axis, bit):
    return lax.ppermute(value, axis, [(i, i ^ bit) for i in range(lax.axis_size(axis))])


def row_steps():
    bits = [1 << i for i in range(1, lax.axis_size("row").bit_length() - 1)]
    return [("row", bit) for bit in bits], [("row", 1)]


def scatter_order():
    far, near = row_steps()
    return [("core", 1)] + near + far


def coordinates(owner):
    row_size = lax.axis_size("row")
    return {"seq": owner // (2 * row_size), "row": (owner // 2) % row_size, "core": owner % 2}


def places_of(order, count):
    owner = coordinates(jnp.arange(count, dtype=jnp.int32))
    place = jnp.zeros((count,), jnp.int32)
    for step, (axis, bit) in enumerate(order):
        place = place + ((((owner[axis] ^ lax.axis_index(axis)) // bit) & 1) << step)
    return place


def scatter_step(parts, axis, bit):
    half = parts.shape[0] // 2
    arrived = flip(parts[half:], axis, bit)
    return (parts[:half].astype(jnp.float32) + arrived.astype(jnp.float32)).astype(jnp.bfloat16)


def sum_small(value, axes):
    for axis in axes:
        bit = 1
        while bit < lax.axis_size(axis):
            value = value + flip(value, axis, bit)
            bit *= 2
    return value


def body(
    incoming_activations,
    upstream_derivative,
    grid_coordinates,
    word_segment_ids,
    asking_matrix,
    asking_shift,
    lookup_matrix,
    content_matrix,
    content_shift,
    mixing_result_matrix,
    mixing_result_shift,
    post_mixing_scaling,
    post_mixing_offset,
    expand_matrix,
    expand_shift,
    contract_matrix,
    contract_shift,
    post_perceptron_scaling,
    post_perceptron_offset,
    pair_gate_scores,
    gate_random_jitter,
    softening_scale,
):
    f32, bf16 = jnp.float32, jnp.bfloat16
    heads = softening_scale.shape[0]
    width = incoming_activations.shape[2]
    rows = incoming_activations.shape[1]
    inner = expand_matrix.shape[1]
    tsize = pair_gate_scores.shape[2]
    score_scale = 1.0 / math.sqrt(width // heads)
    half_width, half_heads = width // 2, heads // 2
    pairs = half_heads // 2
    seq_index = lax.axis_index("seq")
    dp_size = 2 * lax.axis_size("row")
    dp_index = 2 * lax.axis_index("row") + lax.axis_index("core")
    owner = seq_index * dp_size + dp_index
    first_seq = seq_index == 0
    inputs = incoming_activations[0]
    share = asking_matrix.shape[0]
    inner_share = expand_shift.shape[0]
    mask_rows = tsize // (2 * dp_size)
    lanes = tsize // 128
    everyone = ("seq", "row", "core")

    packed = jnp.stack(
        [part.reshape(share, 2, pairs, 128) for part in (asking_matrix, lookup_matrix, content_matrix)], axis=3
    )
    packed = packed.transpose(1, 2, 3, 0, 4).reshape(2, 3 * pairs * share, 128)
    small = jnp.concatenate(
        [
            asking_shift,
            content_shift,
            mixing_result_shift,
            post_mixing_scaling,
            post_mixing_offset,
            contract_shift,
            post_perceptron_scaling,
            post_perceptron_offset,
            expand_shift,
        ]
    )
    lines = jnp.pad(small, (0, 1024 - small.shape[0])).reshape(1, 8, 128)
    smoothed_gate = jax.nn.sigmoid(
        (pair_gate_scores + gate_random_jitter) / softening_scale[:, None, None]
    )
    mask_low = smoothed_gate.astype(bf16).reshape(2, half_heads, mask_rows, lanes, 128)
    mask_low = mask_low.transpose(0, 1, 3, 2, 4).reshape(2, -1, 128)
    packed = jnp.concatenate([packed, jnp.concatenate([lines, lines], axis=0), mask_low], axis=1)
    kept = lax.dynamic_index_in_dim(packed, seq_index, 0, keepdims=False)
    sent = lax.dynamic_index_in_dim(packed, 1 - seq_index, 0, keepdims=False)
    packed = jnp.concatenate([kept, swap_seq(sent)], axis=0)
    other_inputs = swap_seq(inputs)
    hidden_blocks = inner_share // share
    hidden = expand_matrix.reshape(share, 2 * dp_size, hidden_blocks, share)
    contract_blocks = contract_matrix.reshape(hidden_blocks, share, width)
    wide_share = jnp.concatenate(
        [mixing_result_matrix, hidden.transpose(0, 2, 1, 3).reshape(share, inner)]
        + [contract_blocks[k] for k in range(hidden_blocks)],
        axis=1,
    )
    packed, wide_share = lax.optimization_barrier((packed, wide_share))
    gathered = lax.all_gather(packed, ("row", "core"), axis=0, tiled=True)
    wide_matrix = lax.all_gather(wide_share, everyone, axis=0, tiled=True)
    both_inputs = jnp.concatenate([inputs, other_inputs], axis=0)
    start = grid_coordinates[0, 0]
    turned = (jnp.arange(tsize, dtype=jnp.int32) + start) % tsize
    turn = (turned[:, None] == jnp.arange(tsize, dtype=jnp.int32)[None, :]).astype(bf16)
    row = jnp.arange(mask_rows, dtype=jnp.int32)
    table_order = scatter_order()
    table_places = places_of(table_order[::-1], dp_size)
    own_seq = (jnp.arange(2, dtype=jnp.int32) ^ seq_index)[:, None, None]
    input_spots = ((table_places[None, :] * 2 + own_seq[:, :, 0]) * share)[:, :, None] + jnp.arange(share)
    turned_inputs = matmul(
        both_inputs,
        (input_spots.reshape(-1)[:, None] == jnp.arange(width, dtype=jnp.int32)[None, :]).astype(bf16),
    ).astype(bf16)
    table_spots = ((table_places[None, :] * 2 + own_seq[:, :, 0]) * mask_rows)[:, :, None] + row
    table_spots = table_spots.reshape(-1)
    spot_turn = jnp.sum(jnp.where(turn > 0, table_spots[None, :], 0), axis=1)
    turn_back = (jnp.arange(tsize, dtype=jnp.int32)[:, None] == spot_turn[None, :]).astype(bf16)

    gathered, turned_inputs = lax.optimization_barrier((gathered, turned_inputs))
    gathered = gathered.reshape(dp_size, 2, -1, 128)
    weight_lines = 3 * pairs * share

    def seq_ordered(value):
        mine, others = value[:, 0], value[:, 1]
        return jnp.stack([jnp.where(first_seq, mine, others), jnp.where(first_seq, others, mine)])

    heads_matrix = seq_ordered(gathered[:, :, :weight_lines]).reshape(2, dp_size, 3 * pairs, share, 128)
    heads_matrix = heads_matrix.transpose(0, 1, 3, 2, 4).reshape(width, 3 * half_width)
    vectors = seq_ordered(gathered[:, :, weight_lines : weight_lines + 8]).reshape(2 * dp_size, 1024)
    own_mask = gathered[:, :, weight_lines + 8 :].reshape(dp_size, 2, half_heads, lanes, mask_rows, 128)
    own_mask = own_mask.transpose(2, 0, 1, 4, 3, 5).reshape(half_heads, tsize, tsize)

    def vector(index, size=share):
        return vectors[:, index * share : index * share + size].reshape(-1).astype(f32)

    segments = word_segment_ids[0]
    values_range = jnp.arange(8, dtype=jnp.int32)[:, None]
    segment_ends = jnp.sum((segments[None, :] <= values_range).astype(jnp.int32), axis=1)
    row_end = jnp.sum(jnp.where(segments[None, :] == values_range, segment_ends[:, None], 0), axis=0)
    counts = (row_end.reshape(-1, TILE)[:, -1] + (TILE - 1)) // TILE
    full = row_end.reshape(-1, TILE)[:, 0]
    mask_places = (
        (jnp.arange(2, dtype=jnp.int32) ^ seq_index)[None, :, None] * (tsize // 2)
        + jnp.arange(dp_size, dtype=jnp.int32)[:, None, None] * mask_rows
        + row
    ).reshape(-1)
    turn_rows = (turned[:, None] == mask_places[None, :]).astype(bf16)
    tables = jnp.einsum("hab,cb->hca", own_mask, turn, preferred_element_type=f32).astype(bf16)
    tables = jnp.einsum("hca,da->hcd", tables, turn_rows, preferred_element_type=f32) * (4.0 * LOG2E)

    own_columns = lambda index: lax.dynamic_slice_in_dim(
        vector(index), seq_index * half_width, half_width
    ).reshape(pairs, 128)
    query_shift, value_shift = own_columns(0), own_columns(1)
    heads_shift = jnp.stack([query_shift, jnp.zeros_like(query_shift), value_shift], axis=1)
    heads_rows = (matmul(both_inputs, heads_matrix) + heads_shift.reshape(-1)).astype(bf16)
    seq_scalar = seq_index[None].astype(jnp.int32)
    scalars = (seq_scalar, counts, full)
    row_end = row_end[None]
    own_attended, wide_attended, logsum = attend(heads_rows, tables, row_end, scalars, score_scale)
    their_attended = swap_seq(own_attended[rows:])

    inner_shift = vector(8, inner_share).reshape(2 * dp_size, hidden_blocks, share).transpose(1, 0, 2)
    layer_vectors = jnp.stack([vector(i) for i in (2, 3, 4, 5, 6, 7)] + [jnp.zeros((width,), f32)] * 2)
    (layer_out, grad_summed, grad_attended, attended, first_low, active_low, grad_inner_low, grad_outer_low,
     grad_proj_low, vector_sums, inner_sums) = layer(
        seq_scalar,
        own_attended,
        their_attended,
        inputs,
        upstream_derivative[0],
        wide_matrix,
        layer_vectors,
        inner_shift.reshape(1, inner),
    )
    grads_all = []
    for p in range(pairs):
        low, high = grad_attended[:, p * 128 : (p + 1) * 128], grad_attended[:, (pairs + p) * 128 : (pairs + p + 1) * 128]
        arrived = swap_seq(jnp.where(first_seq, high, low))
        grads_all.append(jnp.concatenate([jnp.where(first_seq, low, high), arrived], axis=0))
    wide_grad = layer_weights(
        attended, first_low, active_low, grad_proj_low, grad_outer_low, grad_inner_low
    )
    wide_grad, grads_all = lax.optimization_barrier((wide_grad, grads_all))
    wide_sum = lax.psum_scatter(wide_grad, everyone, scatter_dimension=0, tiled=True).astype(f32)

    grad_heads, head_bias, chains = [], [], []
    for p in range(pairs):
        grad_pair, table_part, weight_part, bias_part = attend_back(
            p, heads_rows, grads_all[p], wide_attended, tables, row_end, logsum,
            turned_inputs, turn_back, turn, scalars, score_scale,
        )
        grad_heads.append(grad_pair)
        head_bias.append(bias_part[0])
        table_part = table_part.reshape(2, 2 * dp_size, mask_rows, lanes, 128)
        table_part = table_part.transpose(1, 0, 3, 2, 4).reshape(dp_size, 2, -1, 128)
        weight_part = weight_part.reshape(2 * dp_size, share, 3, 128).transpose(0, 2, 1, 3)
        weight_part = weight_part.reshape(dp_size, 2, -1, 128)
        chains.append((jnp.concatenate([table_part, weight_part], axis=2), list(table_order)))
        if p + 1 < pairs:
            moved = []
            for parts, steps in chains:
                if steps:
                    parts = scatter_step(parts, *steps[0])
                moved.append((parts, steps[1:]))
            chains = moved
            held = lax.optimization_barrier((grads_all[p + 1], [c[0] for c in chains]))
            grads_all[p + 1] = held[0]
            chains = [(parts, steps) for parts, (unused, steps) in zip(held[1], chains)]

    grad_heads = jnp.concatenate(grad_heads, axis=1)
    their_part = swap_seq(times_transpose(grad_heads[rows:], heads_matrix).astype(bf16))
    input_grad = grad_summed + times_transpose(grad_heads[:rows], heads_matrix) + their_part.astype(f32)
    own_sums, their_sums = [], []
    for parts, steps in chains:
        for step in steps:
            parts = scatter_step(parts, *step)
        own_sums.append(parts[0, 0])
        their_sums.append(swap_seq(parts[0, 1]))

    own_sums, their_sums = jnp.stack(own_sums), jnp.stack(their_sums)
    both_sums = jnp.stack(
        [jnp.where(first_seq, own_sums, their_sums), jnp.where(first_seq, their_sums, own_sums)]
    ).astype(f32)
    table_lines = 2 * mask_rows * lanes
    table_grad = both_sums[:, :, :table_lines].reshape(2, pairs, 2, lanes, mask_rows, 128)
    table_grad = table_grad.transpose(0, 1, 2, 4, 3, 5).reshape(heads, mask_rows, tsize)
    mask_logits_gradient = (
        4.0 * table_grad * smoothed_gate * (1.0 - smoothed_gate) / softening_scale[:, None, None]
    )
    heads_grad = both_sums[:, :, table_lines:].reshape(2, pairs, 3, share, 128)
    heads_grad = heads_grad.transpose(2, 3, 0, 1, 4).reshape(3, share, width)

    layer_sums = sum_small(
        jnp.concatenate([vector_sums[:6].reshape(-1), inner_sums[0]]), ("core", "row", "seq")
    )
    head_bias = sum_small(
        jnp.stack(head_bias).reshape(pairs, 3, 128)[:, ::2].transpose(1, 0, 2).reshape(-1), ("core", "row")
    )

    def piece(index, size=share):
        return lax.dynamic_slice_in_dim(layer_sums, index * width + owner * size, size)

    def bias_piece(index):
        return lax.dynamic_slice_in_dim(head_bias, index * half_width + dp_index * share, share)

    inner_sum = wide_sum[:, width : width + inner].reshape(share, hidden_blocks, 2 * dp_size, share)
    inner_sum = inner_sum.transpose(0, 2, 1, 3).reshape(share, inner)
    outer_sum = jnp.concatenate(
        [wide_sum[:, width + inner + k * width : width + inner + (k + 1) * width] for k in range(hidden_blocks)], axis=0
    )
    inner_piece = lax.dynamic_slice_in_dim(
        layer_sums[6 * width :].reshape(hidden_blocks, 2 * dp_size, share), owner, 1, 1
    ).reshape(inner_share)
    return (
        layer_out[None],
        input_grad[None],
        heads_grad[0],
        bias_piece(0),
        heads_grad[1],
        heads_grad[2],
        bias_piece(1),
        wide_sum[:, :width],
        piece(0),
        piece(1),
        piece(2),
        inner_sum,
        inner_piece,
        outer_sum,
        piece(3),
        piece(4),
        piece(5),
        mask_logits_gradient,
    )


def solution(mesh):
    split = jax.sharding.Mesh(
        mesh.devices.reshape(2, -1, 2), ("seq", "row", "core")
    )
    return jax.shard_map(
        body,
        mesh=split,
        in_specs=(
            P(("row", "core"), "seq", None),
            P(("row", "core"), "seq", None),
            P(("row", "core"), None),
            P(("row", "core"), None),
            P(("seq", "row", "core"), None),
            P(("seq", "row", "core")),
            P(("seq", "row", "core"), None),
            P(("seq", "row", "core"), None),
            P(("seq", "row", "core")),
            P(("seq", "row", "core"), None),
            P(("seq", "row", "core")),
            P(("seq", "row", "core")),
            P(("seq", "row", "core")),
            P(("seq", "row", "core"), None),
            P(("seq", "row", "core")),
            P(("seq", "row", "core"), None),
            P(("seq", "row", "core")),
            P(("seq", "row", "core")),
            P(("seq", "row", "core")),
            P(None, ("seq", "row", "core"), None),
            P(None, ("seq", "row", "core"), None),
            P(),
        ),
        out_specs=(
            P(("row", "core"), "seq", None),
            P(("row", "core"), "seq", None),
            P(("seq", "row", "core"), None),
            P(("seq", "row", "core")),
            P(("seq", "row", "core"), None),
            P(("seq", "row", "core"), None),
            P(("seq", "row", "core")),
            P(("seq", "row", "core"), None),
            P(("seq", "row", "core")),
            P(("seq", "row", "core")),
            P(("seq", "row", "core")),
            P(("seq", "row", "core"), None),
            P(("seq", "row", "core")),
            P(("seq", "row", "core"), None),
            P(("seq", "row", "core")),
            P(("seq", "row", "core")),
            P(("seq", "row", "core")),
            P(None, ("seq", "row", "core"), None),
        ),
        check_vma=False,
    )
```

time: 712 us -> 505 us (0.71)
  waiting for transfers between devices: 282 us -> 117 us
  matrix products: 120 us -> 31.2 us
  Pallas kernels: 160 us -> 230 us
  local copies, waits for them, and re-layouts: 72.2 us -> 52.6 us
    reduce_scatter x2 -> x1, waiting for transfers between devices: 152 us -> 0.01 us  [body(): lax.psum_scatter(wide_grad, everyone, scatter_dimension=0, tiled=True)]
    pallas_call x2 -> x6, Pallas kernels: 160 us -> 230 us  [the longest x3 100 us: attend_back(): pl.pallas_call(functools.partial(attend_back_kernel, rows // TILE // 2, s...]
    dot_general x6 -> x1, matrix products: 48.6 us -> 9.2 us  [body(): jnp.einsum('hca,da->hcd', tables, turn_rows, preferred_element_type=f32)]
    dot_general x4 -> x2, matrix products: 37.3 us -> 9.17 us  [times_transpose(): jnp.einsum('re,de->rd', left_side, right_side, preferred_element_type=jnp...]
    unnamed x91 -> x88, local copies, waits for them, and re-layouts: 31.8 us -> 4.51 us
    dot_general x4 -> x2, matrix products: 33.7 us -> 12.9 us  [matmul(): return jnp.dot(left_side, right_side, preferred_element_type=jnp.float32)]
    all_gather x3 -> x2, waiting for transfers between devices: 33.3 us -> 13.3 us  [the longest x1 13.3 us: body(): gathered = lax.all_gather(packed, ('row', 'core'), axis=0, tiled=True)]
    ppermute x8 -> x10, waiting for transfers between devices: 38.2 us -> 49.2 us  [swap_seq(): return lax.ppermute(value, 'seq', [(0, 1), (1, 0)])]
  transfers between devices with their start and end apart: 24 -> 34, of which waited for: 17 -> 19; matrix products, arithmetic and copies ran while one was open for 15% -> 19% of each run, Pallas kernels for 10% -> 36%
where the time goes in v2:
time: 505 us; the launch traced here: 499 us
  Pallas kernels  230 us (46%)
  waiting for transfers between devices  117 us (23%)
  local copies, waits for them, and re-layouts  52.6 us (10%)
  matrix products  31.2 us (6%)
  starting transfers between devices  26.5 us (5%)
  other arithmetic  26.2 us (5%)
  between operations  15.4 us (3%)
    pallas_call x3, Pallas kernels, attend_back(): pl.pallas_call(functools.partial(attend_back_kernel, rows // TILE // 2, s...  100 us
    pallas_call x1, Pallas kernels, attend(): pl.pallas_call(functools.partial(attend_kernel, rows // TILE // 2, score_...  58.1 us
    ppermute x21, waiting for transfers between devices, flip(): lax.ppermute(value, axis, [(i, i ^ bit) for i in range(lax.axis_size(axis...  54.1 us
    pallas_call x1, Pallas kernels, layer(): pl.pallas_call(layer_kernel, grid_spec=spec, out_shape=[shape(width, low)...  50.8 us
    ppermute x10, waiting for transfers between devices, swap_seq(): return lax.ppermute(value, 'seq', [(0, 1), (1, 0)])  49.2 us
    pallas_call x1, Pallas kernels, layer_weights(): pl.pallas_call(weights_kernel, grid_spec=spec, out_shape=jax.ShapeDtypeSt...  20.6 us
    ppermute x21, starting transfers between devices, flip(): lax.ppermute(value, axis, [(i, i ^ bit) for i in range(lax.axis_size(axis...  13.4 us
    all_gather x1, waiting for transfers between devices, body(): gathered = lax.all_gather(packed, ('row', 'core'), axis=0, tiled=True)  13.3 us
  transfers between devices with their start and end apart: 34, of which 19 were waited for; matrix products, arithmetic and copies ran while one was open for 19% of the time, Pallas kernels for 36%

profile of v2, /device:TPU:0, one launch (start us, length us, event | category | flops | bytes accessed | tf_op | source)
XLA Modules:
  0.0 499.1 jit_solution(9422280753940163891)
XLA Ops:
  7.4 2.1 fusion.50
  11.7 3.0 collective-permute-start.1
  20.3 1.8 collective-permute-start
  25.0 31.1 %collective-permute-done = bf16[1024,768]{1,0:T(8,128)(2,1)S(1)} collective-permute-done((bf16[1024,768]{1,0:T(8,128)(2,1)}, bf16[1024,768]{1,0:T(8,128)(2,1)S(1)}, u32[]{:S(2)}, u32[]{:S(2)}) %collective-permute-start) | collective-permute-done | bytes 1572896 | tf_op jit(solution)/shard_map/ppermute | solution.py:512
  56.1 6.5 %convolution_convert_fusion.turned_ref = bf16[2048,768]{1,0:T(8,128)(2,1)} fusion(bf16[1024,768]{1,0:T(8,128)(2,1)S(1)} %collective-permute-done, bf16[1024,768]{1,0:T(8,128)(2,1)} %bitcast.169, s32[768]{0:T(1024)S(1)} %add.359), kind=kOutput, calls=%fused_computation.1 | convolution fusion | flops 2424373248 | bytes 6294528 | tf_op jit(solution)/shard_map/dot_general | solution.py:483
  62.6 13.3 %all-gather.3.cloned.1.call-done = bf16[19456,128]{1,0:T(8,128)(2,1)} async-done(((bf16[1216,128]{1,0:T(8,128)(2,1)}), bf16[19456,128]{1,0:T(8,128)(2,1)}) %all-gather.3.cloned.1.call-update) | async-done | bytes 4980752 | tf_op jit(solution)/shard_map/all_gather | solution.py:639
  75.9 3.9 slice.344
  81.9 1.6 broadcast_select_fusion.1
  83.5 1.5 copy.88
  84.9 1.6 copy.89
  86.5 1.8 copy.124
  88.3 3.7 reshape.741
  92.0 2.5 pad_maximum_fusion.1
  94.5 9.2 %broadcast_multiply_fusion.tab_ref = f32[6,512,512]{2,1,0:T(8,128)} fusion(bf16[6,512,512]{2,1,0:T(8,128)(2,1)} %reshape.741, s32[512]{0:T(512)S(1)} %add.373, s32[512]{0:T(512)S(1)} %add_select_fusion), kind=kOutput, calls=%fused_computation.8 | convolution fusion | flops 3224895488 | bytes 9441280 | tf_op jit(solution)/shard_map/hca,da->hcd/dot_general | solution.py:689
  103.7 6.4 %add_convert_fusion.qkv_ref = bf16[2048,1152]{1,0:T(8,128)(2,1)S(1)} fusion(f32[1152]{0:T(1024)S(1)} %add.361, bf16[1024,768]{1,0:T(8,128)(2,1)} %copy-done.37, bf16[1024,768]{1,0:T(8,128)(2,1)} %bitcast.170, bf16[96,8,9,128]{3,2,1,0:T(8,128)(2,1)S(1)} %bitcast.141), kind=kOutput, calls=%fused_computation | convolution fusion | flops 3634888704 | bytes 9638400 | tf_op jit(solution)/shard_map/dot_general | solution.py:483
  110.1 58.1 %attend.1 = (bf16[2048,384]{1,0:T(8,128)(2,1)S(1)}, f32[2048,384]{1,0:T(8,128)S(1)}, f32[3,8,2048]{2,1,0:T(8,128)S(1)}) custom-call(s32[1]{0:T(128)} %bitcast.s_ref, s32[8]{0:T(128)S(1)} %and_select_fusion.5.nk_ref, s32[8]{0:T(128)S(1)} %get-tuple-element.96.full_ref, bf16[2048,1152]{1,0:T(8,128)(2,1)S(1)} %add_convert_fusion.qkv_ref, ...), custom_call_target="tpu_custom_call" | custom-call | flops 4294967296 | bytes 8388608 | tf_op jit(solution)/shard_map/attend/pallas_call | solution.py:160
  168.2 1.7 copy-done.5
  170.7 1.6 collective-permute-start.2
  174.4 14.2 %collective-permute-done.2.refs_1_ = bf16[1024,384]{1,0:T(8,128)(2,1)} collective-permute-done((bf16[1024,384]{1,0:T(8,128)(2,1)S(1)}, bf16[1024,384]{1,0:T(8,128)(2,1)}, u32[]{:S(2)}, u32[]{:S(2)}) %collective-permute-start.2) | collective-permute-done | bytes 786464 | tf_op jit(solution)/shard_map/ppermute | solution.py:512
  188.6 50.8 %layer.1 = (bf16[1024,768]{1,0:T(8,128)(2,1)}, f32[1024,768]{1,0:T(8,128)}, bf16[1024,768]{1,0:T(8,128)(2,1)}, bf16[1024,768]{1,0:T(8,128)(2,1)}, bf16[1024,768]...) custom-call(s32[1]{0:T(128)} %bitcast.s_ref, ...), custom_call_target="tpu_custom_call" | custom-call | flops 21743271936 | bytes 37748736 | tf_op jit(solution)/shard_map/layer/pallas_call | solution.py:421
  239.4 1.5 broadcast_select_fusion.3
  240.9 1.6 collective-permute-start.5
  243.0 1.5 collective-permute-start.3
  244.5 20.6 %layer_weights.1 = bf16[768,6912]{1,0:T(8,128)(2,1)} custom-call(bf16[1024,768]{1,0:T(8,128)(2,1)} %get-tuple-element.63.att_ref, bf16[1024,768]{1,0:T(8,128)(2,1)} %get-tuple-element.64.first_ref, bf16[1024,3072]{1,0:T(8,128)(2,1)} %get-tuple-element.65.active_ref, bf16[1024,768]{1,0:T(8,128)(2,1)} %get-tuple-element.66.gproj_ref, ...), custom_call_target="tpu_custom_call" | custom-call | flops 10871635968 | bytes 33554432 | tf_op jit(solution)/shard_map/layer_weights/pallas_call | solution.py:470
  270.1 33.7 %attend_back.3 = (bf16[2048,384]{1,0:T(8,128)(2,1)}, bf16[2,512,512]{2,1,0:T(8,128)(2,1)}, bf16[768,384]{1,0:T(8,128)(2,1)}, f32[8,384]{1,0:T(8,128)}) custom-call(s32[1]{0:T(128)} %bitcast.s_ref, s32[8]{0:T(128)} %copy-done.3, s32[8]{0:T(128)} %copy-done.2, bf16[2048,1152]{1,0:T(8,128)(2,1)} %copy-done.4, bf16[2048,128]{1,0:T(8,128)(2,1)} %pad_maximum_fusion.7.grad_ref, ...), custom_call_target="tpu_custom_call" | custom-call | flops 10737418240 | bytes 12582912 | tf_op jit(solution)/shard_map/attend_back/pallas_call | solution.py:281
  308.8 3.9 collective-permute-done.27
  312.7 3.9 collective-permute-done.28
  316.7 5.5 %collective-permute-done.29 = f32[7680]{0:T(1024)S(1)} collective-permute-done((f32[7680]{0:T(1024)S(1)}, f32[7680]{0:T(1024)S(1)}, u32[]{:S(2)}, u32[]{:S(2)}) %collective-permute-start.29) | collective-permute-done | bytes 30752 | tf_op jit(solution)/shard_map/ppermute | solution.py:516
  322.3 4.5 collective-permute-done.30
  328.2 33.3 %attend_back.4 = (bf16[2048,384]{1,0:T(8,128)(2,1)}, bf16[2,512,512]{2,1,0:T(8,128)(2,1)}, bf16[768,384]{1,0:T(8,128)(2,1)}, f32[8,384]{1,0:T(8,128)}) custom-call(s32[1]{0:T(128)} %bitcast.s_ref, s32[8]{0:T(128)} %copy-done.3, s32[8]{0:T(128)} %copy-done.2, bf16[2048,1152]{1,0:T(8,128)(2,1)} %copy-done.4, bf16[2048,128]{1,0:T(8,128)(2,1)} %pad_maximum_fusion.8.grad_ref, ...), custom_call_target="tpu_custom_call" | custom-call | flops 10737418240 | bytes 12582912 | tf_op jit(solution)/shard_map/attend_back/pallas_call | solution.py:281
  368.8 1.6 constant_dynamic-update-slice_fusion.4
  371.4 11.2 %collective-permute-done.7 = bf16[4,2,200,128]{3,2,1,0:T(8,128)(2,1)S(1)} collective-permute-done((bf16[4,2,200,128]{3,2,1,0:T(8,128)(2,1)S(1)}, bf16[4,2,200,128]{3,2,1,0:T(8,128)(2,1)S(1)}, u32[]{:S(2)}, u32[]{:S(2)}) %collective-permute-start.7) | collective-permute-done | bytes 409632 | tf_op jit(solution)/shard_map/ppermute | solution.py:516
  386.1 33.4 %attend_back.5 = (bf16[2048,384]{1,0:T(8,128)(2,1)}, bf16[2,512,512]{2,1,0:T(8,128)(2,1)}, bf16[768,384]{1,0:T(8,128)(2,1)}, f32[8,384]{1,0:T(8,128)}) custom-call(s32[1]{0:T(128)} %bitcast.s_ref, s32[8]{0:T(128)} %copy-done.3, s32[8]{0:T(128)} %copy-done.2, bf16[2048,1152]{1,0:T(8,128)(2,1)} %copy-done.4, bf16[2048,128]{1,0:T(8,128)(2,1)} %pad_maximum_fusion.9.grad_ref, ...), custom_call_target="tpu_custom_call" | custom-call | flops 10737418240 | bytes 12582912 | tf_op jit(solution)/shard_map/attend_back/pallas_call | solution.py:281
  420.3 2.9 constant_dynamic-update-slice_fusion.2
  424.5 5.7 %fusion.7 = f32[1024,768]{1,0:T(8,128)} fusion(bf16[2048,1152]{1,0:T(8,128)(2,1)} %constant_dynamic-update-slice_fusion.2, bf16[96,8,9,128]{3,2,1,0:T(8,128)(2,1)S(1)} %bitcast.142), kind=kOutput, calls=%fused_computation.12 | convolution fusion | flops 1811939328 | bytes 7274496 | tf_op jit(solution)/shard_map/re,de->rd/dot_general | solution.py:491
  430.4 3.4 fusion.14
  436.3 2.0 reshape.754
  438.4 2.7 collective-permute-start.25
  443.1 2.7 collective-permute-start.11
  446.4 4.4 collective-permute-done.11
  454.0 4.6 collective-permute-done.13
  458.8 4.6 collective-permute-done.16
  463.5 1.8 collective-permute-start.17
  465.5 4.2 collective-permute-done.17
  470.6 5.8 %collective-permute-done.18 = bf16[1,2,200,128]{3,2,1,0:T(8,128)(2,1)S(1)} collective-permute-done((bf16[1,2,200,128]{3,2,1,0:T(8,128)(2,1)S(1)}, bf16[1,2,200,128]{3,2,1,0:T(8,128)(2,1)S(1)}, u32[]{:S(2)}, u32[]{:S(2)}) %collective-permute-start.18) | collective-permute-done | bytes 102432 | tf_op jit(solution)/shard_map/ppermute | solution.py:516
  476.6 2.0 collective-permute-done.9
  478.6 2.2 add_bitcast_fusion
  488.2 2.6 reshape.761
  (280 shorter events, 59.9 us)
Async XLA Ops:
  7.3 7.4 %copy-start.20 = (bf16[24,3072]{1,0:T(8,128)(2,1)S(1)}, bf16[24,3072]{1,0:T(8,128)(2,1)}, u32[]{:S(2)}) copy-start(bf16[24,3072]{1,0:T(8,128)(2,1)} %param.35) | copy-start | bytes 442372
  7.3 68.5 %all-gather.3.cloned.1.call-start = ((), (), s32[]{:S(2)}) async-start(), calls=%async_computation.1 | async-start | bytes 5292032 | tf_op jit(solution)/shard_map/all_gather | solution.py:639
  11.7 7.1 %collective-permute-start.1 = (bf16[608,128]{1,0:T(8,128)(2,1)S(1)}, bf16[608,128]{1,0:T(8,128)(2,1)S(1)}, u32[]{:S(2)}, u32[]{:S(2)}) collective-permute-start(bf16[608,128]{1,0:T(8,128)(2,1)S(1)} %get-tuple-element.114), channel_id=1, source_target_pairs={{0,16},{16,0},{1,17},{17,1},{2,18},{18,2},{3,19},{19,3},{4,20},{20... | collective-permute-start | bytes 466952 | tf_op jit(solution)/shard_map/ppermute | solution.py:512
  15.9 7.9 %copy-start.24 = (s32[1,2048]{1,0:T(1,128)S(1)}, s32[1,2048]{1,0:T(1,128)}, u32[]{:S(2)}) copy-start(s32[1,2048]{1,0:T(1,128)} %param.25) | copy-start | bytes 24580
  19.5 169.1 %all-gather.5.cloned.1.call-start = ((), (), s32[]{:S(2)}) async-start(), calls=%async_computation.2 | async-start | bytes 10948608 | tf_op jit(solution)/shard_map/all_gather | solution.py:640
  20.2 464.7 %reduce-scatter.2.cloned.1.call-start = ((), (), s32[]{:S(2)}) async-start(), calls=%async_computation.3 | async-start | bytes 10948608 | tf_op jit(solution)/shard_map/reduce_scatter | solution.py:725
  20.3 35.9 %collective-permute-start = (bf16[1024,768]{1,0:T(8,128)(2,1)}, bf16[1024,768]{1,0:T(8,128)(2,1)S(1)}, u32[]{:S(2)}, u32[]{:S(2)}) collective-permute-start(bf16[1024,768]{1,0:T(8,128)(2,1)} %bitcast.168), channel_id=1, source_target_pairs={{0,16},{16,0},{1,17},{17,1},{2,18},{18,2},{3,19},{19,3},{4,20},{20... | collective-permute-start | bytes 4718600 | tf_op jit(solution)/shard_map/ppermute | solution.py:512
  24.0 86.1 %copy-start.1 = (s32[2048]{0:T(1024)}, s32[2048]{0:T(1024)S(1)}, u32[]{:S(2)}) copy-start(s32[2048]{0:T(1024)S(1)} %select_reduce_fusion.1) | copy-start | bytes 24580
  25.0 85.2 %copy-start.2 = (s32[8]{0:T(128)}, s32[8]{0:T(128)S(1)}, u32[]{:S(2)}) copy-start(s32[8]{0:T(128)S(1)} %get-tuple-element.96.full_ref) | copy-start | bytes 100
  25.0 85.2 %copy-start.3 = (s32[8]{0:T(128)}, s32[8]{0:T(128)S(1)}, u32[]{:S(2)}) copy-start(s32[8]{0:T(128)S(1)} %and_select_fusion.5.nk_ref) | copy-start | bytes 100
  56.1 6.5 %copy-start.37 = (bf16[1024,768]{1,0:T(8,128)(2,1)}, bf16[1024,768]{1,0:T(8,128)(2,1)S(1)}, u32[]{:S(2)}) copy-start(bf16[1024,768]{1,0:T(8,128)(2,1)S(1)} %collective-permute-done) | copy-start | bytes 4718596
  94.5 9.2 %copy-start.8 = (bf16[2,16,9,24,128]{4,2,3,1,0:T(8,128)(2,1)}, bf16[2,16,9,24,128]{4,2,3,1,0:T(8,128)(2,1)S(1)}, u32[]{:S(2)}) copy-start(bf16[2,16,9,24,128]{4,2,3,1,0:T(8,128)(2,1)S(1)} %pad_maximum_fusion.1) | copy-start | bytes 5308420
  110.1 58.1 %copy-start.4 = (bf16[2048,1152]{1,0:T(8,128)(2,1)}, bf16[2048,1152]{1,0:T(8,128)(2,1)S(1)}, u32[]{:S(2)}) copy-start(bf16[2048,1152]{1,0:T(8,128)(2,1)S(1)} %add_convert_fusion.qkv_ref) | copy-start | bytes 14155780
  170.6 18.0 %copy-start = (bf16[2048,384]{1,0:T(8,128)(2,1)}, bf16[2048,384]{1,0:T(8,128)(2,1)S(1)}, u32[]{:S(2)}) copy-start(bf16[2048,384]{1,0:T(8,128)(2,1)S(1)} %get-tuple-element.59.refs_0_) | copy-start | bytes 4718596
  170.7 17.9 %collective-permute-start.2 = (bf16[1024,384]{1,0:T(8,128)(2,1)S(1)}, bf16[1024,384]{1,0:T(8,128)(2,1)}, u32[]{:S(2)}, u32[]{:S(2)}) collective-permute-start(bf16[1024,384]{1,0:T(8,128)(2,1)S(1)} %slice.271), channel_id=1, source_target_pairs={{0,16},{16,0},{1,17},{17,1},{2,18},{18,2},{3,19},{19,3},{4,20},{20... | collective-permute-start | bytes 2359304 | tf_op jit(solution)/shard_map/ppermute | solution.py:512
  240.9 24.2 %collective-permute-start.5 = (bf16[1024,128]{1,0:T(8,128)(2,1)S(1)}, bf16[1024,128]{1,0:T(8,128)(2,1)S(1)}, u32[]{:S(2)}, u32[]{:S(2)}) collective-permute-start(bf16[1024,128]{1,0:T(8,128)(2,1)S(1)} %get-tuple-element.106), channel_id=1, source_target_pairs={{0,16},{16,0},{1,17},{17,1},{2,18},{18,2},{3,19},{19,3},{4,20},{20... | collective-permute-start | bytes 786440 | tf_op jit(solution)/shard_map/ppermute | solution.py:512
  242.5 23.4 %collective-permute-start.4 = (bf16[1024,128]{1,0:T(8,128)(2,1)S(1)}, bf16[1024,128]{1,0:T(8,128)(2,1)S(1)}, u32[]{:S(2)}, u32[]{:S(2)}) collective-permute-start(bf16[1024,128]{1,0:T(8,128)(2,1)S(1)} %get-tuple-element.105), channel_id=1, source_target_pairs={{0,16},{16,0},{1,17},{17,1},{2,18},{18,2},{3,19},{19,3},{4,20},{20... | collective-permute-start | bytes 786440 | tf_op jit(solution)/shard_map/ppermute | solution.py:512
  243.0 23.8 %collective-permute-start.3 = (bf16[1024,128]{1,0:T(8,128)(2,1)S(1)}, bf16[1024,128]{1,0:T(8,128)(2,1)S(1)}, u32[]{:S(2)}, u32[]{:S(2)}) collective-permute-start(bf16[1024,128]{1,0:T(8,128)(2,1)S(1)} %get-tuple-element.103), channel_id=1, source_target_pairs={{0,16},{16,0},{1,17},{17,1},{2,18},{18,2},{3,19},{19,3},{4,20},{20... | collective-permute-start | bytes 786440 | tf_op jit(solution)/shard_map/ppermute | solution.py:512
  306.2 20.6 %collective-permute-start.6 = (bf16[8,2,200,128]{3,2,1,0:T(8,128)(2,1)S(1)}, bf16[8,2,200,128]{3,2,1,0:T(8,128)(2,1)}, u32[]{:S(2)}, u32[]{:S(2)}) collective-permute-start(bf16[8,2,200,128]{3,2,1,0:T(8,128)(2,1)S(1)} %pad_maximum_fusion.6), channel_id=1, source_target_pairs={{0,1},{1,0},{2,3},{3,2},{4,5},{5,4},{6,7},{7,6},{8,9},{9,8},{10,11... | collective-permute-start | bytes 2457608 | tf_op jit(solution)/shard_map/ppermute | solution.py:516
  307.2 1.5 collective-permute-start.26
  308.7 4.0 collective-permute-start.27
  312.7 3.9 collective-permute-start.28
  316.6 5.5 %collective-permute-start.29 = (f32[7680]{0:T(1024)S(1)}, f32[7680]{0:T(1024)S(1)}, u32[]{:S(2)}, u32[]{:S(2)}) collective-permute-start(f32[7680]{0:T(1024)S(1)} %add.402), channel_id=1, source_target_pairs={{0,8},{2,10},{4,12},{6,14},{8,0},{10,2},{12,4},{14,6},{1,9},{3,11}... | collective-permute-start | bytes 92168 | tf_op jit(solution)/shard_map/ppermute | solution.py:516
  322.2 4.6 collective-permute-start.30
  366.3 16.4 %collective-permute-start.8 = (bf16[8,2,200,128]{3,2,1,0:T(8,128)(2,1)}, bf16[8,2,200,128]{3,2,1,0:T(8,128)(2,1)}, u32[]{:S(2)}, u32[]{:S(2)}) collective-permute-start(bf16[8,2,200,128]{3,2,1,0:T(8,128)(2,1)} %pad_maximum_fusion.5), channel_id=1, source_target_pairs={{0,1},{1,0},{2,3},{3,2},{4,5},{5,4},{6,7},{7,6},{8,9},{9,8},{10,11... | collective-permute-start | bytes 2457608 | tf_op jit(solution)/shard_map/ppermute | solution.py:516
  368.5 14.1 %collective-permute-start.7 = (bf16[4,2,200,128]{3,2,1,0:T(8,128)(2,1)S(1)}, bf16[4,2,200,128]{3,2,1,0:T(8,128)(2,1)S(1)}, u32[]{:S(2)}, u32[]{:S(2)}) collective-permute-start(bf16[4,2,200,128]{3,2,1,0:T(8,128)(2,1)S(1)} %slice.288), channel_id=1, source_target_pairs={{0,2},{2,0},{4,6},{6,4},{8,10},{10,8},{12,14},{14,12},{1,3},{3,1},... | collective-permute-start | bytes 1228808 | tf_op jit(solution)/shard_map/ppermute | solution.py:516
  371.4 13.4 %copy-start.18 = (bf16[2048,1152]{1,0:T(8,128)(2,1)}, bf16[2048,1152]{1,0:T(8,128)(2,1)S(1)}, u32[]{:S(2)}) copy-start(bf16[2048,1152]{1,0:T(8,128)(2,1)S(1)} %constant_dynamic-update-slice_fusion.3) | copy-start | bytes 14155780
  384.8 58.2 %collective-permute-start.10 = (bf16[2,2,200,128]{3,2,1,0:T(8,128)(2,1)}, bf16[2,2,200,128]{3,2,1,0:T(8,128)(2,1)S(1)}, u32[]{:S(2)}, u32[]{:S(2)}) collective-permute-start(bf16[2,2,200,128]{3,2,1,0:T(8,128)(2,1)} %slice.294), channel_id=1, source_target_pairs={{0,4},{2,6},{4,0},{6,2},{8,12},{10,14},{12,8},{14,10},{1,5},{3,7},... | collective-permute-start | bytes 614408 | tf_op jit(solution)/shard_map/ppermute | solution.py:516
  420.2 3.0 collective-permute-start.22
  423.2 7.1 %slice-start = ((s8[4718592]{0:T(1024)(128)(4,1)}), s8[4194304]{0:T(1024)(128)(4,1)S(1)}, s32[]{:S(2)}) async-start(s8[4718592]{0:T(1024)(128)(4,1)} %bitcast.153), calls=%async_computation.4 | async-start | bytes 8388608
  423.2 7.1 %slice-start.1 = ((s8[4718592]{0:T(1024)(128)(4,1)}), s8[524288]{0:T(1024)(128)(4,1)S(1)}, s32[]{:S(2)}) async-start(s8[4718592]{0:T(1024)(128)(4,1)} %bitcast.153), calls=%async_computation.5 | async-start | bytes 1048576
  423.2 7.0 %collective-permute-start.23 = (f32[768]{0:T(1024)S(1)}, f32[768]{0:T(1024)S(1)}, u32[]{:S(2)}, u32[]{:S(2)}) collective-permute-start(f32[768]{0:T(1024)S(1)} %add.392), channel_id=1, source_target_pairs={{0,2},{2,0},{4,6},{6,4},{8,10},{10,8},{12,14},{14,12},{1,3},{3,1},... | collective-permute-start | bytes 9224 | tf_op jit(solution)/shard_map/ppermute | solution.py:516
  430.3 8.1 %collective-permute-start.24 = (f32[768]{0:T(1024)S(1)}, f32[768]{0:T(1024)S(1)}, u32[]{:S(2)}, u32[]{:S(2)}) collective-permute-start(f32[768]{0:T(1024)S(1)} %add.393), channel_id=1, source_target_pairs={{0,4},{2,6},{4,0},{6,2},{8,12},{10,14},{12,8},{14,10},{1,5},{3,7},... | collective-permute-start | bytes 9224 | tf_op jit(solution)/shard_map/ppermute | solution.py:516
  434.6 16.2 %collective-permute-start.12 = (bf16[4,2,200,128]{3,2,1,0:T(8,128)(2,1)}, bf16[4,2,200,128]{3,2,1,0:T(8,128)(2,1)}, u32[]{:S(2)}, u32[]{:S(2)}) collective-permute-start(bf16[4,2,200,128]{3,2,1,0:T(8,128)(2,1)} %slice.299), channel_id=1, source_target_pairs={{0,2},{2,0},{4,6},{6,4},{8,10},{10,8},{12,14},{14,12},{1,3},{3,1},... | collective-permute-start | bytes 1228808 | tf_op jit(solution)/shard_map/ppermute | solution.py:516
  438.4 4.6 collective-permute-start.25
  441.2 10.8 %collective-permute-start.15 = (bf16[8,2,200,128]{3,2,1,0:T(8,128)(2,1)S(1)}, bf16[8,2,200,128]{3,2,1,0:T(8,128)(2,1)S(1)}, u32[]{:S(2)}, u32[]{:S(2)}) collective-permute-start(bf16[8,2,200,128]{3,2,1,0:T(8,128)(2,1)S(1)} %pad_maximum_fusion.4), channel_id=1, source_target_pairs={{0,1},{1,0},{2,3},{3,2},{4,5},{5,4},{6,7},{7,6},{8,9},{9,8},{10,11... | collective-permute-start | bytes 2457608 | tf_op jit(solution)/shard_map/ppermute | solution.py:516
  441.3 37.3 %collective-permute-start.9 = (bf16[1024,768]{1,0:T(8,128)(2,1)S(1)}, bf16[1024,768]{1,0:T(8,128)(2,1)S(1)}, u32[]{:S(2)}, u32[]{:S(2)}) collective-permute-start(bf16[1024,768]{1,0:T(8,128)(2,1)S(1)} %copy-done.36), channel_id=1, source_target_pairs={{0,16},{16,0},{1,17},{17,1},{2,18},{18,2},{3,19},{19,3},{4,20},{20... | collective-permute-start | bytes 4718600 | tf_op jit(solution)/shard_map/ppermute | solution.py:512
  443.1 7.7 %collective-permute-start.11 = (bf16[1,2,200,128]{3,2,1,0:T(8,128)(2,1)S(1)}, bf16[1,2,200,128]{3,2,1,0:T(8,128)(2,1)S(1)}, u32[]{:S(2)}, u32[]{:S(2)}) collective-permute-start(bf16[1,2,200,128]{3,2,1,0:T(8,128)(2,1)S(1)} %slice.359), channel_id=1, source_target_pairs={{0,8},{2,10},{4,12},{6,14},{8,0},{10,2},{12,4},{14,6},{1,9},{3,11}... | collective-permute-start | bytes 307208 | tf_op jit(solution)/shard_map/ppermute | solution.py:516
  451.9 6.7 %collective-permute-start.13 = (bf16[2,2,200,128]{3,2,1,0:T(8,128)(2,1)S(1)}, bf16[2,2,200,128]{3,2,1,0:T(8,128)(2,1)S(1)}, u32[]{:S(2)}, u32[]{:S(2)}) collective-permute-start(bf16[2,2,200,128]{3,2,1,0:T(8,128)(2,1)S(1)} %slice.362), channel_id=1, source_target_pairs={{0,4},{2,6},{4,0},{6,2},{8,12},{10,14},{12,8},{14,10},{1,5},{3,7},... | collective-permute-start | bytes 614408 | tf_op jit(solution)/shard_map/ppermute | solution.py:516
  452.0 26.5 %copy-start.11 = (f32[1024,768]{1,0:T(8,128)S(1)}, f32[1024,768]{1,0:T(8,128)}, u32[]{:S(2)}) copy-start(f32[1024,768]{1,0:T(8,128)} %fusion.7) | copy-start | bytes 9437188
  452.3 26.3 %copy-start.10 = (f32[1024,768]{1,0:T(8,128)S(1)}, f32[1024,768]{1,0:T(8,128)}, u32[]{:S(2)}) copy-start(f32[1024,768]{1,0:T(8,128)} %get-tuple-element.62) | copy-start | bytes 9437188
  452.3 11.1 %collective-permute-start.16 = (bf16[4,2,200,128]{3,2,1,0:T(8,128)(2,1)S(1)}, bf16[4,2,200,128]{3,2,1,0:T(8,128)(2,1)S(1)}, u32[]{:S(2)}, u32[]{:S(2)}) collective-permute-start(bf16[4,2,200,128]{3,2,1,0:T(8,128)(2,1)S(1)} %slice.369), channel_id=1, source_target_pairs={{0,2},{2,0},{4,6},{6,4},{8,10},{10,8},{12,14},{14,12},{1,3},{3,1},... | collective-permute-start | bytes 1228808 | tf_op jit(solution)/shard_map/ppermute | solution.py:516
  453.3 27.5 %collective-permute-start.19 = (bf16[200,128]{1,0:T(8,128)(2,1)S(1)}, bf16[200,128]{1,0:T(8,128)(2,1)S(1)}, u32[]{:S(2)}, u32[]{:S(2)}) collective-permute-start(bf16[200,128]{1,0:T(8,128)(2,1)S(1)} %get-tuple-element.121), channel_id=1, source_target_pairs={{0,16},{16,0},{1,17},{17,1},{2,18},{18,2},{3,19},{19,3},{4,20},{20... | collective-permute-start | bytes 153608 | tf_op jit(solution)/shard_map/ppermute | solution.py:512
  458.7 6.8 %collective-permute-start.14 = (bf16[1,2,200,128]{3,2,1,0:T(8,128)(2,1)S(1)}, bf16[1,2,200,128]{3,2,1,0:T(8,128)(2,1)S(1)}, u32[]{:S(2)}, u32[]{:S(2)}) collective-permute-start(bf16[1,2,200,128]{3,2,1,0:T(8,128)(2,1)S(1)} %slice.364), channel_id=1, source_target_pairs={{0,8},{2,10},{4,12},{6,14},{8,0},{10,2},{12,4},{14,6},{1,9},{3,11}... | collective-permute-start | bytes 307208 | tf_op jit(solution)/shard_map/ppermute | solution.py:516
  463.5 6.1 %collective-permute-start.17 = (bf16[2,2,200,128]{3,2,1,0:T(8,128)(2,1)S(1)}, bf16[2,2,200,128]{3,2,1,0:T(8,128)(2,1)S(1)}, u32[]{:S(2)}, u32[]{:S(2)}) collective-permute-start(bf16[2,2,200,128]{3,2,1,0:T(8,128)(2,1)S(1)} %slice.371), channel_id=1, source_target_pairs={{0,4},{2,6},{4,0},{6,2},{8,12},{10,14},{12,8},{14,10},{1,5},{3,7},... | collective-permute-start | bytes 614408 | tf_op jit(solution)/shard_map/ppermute | solution.py:516
  469.7 6.7 %collective-permute-start.18 = (bf16[1,2,200,128]{3,2,1,0:T(8,128)(2,1)S(1)}, bf16[1,2,200,128]{3,2,1,0:T(8,128)(2,1)S(1)}, u32[]{:S(2)}, u32[]{:S(2)}) collective-permute-start(bf16[1,2,200,128]{3,2,1,0:T(8,128)(2,1)S(1)} %slice.373), channel_id=1, source_target_pairs={{0,8},{2,10},{4,12},{6,14},{8,0},{10,2},{12,4},{14,6},{1,9},{3,11}... | collective-permute-start | bytes 307208 | tf_op jit(solution)/shard_map/ppermute | solution.py:516
  469.8 10.9 %collective-permute-start.20 = (bf16[200,128]{1,0:T(8,128)(2,1)S(1)}, bf16[200,128]{1,0:T(8,128)(2,1)S(1)}, u32[]{:S(2)}, u32[]{:S(2)}) collective-permute-start(bf16[200,128]{1,0:T(8,128)(2,1)S(1)} %get-tuple-element.123), channel_id=1, source_target_pairs={{0,16},{16,0},{1,17},{17,1},{2,18},{18,2},{3,19},{19,3},{4,20},{20... | collective-permute-start | bytes 153608 | tf_op jit(solution)/shard_map/ppermute | solution.py:512
  476.5 4.9 collective-permute-start.21
  (26 other events, 89.9 us)
Sparse Core Ops, SparseCore 0:
  19.6 56.2 all-gather.2
  78.7 85.6 all-gather.4
  267.8 140.3 reduce-scatter.1

commit v3 on v2

v3 whole, which is shorter than its diff:
```python
import functools
import math

import jax
import jax.numpy as jnp
from jax import lax
from jax.experimental import pallas as pl
from jax.experimental.pallas import tpu as pltpu
from jax.sharding import PartitionSpec as P

EPSILON = 1e-06
LOG2E = math.log2(math.e)
MASKED = -1e30
TILE = 256
NT = (((1,), (1,)), ((), ()))
NN = (((1,), (0,)), ((), ()))
TN = (((0,), (0,)), ((), ()))


def dot(a, b, dims=NN):
    return lax.dot_general(a, b, dims, preferred_element_type=jnp.float32)


def local_row(block, seq_index, half_blocks):
    return ((block // half_blocks) ^ seq_index) * (half_blocks * TILE) + (block % half_blocks) * TILE


def split_pair(rows):
    lane = lax.broadcasted_iota(jnp.int32, rows.shape, 1)
    zero = jnp.zeros_like(rows)
    return jnp.where(lane < 64, rows, zero), jnp.where(lane < 64, zero, rows)


CHUNK = 256
UNROLL = 8
BACK = 256
BACK_UNROLL = 4
LINES = 32


def chunk_row(block, seq_index, half_blocks):
    return pl.multiple_of(local_row(block, seq_index, half_blocks), TILE)


def attend_kernel(half_blocks, scale, s_ref, nk_ref, items_ref, qkv_ref, tab_ref, end_ref, att_ref, o32_ref, lse_ref, vt_ref, st_ref, acc_ref, even_ref, odd_ref):
    seq_index = s_ref[0]
    table_size = tab_ref.shape[1]
    per = CHUNK // TILE
    rows = qkv_ref.shape[0]
    pick = split_pair(jnp.ones((128, 128), jnp.bfloat16))
    reach = jnp.zeros((1, 1), jnp.float32)
    for half in pick:
        longest = []
        for at in (0, 128):
            part = qkv_ref[:, at : at + 128].astype(jnp.float32)
            squares = dot((part * part).astype(jnp.bfloat16), half, NT)
            longest.append(jnp.max(squares, keepdims=True))
        reach = jnp.maximum(reach, jnp.sqrt(longest[0]) * jnp.sqrt(longest[1]) * scale)
    small = reach[0, 0] < 80.0
    vt = qkv_ref[:, 256:384].astype(jnp.float32).T
    sub = lax.broadcasted_iota(jnp.int32, vt.shape, 0)
    vt_ref[0, 0:128] = jnp.where(sub < 64, vt, 0.0).astype(jnp.bfloat16)
    vt_ref[1, 0:128] = jnp.where(sub < 64, 0.0, vt).astype(jnp.bfloat16)
    sub = lax.broadcasted_iota(jnp.int32, (16, vt.shape[1]), 0)
    vt_ref[0, 128:144] = jnp.where(sub < 8, 1.0, 0.0).astype(jnp.bfloat16)
    vt_ref[1, 128:144] = jnp.where(sub < 8, 0.0, 1.0).astype(jnp.bfloat16)
    sub = lax.broadcasted_iota(jnp.int32, (CHUNK, TILE), 0)

    def products(block, j):
        queries = split_pair(qkv_ref[pl.ds(chunk_row(block, seq_index, half_blocks), TILE), 0:128])
        keys = qkv_ref[pl.ds(chunk_row((j * per) % (2 * half_blocks), seq_index, half_blocks), CHUNK), 128:256]
        return [dot(keys, queries[h], NT) for h in range(2)]

    def logits(block, j, raw):
        row_end = end_ref[0:1, pl.ds(pl.multiple_of(block * TILE, TILE), TILE)]
        lane0 = pl.multiple_of((block * TILE) % table_size, TILE)
        trow = pl.multiple_of((j * CHUNK) % table_size, CHUNK)
        allowed = sub < row_end - j * CHUNK
        return [
            jnp.where(allowed, raw[h] * scale + tab_ref[h, pl.ds(trow, CHUNK), pl.ds(lane0, TILE)], MASKED)
            for h in range(2)
        ]

    def accumulate(block, j, probs):
        there = chunk_row((j * per) % (2 * half_blocks), seq_index, half_blocks)
        values = jnp.concatenate([vt_ref[h, :, pl.ds(there, CHUNK)] for h in range(2)], axis=1)
        acc_ref[block] += dot(values, jnp.concatenate([p.astype(jnp.bfloat16) for p in probs], axis=0))

    def finish(block, peak):
        here = chunk_row(block, seq_index, half_blocks)
        at = pl.multiple_of(block * TILE, TILE)
        acc = acc_ref[block]
        sums = [acc[128:129], acc[136:137]]
        out = jnp.concatenate([acc[0:64] / sums[0], acc[64:128] / sums[1]], axis=0).T
        o32_ref[pl.ds(here, TILE), :] = out
        att_ref[pl.ds(here, TILE), :] = out.astype(jnp.bfloat16)
        for h in range(2):
            lse_ref[0, h : h + 1, pl.ds(at, TILE)] = peak[h] + jnp.log2(sums[h])

    acc_ref[...] = jnp.zeros_like(acc_ref)

    @pl.when(small)
    def _():
        last = nk_ref.shape[0] - 1
        buffers = (even_ref, odd_ref)

        def prepare(t, to_ref):
            for h, raw in enumerate(products(jnp.minimum(items_ref[0, t], last), items_ref[1, t])):
                to_ref[h] = raw

        def use(t, from_ref):
            block, j = jnp.minimum(items_ref[0, t], last), items_ref[1, t]
            accumulate(block, j, [jnp.exp2(x) for x in logits(block, j, [from_ref[h] for h in range(2)])])

        prepare(0, even_ref)

        def step(i, carry):
            for u in range(0, UNROLL, 2):
                t = UNROLL * i + u
                prepare(t + 1, odd_ref)
                use(t, even_ref)
                prepare(t + 2, even_ref)
                use(t + 1, odd_ref)
            return carry

        lax.fori_loop(0, (items_ref[2, 0] + UNROLL - 1) // UNROLL, step, 0)

        def close(block, carry):
            finish(block, [0.0, 0.0])
            return carry

        lax.fori_loop(0, last + 1, close, 0)

    @pl.when(jnp.logical_not(small))
    def _():
        def query_block(block, carry):
            count = (nk_ref[block] + per - 1) // per

            def score(j, peaks):
                out = []
                for h, x in enumerate(logits(block, j, products(block, j))):
                    st_ref[h, pl.ds(pl.multiple_of(j * CHUNK, CHUNK), CHUNK), :] = x
                    out.append(jnp.maximum(peaks[h], jnp.max(x.reshape(CHUNK // 8, 8, TILE), axis=0)))
                return tuple(out)

            start = jnp.full((8, TILE), MASKED, jnp.float32)
            peaks = lax.fori_loop(0, count, score, (start, start))
            peak = [jnp.max(p, axis=0, keepdims=True) for p in peaks]

            def mix(j, carry):
                at_chunk = pl.ds(pl.multiple_of(j * CHUNK, CHUNK), CHUNK)
                accumulate(block, j, [jnp.exp2(st_ref[h, at_chunk, :] - peak[h]) for h in range(2)])
                return carry

            lax.fori_loop(0, count, mix, 0)
            finish(block, peak)
            return carry

        lax.fori_loop(0, nk_ref.shape[0], query_block, 0)


def work_items(counts, per):
    chunks = (counts + (per - 1)) // per
    ends = jnp.sum(jnp.where(jnp.arange(len(counts))[:, None] >= jnp.arange(len(counts))[None, :], chunks[None, :], 0), axis=1)
    step = jnp.arange(len(counts) * len(counts) // per + 16, dtype=jnp.int32)
    block = jnp.sum((step[:, None] >= ends[None, :]).astype(jnp.int32), axis=1)
    first = jnp.sum(jnp.where(jnp.arange(len(counts))[None, :] < block[:, None], chunks[None, :], 0), axis=1)
    inside = block < len(counts)
    chunk = jnp.where(inside, step - first, len(counts) // per)
    return jnp.stack([jnp.where(inside, block, len(counts)), chunk, jnp.full_like(step, ends[-1])]).astype(jnp.int32)


def attend(qkv, tables, row_end, scalars, score_scale):
    rows = qkv.shape[0]
    pairs = qkv.shape[1] // 384
    tsize = tables.shape[1]
    spec = pltpu.PrefetchScalarGridSpec(
        num_scalar_prefetch=len(scalars),
        grid=(pairs,),
        in_specs=[
            pl.BlockSpec((rows, 384), lambda p, *_: (0, p)),
            pl.BlockSpec((2, tsize, tsize), lambda p, *_: (p, 0, 0)),
            pl.BlockSpec((1, rows), lambda p, *_: (0, 0)),
        ],
        out_specs=[
            pl.BlockSpec((rows, 128), lambda p, *_: (0, p)),
            pl.BlockSpec((rows, 128), lambda p, *_: (0, p)),
            pl.BlockSpec((1, 8, rows), lambda p, *_: (p, 0, 0)),
        ],
        scratch_shapes=[
            pltpu.VMEM((2, 144, rows), jnp.bfloat16),
            pltpu.VMEM((2, rows, TILE), jnp.float32),
            pltpu.VMEM((rows // TILE, 144, TILE), jnp.float32),
            pltpu.VMEM((2, CHUNK, TILE), jnp.float32),
            pltpu.VMEM((2, CHUNK, TILE), jnp.float32),
        ],
    )
    return pl.pallas_call(
        functools.partial(attend_kernel, rows // TILE // 2, score_scale * LOG2E),
        grid_spec=spec,
        out_shape=[
            jax.ShapeDtypeStruct((rows, pairs * 128), jnp.bfloat16),
            jax.ShapeDtypeStruct((rows, pairs * 128), jnp.float32),
            jax.ShapeDtypeStruct((pairs, 8, rows), jnp.float32),
        ],
        compiler_params=pltpu.CompilerParams(dimension_semantics=("arbitrary",), vmem_limit_bytes=40 << 20),
        cost_estimate=pl.CostEstimate(flops=40 * rows * rows * 128, transcendentals=2 * rows * rows, bytes_accessed=8 << 20),
        name="attend",
    )(*scalars, qkv, tables, row_end)


def attend_back_kernel(half_blocks, scale, score_scale, s_ref, items_ref, qkv_ref, grad_ref, o32_ref, tab_ref, end_ref, lse_ref,
                       turned_ref, back_ref, turn_ref, dqkv_ref, parts_ref, gtab_ref, kt_ref, dk_ref, dv_ref,
                       dq_ref, delta_ref, even_ref, odd_ref):
    seq_index = s_ref[0]
    table_size = tab_ref.shape[1]
    per = BACK // TILE
    blocks = 2 * half_blocks
    kt = qkv_ref[:, 128:256].astype(jnp.float32).T
    sub = lax.broadcasted_iota(jnp.int32, kt.shape, 0)
    kt_ref[0] = jnp.where(sub < 64, kt, 0.0).astype(jnp.bfloat16)
    kt_ref[1] = jnp.where(sub < 64, 0.0, kt).astype(jnp.bfloat16)
    dk_ref[...] = jnp.zeros_like(dk_ref)
    dv_ref[...] = jnp.zeros_like(dv_ref)
    dq_ref[...] = jnp.zeros_like(dq_ref)
    gtab_ref[...] = jnp.zeros_like(gtab_ref)
    inner = (grad_ref[...].astype(jnp.float32) * o32_ref[...]).T
    delta_ref[0:1, :] = jnp.sum(inner[0:64], axis=0, keepdims=True)
    delta_ref[1:2, :] = jnp.sum(inner[64:128], axis=0, keepdims=True)
    sub = lax.broadcasted_iota(jnp.int32, (BACK, TILE), 0)

    def item(t):
        block, j = jnp.minimum(items_ref[0, t], blocks - 1), items_ref[1, t]
        here = pl.ds(chunk_row(block, seq_index, half_blocks), TILE)
        there = pl.ds(chunk_row((j * per) % blocks, seq_index, half_blocks), BACK)
        return block, j, here, there

    def prepare(t, to_ref):
        block, j, here, there = item(t)
        queries, grads = split_pair(qkv_ref[here, 0:128]), split_pair(grad_ref[here, :])
        keys, values = qkv_ref[there, 128:256], qkv_ref[there, 256:384]
        for h in range(2):
            to_ref[h] = dot(keys, queries[h], NT)
            to_ref[2 + h] = dot(values, grads[h], NT)

    def use(t, from_ref):
        block, j, here, there = item(t)
        at = pl.ds(pl.multiple_of(block * TILE, TILE), TILE)
        lane0 = pl.ds(pl.multiple_of((block * TILE) % table_size, TILE), TILE)
        trow = pl.ds(pl.multiple_of((j * BACK) % table_size, BACK), BACK)
        allowed = sub < end_ref[0:1, at] - j * BACK
        probs, scores = [], []
        for h in range(2):
            x = from_ref[h] * scale + tab_ref[h, trow, lane0] - lse_ref[0, h : h + 1, at]
            p = jnp.exp2(jnp.where(allowed, x, MASKED))
            d = p * (from_ref[2 + h] - delta_ref[h : h + 1, here])
            gtab_ref[h, trow, lane0] += d
            probs.append(p.astype(jnp.bfloat16))
            scores.append(d.astype(jnp.bfloat16))
        queries, grads = split_pair(qkv_ref[here, 0:128]), split_pair(grad_ref[here, :])
        dv_ref[there, :] += dot(jnp.concatenate(probs, axis=1), jnp.concatenate(grads, axis=0))
        dk_ref[there, :] += dot(jnp.concatenate(scores, axis=1), jnp.concatenate(queries, axis=0))
        kt = jnp.concatenate([kt_ref[h, :, there] for h in range(2)], axis=1)
        dq_ref[block] += dot(kt, jnp.concatenate(scores, axis=0))

    prepare(0, even_ref)

    def step(i, carry):
        for u in range(0, BACK_UNROLL, 2):
            t = BACK_UNROLL * i + u
            prepare(t + 1, odd_ref)
            use(t, even_ref)
            prepare(t + 2, even_ref)
            use(t + 1, odd_ref)
        return carry

    lax.fori_loop(0, (items_ref[2, 0] + BACK_UNROLL - 1) // BACK_UNROLL, step, 0)

    def close(block, carry):
        here = pl.ds(chunk_row(block, seq_index, half_blocks), TILE)
        dqkv_ref[here, 0:128] = (dq_ref[block] * score_scale).T.astype(jnp.bfloat16)
        return carry

    lax.fori_loop(0, blocks, close, 0)
    dqkv_ref[:, 128:256] = (dk_ref[...] * score_scale).astype(jnp.bfloat16)
    dqkv_ref[:, 256:384] = dv_ref[...].astype(jnp.bfloat16)
    owners, lines = 2 * parts_ref.shape[0], parts_ref.shape[3]
    mask_rows = table_size // owners
    share = turned_ref.shape[1] // owners
    table_lines = lines - 3 * LINES
    for h in range(2):
        table = dot(back_ref[...], gtab_ref[h].astype(jnp.bfloat16), NT).astype(jnp.bfloat16)
        table = dot(table, turn_ref[...])
        for i in range(table_size // 128):
            at = (h * (table_size // 128) + i) * mask_rows
            part = table[:, i * 128 : (i + 1) * 128].reshape(owners // 2, 2, mask_rows, 128)
            parts_ref[:, 0, :, at : at + mask_rows, :] = part.astype(jnp.bfloat16)
    bias = jnp.sum(dqkv_ref[...].astype(jnp.float32), axis=0, keepdims=True)
    step = 384 // share
    for i in range(owners // step):
        part = dot(turned_ref[:, i * 384 : (i + 1) * 384], dqkv_ref[...], TN)
        for c in range(3):
            lanes = slice(c * 128, (c + 1) * 128)
            sums = jnp.broadcast_to(bias[:, lanes], (step * (LINES - share), 128))
            block = jnp.concatenate(
                [part[:, lanes].reshape(step, share, 128), sums.reshape(step, LINES - share, 128)], axis=1
            )
            at = table_lines + c * LINES
            block = block.reshape(step // 2, 2, LINES, 128)
            parts_ref[i * step // 2 : (i + 1) * step // 2, 0, :, at : at + LINES, :] = block.astype(jnp.bfloat16)


def attend_back(first, pairs, owners, qkv, grads, o32, tables, row_end, lse, turned, back, turn, scalars, score_scale):
    rows = qkv.shape[0]
    tsize = tables.shape[1]
    width = turned.shape[1]
    lines = 2 * (tsize // owners) * (tsize // 128) + 3 * LINES
    spec = pltpu.PrefetchScalarGridSpec(
        num_scalar_prefetch=len(scalars),
        grid=(pairs,),
        in_specs=[
            pl.BlockSpec((rows, 384), lambda p, *_: (0, first + p)),
            pl.BlockSpec((rows, 128), lambda p, *_: (0, first + p)),
            pl.BlockSpec((rows, 128), lambda p, *_: (0, first + p)),
            pl.BlockSpec((2, tsize, tsize), lambda p, *_: (first + p, 0, 0)),
            pl.BlockSpec((1, rows), lambda p, *_: (0, 0)),
            pl.BlockSpec((1, 8, rows), lambda p, *_: (first + p, 0, 0)),
            pl.BlockSpec((rows, width), lambda p, *_: (0, 0), pipeline_mode=pl.Buffered(1)),
            pl.BlockSpec((tsize, tsize), lambda p, *_: (0, 0), pipeline_mode=pl.Buffered(1)),
            pl.BlockSpec((tsize, tsize), lambda p, *_: (0, 0), pipeline_mode=pl.Buffered(1)),
        ],
        out_specs=[
            pl.BlockSpec((rows, 384), lambda p, *_: (0, p)),
            pl.BlockSpec((owners // 2, 1, 2, lines, 128), lambda p, *_: (0, p, 0, 0, 0)),
        ],
        scratch_shapes=[
            pltpu.VMEM((2, tsize, tsize), jnp.float32),
            pltpu.VMEM((2, 128, rows), jnp.bfloat16),
            pltpu.VMEM((rows, 128), jnp.float32),
            pltpu.VMEM((rows, 128), jnp.float32),
            pltpu.VMEM((rows // TILE, 128, TILE), jnp.float32),
            pltpu.VMEM((8, rows), jnp.float32),
            pltpu.VMEM((4, BACK, TILE), jnp.float32),
            pltpu.VMEM((4, BACK, TILE), jnp.float32),
        ],
    )
    return pl.pallas_call(
        functools.partial(attend_back_kernel, rows // TILE // 2, score_scale * LOG2E, score_scale),
        grid_spec=spec,
        out_shape=[
            jax.ShapeDtypeStruct((rows, pairs * 384), jnp.bfloat16),
            jax.ShapeDtypeStruct((owners // 2, pairs, 2, lines, 128), jnp.bfloat16),
        ],
        compiler_params=pltpu.CompilerParams(dimension_semantics=("arbitrary",), vmem_limit_bytes=56 << 20),
        cost_estimate=pl.CostEstimate(
            flops=pairs * rows * rows, transcendentals=rows * rows // 64, bytes_accessed=1 << 20
        ),
        name="attend_back",
    )(*scalars, qkv, grads, o32, tables, row_end, lse, turned, back, turn)


GELU_A = math.sqrt(2.0 / math.pi)
GELU_B = 0.044715


def row_stats(values):
    center = values - jnp.mean(values, axis=-1, keepdims=True)
    rstdev = lax.rsqrt(jnp.mean(center * center, axis=-1, keepdims=True) + EPSILON)
    return center * rstdev, rstdev


def row_back(gradient, normed, rstdev, gain):
    scaled = gradient * gain
    return rstdev * (
        scaled
        - jnp.mean(scaled, axis=-1, keepdims=True)
        - normed * jnp.mean(scaled * normed, axis=-1, keepdims=True)
    )


def layer_kernel(s_ref, *refs):
    f32, bf16 = jnp.float32, jnp.bfloat16
    (own_ref, their_ref, x_ref, up_ref, wide_ref,
     out_ref, gsum_ref, gatt_ref, att_ref, first_ref, active_ref, ginner_ref, gouter_ref, gproj_ref,
     vsum_ref, slope_ref, acc_ref, n1_ref, f1_ref, vec_ref) = refs
    width = x_ref.shape[1]
    inner = active_ref.shape[1]
    step = width
    vec = lambda i: vec_ref[i : i + 1, :]
    total = lambda value: jnp.sum(value, axis=0, keepdims=True)

    def outer_rows(c):
        return wide_ref[:, pl.ds(pl.multiple_of(width + inner + c * step, 128), width)]

    @pl.when(pl.program_id(0) == 0)
    def _():
        vsum_ref[...] = jnp.zeros_like(vsum_ref)
        vec_ref[...] = wide_ref[:, width + 2 * inner :].astype(f32).T

    first_seq = s_ref[0] == 0
    mine, others = own_ref[...], their_ref[...]

    @pl.when(first_seq)
    def _():
        att_ref[:, : width // 2] = mine
        att_ref[:, width // 2 :] = others

    @pl.when(jnp.logical_not(first_seq))
    def _():
        att_ref[:, : width // 2] = others
        att_ref[:, width // 2 :] = mine

    summed = x_ref[...].astype(f32) + (dot(att_ref[...], wide_ref[:, :width]) + vec(0))
    normed, rstdev1 = row_stats(summed)
    n1_ref[...] = normed
    first = normed * vec(1) + vec(2)
    f1_ref[...] = first
    first_ref[...] = first.astype(bf16)
    acc_ref[...] = jnp.zeros_like(acc_ref)

    def up(c, carry):
        at = pl.ds(pl.multiple_of(c * step, 128), step)
        w_at = pl.ds(pl.multiple_of(width + c * step, 128), step)
        u = dot(first_ref[...], wide_ref[:, w_at]) + vec_ref[pl.ds(6 + c, 1), :]
        square = u * u
        t = jnp.tanh(GELU_A * (u + GELU_B * (square * u)))
        half = 0.5 * (1.0 + t)
        slope_ref[:, at] = half + 0.5 * u * (1.0 - t * t) * (GELU_A * (1.0 + 3.0 * GELU_B * square))
        active = (u * half).astype(bf16)
        active_ref[:, at] = active
        acc_ref[...] += dot(active, outer_rows(c))
        return carry

    lax.fori_loop(0, inner // step, up, 0)
    normed, rstdev = row_stats(f1_ref[...] + (acc_ref[...] + vec(3)))
    out_ref[...] = (normed * vec(4) + vec(5)).astype(bf16)
    gradient = up_ref[...].astype(f32)
    vsum_ref[4:5, :] += total(gradient * normed)
    vsum_ref[5:6, :] += total(gradient)
    grad_sum = row_back(gradient, normed, rstdev, vec(4))
    grad_low = grad_sum.astype(bf16)
    gouter_ref[...] = grad_low
    vsum_ref[3:4, :] += total(grad_low.astype(f32))
    acc_ref[...] = grad_sum

    def down(c, carry):
        at = pl.ds(pl.multiple_of(c * step, 128), step)
        w_at = pl.ds(pl.multiple_of(width + c * step, 128), step)
        g = (dot(gouter_ref[...], outer_rows(c), NT) * slope_ref[:, at]).astype(bf16)
        ginner_ref[:, at] = g
        vsum_ref[pl.ds(6 + c, 1), :] += total(g.astype(f32))
        acc_ref[...] += dot(g, wide_ref[:, w_at], NT)
        return carry

    lax.fori_loop(0, inner // step, down, 0)
    grad_first = acc_ref[...]
    normed = n1_ref[...]
    vsum_ref[1:2, :] += total(grad_first * normed)
    vsum_ref[2:3, :] += total(grad_first)
    grad_summed = row_back(grad_first, normed, rstdev1, vec(1))
    gsum_ref[...] = grad_summed
    grad_low = grad_summed.astype(bf16)
    gproj_ref[...] = grad_low
    vsum_ref[0:1, :] += total(grad_low.astype(f32))
    gatt_ref[...] = dot(grad_low, wide_ref[:, :width], NT).astype(bf16)


def layer(seq_index, own, their, x, upstream, wide):
    rows, width = x.shape
    inner = (wide.shape[1] - width - 128) // 2
    block = 256
    by_rows = lambda size: pl.BlockSpec((block, size), lambda i, *_: (i, 0))
    whole = lambda shape: pl.BlockSpec(shape, lambda i, *_: (0,) * len(shape), pipeline_mode=pl.Buffered(1))
    once = lambda shape: pl.BlockSpec(shape, lambda i, *_: (0, 0))
    spec = pltpu.PrefetchScalarGridSpec(
        num_scalar_prefetch=1,
        grid=(rows // block,),
        in_specs=[by_rows(width // 2)] * 2
        + [by_rows(width), by_rows(width), whole(wide.shape)],
        out_specs=[by_rows(width)] * 5
        + [by_rows(inner)] * 2
        + [by_rows(width)] * 2
        + [once((16, width))],
        scratch_shapes=[pltpu.VMEM((block, inner), jnp.float32)] + [pltpu.VMEM((block, width), jnp.float32)] * 3
        + [pltpu.VMEM((128, width), jnp.float32)],
    )
    shape = lambda size, dtype: jax.ShapeDtypeStruct((rows, size), dtype)
    low = jnp.bfloat16
    return pl.pallas_call(
        layer_kernel,
        grid_spec=spec,
        out_shape=[shape(width, low), shape(width, jnp.float32), shape(width, low), shape(width, low), shape(width, low)]
        + [shape(inner, low)] * 2
        + [shape(width, low)] * 2
        + [jax.ShapeDtypeStruct((16, width), jnp.float32)],
        compiler_params=pltpu.CompilerParams(dimension_semantics=("arbitrary",), vmem_limit_bytes=56 << 20),
        cost_estimate=pl.CostEstimate(
            flops=8 * rows * width * (width // 2 + inner), transcendentals=rows * inner, bytes_accessed=36 << 20
        ),
        name="layer",
    )(seq_index, own, their, x, upstream, wide)


def weights_kernel(s_ref, place_ref, vsum_ref, att_ref, first_ref, active_ref, gproj_ref, gouter_ref, ginner_ref,
                   wide_ref, mine_ref, their_ref):
    bf16 = jnp.bfloat16
    i, c = pl.program_id(0), pl.program_id(1)
    width = gproj_ref.shape[1]
    inner = width * pl.num_programs(1)
    owners, share = mine_ref.shape[0], mine_ref.shape[3]

    @pl.when(c == 0)
    def _():
        wide_ref[:, :width] = dot(att_ref[...], gproj_ref[...], TN).astype(bf16)
        sums = vsum_ref[...]
        sums = jnp.concatenate([sums, jnp.zeros((128 - sums.shape[0], sums.shape[1]), jnp.float32)], axis=0)
        wide_ref[:, width + inner :] = sums.T.astype(bf16)

    at = pl.ds(pl.multiple_of(width * (c + 1), 128), width)
    wide_ref[:, at] = dot(first_ref[...], ginner_ref[...], TN).astype(bf16)
    part = dot(active_ref[...], gouter_ref[...], TN)

    def place(out_ref):
        for k in range(owners):
            rows = part[k * share : (k + 1) * share].astype(bf16)
            for i in range(width // 128):
                out_ref[place_ref[k], i, c] = rows[:, i * 128 : (i + 1) * 128]

    @pl.when(i == s_ref[0])
    def _():
        place(mine_ref)

    @pl.when(i != s_ref[0])
    def _():
        place(their_ref)


def layer_weights(seq_index, places, sums, attended, first, active, gproj, gouter, ginner):
    rows, width = gproj.shape
    inner = ginner.shape[1]
    half = width // 2
    steps = inner // width
    owners = places.shape[0]
    blocks = (owners, width // 128, steps, half // owners, 128)
    spec = pltpu.PrefetchScalarGridSpec(
        num_scalar_prefetch=2,
        grid=(2, steps),
        in_specs=[
            pl.BlockSpec((sums.shape[0], half), lambda i, c, *_: (0, i)),
            pl.BlockSpec((rows, half), lambda i, c, *_: (0, i)),
            pl.BlockSpec((rows, half), lambda i, c, *_: (0, i)),
            pl.BlockSpec((rows, half), lambda i, c, *_: (0, 2 * c + i)),
            pl.BlockSpec((rows, width), lambda i, c, *_: (0, 0)),
            pl.BlockSpec((rows, width), lambda i, c, *_: (0, 0)),
            pl.BlockSpec((rows, width), lambda i, c, *_: (0, c)),
        ],
        out_specs=[
            pl.BlockSpec((half, width + inner + 128), lambda i, c, *_: (0, i)),
            pl.BlockSpec(blocks, lambda i, c, *_: (0, 0, 0, 0, 0)),
            pl.BlockSpec(blocks, lambda i, c, *_: (0, 0, 0, 0, 0)),
        ],
    )
    return pl.pallas_call(
        weights_kernel,
        grid_spec=spec,
        out_shape=[
            jax.ShapeDtypeStruct((half, 2 * (width + inner + 128)), jnp.bfloat16),
            jax.ShapeDtypeStruct(blocks, jnp.bfloat16),
            jax.ShapeDtypeStruct(blocks, jnp.bfloat16),
        ],
        compiler_params=pltpu.CompilerParams(dimension_semantics=("arbitrary", "arbitrary"), vmem_limit_bytes=56 << 20),
        cost_estimate=pl.CostEstimate(
            flops=4 * rows * width * (width // 2 + inner), transcendentals=0, bytes_accessed=32 << 20
        ),
        name="layer_weights",
    )(seq_index, places, sums, attended, first, active, gproj, gouter, ginner)


def matmul(left_side, right_side):
    return jnp.dot(left_side, right_side, preferred_element_type=jnp.float32)


def contract_rows(left_side, right_side):
    return jnp.einsum("rd,re->de", left_side, right_side, preferred_element_type=jnp.float32)


def times_transpose(left_side, right_side):
    return jnp.einsum("re,de->rd", left_side, right_side, preferred_element_type=jnp.float32)


def norm_forward(values, norm_gain, norm_shift):
    center = values - jnp.mean(values, axis=-1, keepdims=True)
    rstdev = lax.rsqrt(jnp.mean(center * center, axis=-1, keepdims=True) + EPSILON)
    normed = center * rstdev
    return (normed * norm_gain + norm_shift, normed, rstdev)


def norm_backward(gradient, normed, rstdev, norm_gain):
    scaled = gradient * norm_gain
    back = rstdev * (
        scaled
        - jnp.mean(scaled, axis=-1, keepdims=True)
        - normed * jnp.mean(scaled * normed, axis=-1, keepdims=True)
    )
    return (back, jnp.sum(gradient * normed, axis=0), jnp.sum(gradient, axis=0))


def swap_seq(value):
    return lax.ppermute(value, "seq", [(0, 1), (1, 0)])


def flip(value, axis, bit):
    return lax.ppermute(value, axis, [(i, i ^ bit) for i in range(lax.axis_size(axis))])


def row_steps():
    bits = [1 << i for i in range(1, lax.axis_size("row").bit_length() - 1)]
    return [("row", bit) for bit in bits], [("row", 1)]


def scatter_order():
    far, near = row_steps()
    return [("core", 1)] + near + far


def coordinates(owner):
    row_size = lax.axis_size("row")
    return {"seq": owner // (2 * row_size), "row": (owner // 2) % row_size, "core": owner % 2}


def places_of(order, count):
    owner = coordinates(jnp.arange(count, dtype=jnp.int32))
    place = jnp.zeros((count,), jnp.int32)
    for step, (axis, bit) in enumerate(order):
        place = place + ((((owner[axis] ^ lax.axis_index(axis)) // bit) & 1) << step)
    return place


def scatter_start(parts, axis, bit):
    half = parts[0].shape[0] // 2
    kept = [part[:half] for part in parts]
    sent = [part[half:] for part in parts]
    joined = lambda values: values[0] if len(values) == 1 else jnp.concatenate(values, axis=1)
    return joined(kept), flip(joined(sent), axis, bit)


def scatter_end(kept, arrived):
    return (kept.astype(jnp.float32) + arrived.astype(jnp.float32)).astype(jnp.bfloat16)


def body(
    incoming_activations,
    upstream_derivative,
    grid_coordinates,
    word_segment_ids,
    asking_matrix,
    asking_shift,
    lookup_matrix,
    content_matrix,
    content_shift,
    mixing_result_matrix,
    mixing_result_shift,
    post_mixing_scaling,
    post_mixing_offset,
    expand_matrix,
    expand_shift,
    contract_matrix,
    contract_shift,
    post_perceptron_scaling,
    post_perceptron_offset,
    pair_gate_scores,
    gate_random_jitter,
    softening_scale,
):
    f32, bf16 = jnp.float32, jnp.bfloat16
    heads = softening_scale.shape[0]
    width = incoming_activations.shape[2]
    rows = incoming_activations.shape[1]
    inner = expand_matrix.shape[1]
    tsize = pair_gate_scores.shape[2]
    score_scale = 1.0 / math.sqrt(width // heads)
    half_width, half_heads = width // 2, heads // 2
    pairs = half_heads // 2
    seq_index = lax.axis_index("seq")
    dp_size = 2 * lax.axis_size("row")
    dp_index = 2 * lax.axis_index("row") + lax.axis_index("core")
    owner = seq_index * dp_size + dp_index
    first_seq = seq_index == 0
    inputs = incoming_activations[0]
    share = asking_matrix.shape[0]
    inner_share = expand_shift.shape[0]
    mask_rows = tsize // (2 * dp_size)
    lanes = tsize // 128

    def seq_ordered(mine, others):
        return jnp.stack([jnp.where(first_seq, mine, others), jnp.where(first_seq, others, mine)])


    packed = jnp.stack(
        [part.reshape(share, 2, pairs, 128) for part in (asking_matrix, lookup_matrix, content_matrix)], axis=3
    )
    packed = packed.transpose(1, 2, 3, 0, 4).reshape(2, 3 * pairs * share, 128)
    lines = jnp.stack([asking_shift, content_shift])
    lines = jnp.pad(lines, ((0, 6), (0, 128 - share)))[None]
    smoothed_gate = jax.nn.sigmoid(
        (pair_gate_scores + gate_random_jitter) / softening_scale[:, None, None]
    )
    mask_low = smoothed_gate.astype(bf16).reshape(2, half_heads, mask_rows, lanes, 128)
    mask_low = mask_low.transpose(0, 1, 3, 2, 4).reshape(2, -1, 128)
    packed = jnp.concatenate([packed, jnp.concatenate([lines, lines], axis=0), mask_low], axis=1)
    kept = lax.dynamic_index_in_dim(packed, seq_index, 0, keepdims=False)
    sent = lax.dynamic_index_in_dim(packed, 1 - seq_index, 0, keepdims=False)
    packed = seq_ordered(kept, swap_seq(sent))
    other_inputs = swap_seq(inputs)
    hidden_blocks = inner_share // share
    hidden = expand_matrix.reshape(share, 2 * dp_size, hidden_blocks, share)
    contract_blocks = contract_matrix.reshape(hidden_blocks, share, width)
    columns = jnp.stack(
        [
            mixing_result_shift,
            post_mixing_scaling,
            post_mixing_offset,
            contract_shift,
            post_perceptron_scaling,
            post_perceptron_offset,
        ]
        + [expand_shift[k * share : (k + 1) * share] for k in range(hidden_blocks)],
        axis=1,
    )
    wide_share = jnp.concatenate(
        [mixing_result_matrix, hidden.transpose(0, 2, 1, 3).reshape(share, inner)]
        + [contract_blocks[k] for k in range(hidden_blocks)]
        + [jnp.pad(columns, ((0, 0), (0, 128 - columns.shape[1])))],
        axis=1,
    )
    wide_share = seq_ordered(wide_share, swap_seq(wide_share))
    wide_share, unused = lax.optimization_barrier((wide_share, packed))
    gathered = lax.all_gather(packed, ("row", "core"), axis=1, tiled=True)
    wide_matrix = lax.all_gather(wide_share, ("row", "core"), axis=1, tiled=True).reshape(width, -1)
    both_inputs = jnp.concatenate([inputs, other_inputs], axis=0)
    start = grid_coordinates[0, 0]
    turned = (jnp.arange(tsize, dtype=jnp.int32) + start) % tsize
    turn = (turned[:, None] == jnp.arange(tsize, dtype=jnp.int32)[None, :]).astype(bf16)
    row = jnp.arange(mask_rows, dtype=jnp.int32)
    table_order = scatter_order()
    table_places = places_of(table_order[::-1], dp_size)
    own_seq = (jnp.arange(2, dtype=jnp.int32) ^ seq_index)[:, None, None]
    input_spots = ((table_places[None, :] * 2 + own_seq[:, :, 0]) * share)[:, :, None] + jnp.arange(share)
    turned_inputs = matmul(
        both_inputs,
        (input_spots.reshape(-1)[:, None] == jnp.arange(width, dtype=jnp.int32)[None, :]).astype(bf16),
    ).astype(bf16)
    table_spots = ((table_places[None, :] * 2 + own_seq[:, :, 0]) * mask_rows)[:, :, None] + row
    table_spots = table_spots.reshape(-1)
    spot_turn = jnp.sum(jnp.where(turn > 0, table_spots[None, :], 0), axis=1)
    turn_back = (jnp.arange(tsize, dtype=jnp.int32)[:, None] == spot_turn[None, :]).astype(bf16)

    gathered, turned_inputs = lax.optimization_barrier((gathered, turned_inputs))
    gathered = gathered.reshape(2, dp_size, -1, 128)
    weight_lines = 3 * pairs * share
    heads_matrix = gathered[:, :, :weight_lines].reshape(2, dp_size, 3 * pairs, share, 128)
    heads_matrix = heads_matrix.transpose(0, 1, 3, 2, 4).reshape(width, 3 * half_width)
    shifts = lax.dynamic_index_in_dim(gathered, seq_index, 0, keepdims=False)
    shifts = shifts[:, weight_lines : weight_lines + 2, :share].astype(f32).transpose(1, 0, 2).reshape(2, pairs, 128)
    own_mask = gathered[:, :, weight_lines + 8 :].reshape(2 * dp_size, half_heads, lanes, mask_rows, 128)
    own_mask = own_mask.transpose(1, 0, 3, 2, 4).reshape(half_heads, tsize, tsize)

    segments = word_segment_ids[0]
    values_range = jnp.arange(8, dtype=jnp.int32)[:, None]
    segment_ends = jnp.sum((segments[None, :] <= values_range).astype(jnp.int32), axis=1)
    row_end = jnp.sum(jnp.where(segments[None, :] == values_range, segment_ends[:, None], 0), axis=0)
    counts = (row_end.reshape(-1, TILE)[:, -1] + (TILE - 1)) // TILE
    tables = jnp.einsum("hab,cb->hca", own_mask, turn, preferred_element_type=f32).astype(bf16)
    tables = jnp.einsum("hca,da->hcd", tables, turn, preferred_element_type=f32) * (4.0 * LOG2E)

    heads_shift = jnp.stack([shifts[0], jnp.zeros_like(shifts[0]), shifts[1]], axis=1)
    heads_rows = (matmul(both_inputs, heads_matrix) + heads_shift.reshape(-1)).astype(bf16)
    seq_scalar = seq_index[None].astype(jnp.int32)
    items = work_items(counts, CHUNK // TILE)
    scalars = (seq_scalar, counts, items)
    back_scalars = (seq_scalar, work_items(counts, BACK // TILE))
    row_end = row_end[None]
    own_attended, wide_attended, logsum = attend(heads_rows, tables, row_end, scalars, score_scale)
    their_attended = swap_seq(own_attended[rows:])

    their_columns = swap_seq(heads_matrix[:, (pairs - 1) * 384 :])

    (layer_out, grad_summed, grad_attended, attended, first_low, active_low, grad_inner_low, grad_outer_low,
     grad_proj_low, vector_sums) = layer(
        seq_scalar,
        own_attended,
        their_attended,
        inputs,
        upstream_derivative[0],
        wide_matrix,
    )
    low, high = grad_attended[:, :half_width], grad_attended[:, half_width:]
    arrived = swap_seq(jnp.where(first_seq, high, low))
    grads_all = jnp.concatenate([jnp.where(first_seq, low, high), arrived], axis=0)
    table_places_here = places_of(table_order[::-1], dp_size)
    wide_grad, outer_mine, outer_theirs = layer_weights(
        seq_scalar, table_places_here, vector_sums, attended, first_low, active_low,
        grad_proj_low, grad_outer_low, grad_inner_low,
    )
    wide_grad, grads_all, outer_mine, outer_theirs = lax.optimization_barrier(
        (wide_grad, grads_all, outer_mine, outer_theirs)
    )
    wide_half = lax.psum_scatter(wide_grad, ("row", "core"), scatter_dimension=0, tiled=True)
    wide_half = wide_half.reshape(share, 2, -1)
    outer_arrived = swap_seq(outer_theirs)

    split = pairs - 1
    back = lambda first, count, grads: attend_back(
        first, count, 2 * dp_size, heads_rows, grads, wide_attended, tables, row_end, logsum,
        turned_inputs, turn_back, turn, back_scalars, score_scale,
    )
    heads_columns = lambda first, last: heads_matrix[:, first * 384 : last * 384]
    early_heads, early_parts = back(0, split, grads_all)
    flat = lambda parts: parts.reshape(dp_size, -1, 128)
    early_heads, early_parts, outer_arrived = lax.optimization_barrier((early_heads, early_parts, outer_arrived))
    outer_parts = scatter_end(outer_mine, outer_arrived)
    parts = scatter_end(*scatter_start([flat(early_parts), flat(outer_parts)], *table_order[0]))
    early_sent = times_transpose(early_heads[rows:], heads_columns(0, split)).astype(bf16)
    grads_all, parts, early_sent = lax.optimization_barrier((grads_all, parts, early_sent))
    early_theirs = swap_seq(early_sent)
    parts, parts_flip = scatter_start([parts], *table_order[1])
    late_heads, late_parts = back(split, 1, grads_all)
    late_heads, late_parts, parts_flip, early_theirs, wide_half = lax.optimization_barrier(
        (late_heads, late_parts, parts_flip, early_theirs, wide_half)
    )
    late_theirs = swap_seq(late_heads[rows:])
    late_parts = flat(late_parts)
    parts = scatter_end(parts, parts_flip)
    for step in table_order:
        late_parts = scatter_end(*scatter_start([late_parts], *step))
    for step in table_order[2:]:
        parts = scatter_end(*scatter_start([parts], *step))
    lines = late_parts.shape[1] // 2
    outer_parts = parts[0, 2 * split * lines :]
    all_parts = jnp.concatenate(
        [parts[0, : 2 * split * lines].reshape(split, 2, lines, 128), late_parts[0].reshape(1, 2, lines, 128)], axis=0
    )
    own_sums, their_sums = all_parts[:, 0], swap_seq(all_parts[:, 1])
    input_grad = (
        grad_summed
        + times_transpose(early_heads[:rows], heads_columns(0, split))
        + times_transpose(late_heads[:rows], heads_columns(split, pairs))
        + early_theirs.astype(f32)
        + times_transpose(late_theirs, their_columns)
    )

    both_sums = jnp.stack(
        [jnp.where(first_seq, own_sums, their_sums), jnp.where(first_seq, their_sums, own_sums)]
    ).astype(f32)
    table_lines = 2 * mask_rows * lanes
    table_grad = both_sums[:, :, :table_lines].reshape(2, pairs, 2, lanes, mask_rows, 128)
    table_grad = table_grad.transpose(0, 1, 2, 4, 3, 5).reshape(heads, mask_rows, tsize)
    mask_logits_gradient = (
        4.0 * table_grad * smoothed_gate * (1.0 - smoothed_gate) / softening_scale[:, None, None]
    )
    heads_lines = both_sums[:, :, table_lines:].reshape(2, pairs, 3, LINES, 128)
    heads_grad = heads_lines[:, :, :, :share].transpose(2, 3, 0, 1, 4).reshape(3, share, width)
    head_bias = own_sums[:, table_lines:].reshape(pairs, 3, LINES, 128)[:, :, share].astype(f32)

    own_half = lax.dynamic_index_in_dim(wide_half, seq_index, 1, keepdims=False)
    their_half = lax.dynamic_index_in_dim(wide_half, 1 - seq_index, 1, keepdims=False)
    wide_sum = own_half.astype(f32) + swap_seq(their_half).astype(f32)

    vector_columns = wide_sum[:, width + inner :]
    piece = lambda index: vector_columns[:, index]

    def bias_piece(index):
        return lax.dynamic_slice_in_dim(head_bias[:, index].reshape(half_width), dp_index * share, share)

    inner_sum = wide_sum[:, width : width + inner].reshape(share, hidden_blocks, 2 * dp_size, share)
    inner_sum = inner_sum.transpose(0, 2, 1, 3).reshape(share, inner)
    outer_sum = outer_parts.reshape(width // 128, inner_share, 128).transpose(1, 0, 2).reshape(inner_share, width)
    outer_sum = outer_sum.astype(f32)
    inner_piece = vector_columns[:, 6 : 6 + hidden_blocks].T.reshape(inner_share)
    return (
        layer_out[None],
        input_grad[None],
        heads_grad[0],
        bias_piece(0),
        heads_grad[1],
        heads_grad[2],
        bias_piece(2),
        wide_sum[:, :width],
        piece(0),
        piece(1),
        piece(2),
        inner_sum,
        inner_piece,
        outer_sum,
        piece(3),
        piece(4),
        piece(5),
        mask_logits_gradient,
    )


def solution(mesh):
    split = jax.sharding.Mesh(
        mesh.devices.reshape(2, -1, 2), ("seq", "row", "core")
    )
    return jax.shard_map(
        body,
        mesh=split,
        in_specs=(
            P(("row", "core"), "seq", None),
            P(("row", "core"), "seq", None),
            P(("row", "core"), None),
            P(("row", "core"), None),
            P(("seq", "row", "core"), None),
            P(("seq", "row", "core")),
            P(("seq", "row", "core"), None),
            P(("seq", "row", "core"), None),
            P(("seq", "row", "core")),
            P(("seq", "row", "core"), None),
            P(("seq", "row", "core")),
            P(("seq", "row", "core")),
            P(("seq", "row", "core")),
            P(("seq", "row", "core"), None),
            P(("seq", "row", "core")),
            P(("seq", "row", "core"), None),
            P(("seq", "row", "core")),
            P(("seq", "row", "core")),
            P(("seq", "row", "core")),
            P(None, ("seq", "row", "core"), None),
            P(None, ("seq", "row", "core"), None),
            P(),
        ),
        out_specs=(
            P(("row", "core"), "seq", None),
            P(("row", "core"), "seq", None),
            P(("seq", "row", "core"), None),
            P(("seq", "row", "core")),
            P(("seq", "row", "core"), None),
            P(("seq", "row", "core"), None),
            P(("seq", "row", "core")),
            P(("seq", "row", "core"), None),
            P(("seq", "row", "core")),
            P(("seq", "row", "core")),
            P(("seq", "row", "core")),
            P(("seq", "row", "core"), None),
            P(("seq", "row", "core")),
            P(("seq", "row", "core"), None),
            P(("seq", "row", "core")),
            P(("seq", "row", "core")),
            P(("seq", "row", "core")),
            P(None, ("seq", "row", "core"), None),
        ),
        check_vma=False,
    )
```

time: 505 us -> 488 us (0.966)
  waiting for transfers between devices: 117 us -> 81.6 us
  Pallas kernels: 230 us -> 242 us
    ppermute x21 -> x8, waiting for transfers between devices: 54.1 us -> 24 us  [flip(): lax.ppermute(value, axis, [(i, i ^ bit) for i in range(lax.axis_size(axis...]
    pallas_call x1, Pallas kernels: 58.1 us -> 75.5 us  [attend(): pl.pallas_call(functools.partial(attend_kernel, rows // TILE // 2, score_...]
    all_gather x2, waiting for transfers between devices: 13.3 us -> 0.75 us  [the longest x1 0.75 us: body(): gathered = lax.all_gather(packed, ('row', 'core'), axis=1, tiled=True)]
    reshape x19 -> x3, local copies, waits for them, and re-layouts: 14.3 us -> 5.35 us  [the longest x1 3.66 us: body(): own_mask.transpose(1, 0, 3, 2, 4).reshape(half_heads, tsize, tsize)]
    ppermute x10 -> x11, waiting for transfers between devices: 49.2 us -> 56.8 us  [swap_seq(): return lax.ppermute(value, 'seq', [(0, 1), (1, 0)])]
    pallas_call x3 -> x2, Pallas kernels: 100 us -> 93.7 us  [attend_back(): pl.pallas_call(functools.partial(attend_back_kernel, rows // TILE // 2, s...]
    slice x19 -> x21, local copies, waits for them, and re-layouts: 5.52 us -> 11.2 us  [the longest x6 2.32 us: scatter_start(): sent = [part[half:] for part in parts]]
    dot_general x2 -> x4, matrix products: 9.17 us -> 14 us  [times_transpose(): jnp.einsum('re,de->rd', left_side, right_side, preferred_element_type=jnp...]
  transfers between devices with their start and end apart: 34 -> 22, of which waited for: 19 -> 11; matrix products, arithmetic and copies ran while one was open for 19% -> 19% of each run, Pallas kernels for 36% -> 40%
where the time goes in v3:
time: 488 us; the launch traced here: 483 us
  Pallas kernels  242 us (50%)
  waiting for transfers between devices  81.6 us (17%)
  local copies, waits for them, and re-layouts  56.1 us (11%)
  matrix products  34.3 us (7%)
  starting transfers between devices  31.3 us (6%)
  other arithmetic  22.5 us (5%)
  between operations  15.1 us (3%)
    pallas_call x2, Pallas kernels, attend_back(): pl.pallas_call(functools.partial(attend_back_kernel, rows // TILE // 2, s...  93.7 us
    pallas_call x1, Pallas kernels, attend(): pl.pallas_call(functools.partial(attend_kernel, rows // TILE // 2, score_...  75.5 us
    ppermute x11, waiting for transfers between devices, swap_seq(): return lax.ppermute(value, 'seq', [(0, 1), (1, 0)])  56.8 us
    pallas_call x1, Pallas kernels, layer(): pl.pallas_call(layer_kernel, grid_spec=spec, out_shape=[shape(width, low)...  51.1 us
    ppermute x8, waiting for transfers between devices, flip(): lax.ppermute(value, axis, [(i, i ^ bit) for i in range(lax.axis_size(axis...  24 us
    pallas_call x1, Pallas kernels, layer_weights(): pl.pallas_call(weights_kernel, grid_spec=spec, out_shape=[jax.ShapeDtypeS...  21.9 us
    ppermute x8, starting transfers between devices, flip(): lax.ppermute(value, axis, [(i, i ^ bit) for i in range(lax.axis_size(axis...  15.7 us
    ppermute x11, starting transfers between devices, swap_seq(): return lax.ppermute(value, 'seq', [(0, 1), (1, 0)])  15.4 us
  transfers between devices with their start and end apart: 22, of which 11 were waited for; matrix products, arithmetic and copies ran while one was open for 19% of the time, Pallas kernels for 40%

profile of v3, /device:TPU:0, one launch (start us, length us, event | category | flops | bytes accessed | tf_op | source)
XLA Modules:
  0.0 483.0 jit_solution(10769082592515426162)
XLA Ops:
  7.3 2.1 fusion.48
  12.8 3.0 collective-permute-start.1
  15.9 4.0 collective-permute-done.1
  24.7 1.8 collective-permute-start.3
  26.5 7.4 %collective-permute-done.3 = bf16[24,7040]{1,0:T(8,128)(2,1)S(1)} collective-permute-done((bf16[24,7040]{1,0:T(8,128)(2,1)S(1)}, bf16[24,7040]{1,0:T(8,128)(2,1)S(1)}, u32[]{:S(2)}, u32[]{:S(2)}) %collective-permute-start.3) | collective-permute-done | bytes 337952 | tf_op jit(solution)/shard_map/ppermute | solution.py:609
  35.0 1.5 collective-permute-start
  41.3 28.8 %collective-permute-done = bf16[1024,768]{1,0:T(8,128)(2,1)} collective-permute-done((bf16[1024,768]{1,0:T(8,128)(2,1)}, bf16[1024,768]{1,0:T(8,128)(2,1)}, u32[]{:S(2)}, u32[]{:S(2)}) %collective-permute-start) | collective-permute-done | bytes 1572896 | tf_op jit(solution)/shard_map/ppermute | solution.py:609
  70.0 6.3 %convolution_convert_fusion.turned_ref = bf16[2048,768]{1,0:T(8,128)(2,1)} fusion(bf16[1024,768]{1,0:T(8,128)(2,1)} %collective-permute-done, bf16[1024,768]{1,0:T(8,128)(2,1)} %bitcast.188, s32[768]{0:T(1024)S(1)} %add.266), kind=kOutput, calls=%fused_computation.3 | convolution fusion | flops 2424373248 | bytes 6294528 | tf_op jit(solution)/shard_map/dot_general | solution.py:580
  77.1 1.6 slice.306
  78.7 4.1 slice.310
  84.1 2.0 copy.147
  86.7 1.8 copy.118
  88.5 3.7 reshape.374
  92.2 8.3 %broadcast_multiply_fusion.tab_ref = f32[6,512,512]{2,1,0:T(8,128)} fusion(bf16[6,512,512]{2,1,0:T(8,128)(2,1)} %reshape.374, s32[512]{0:T(512)S(1)} %add_select_fusion), kind=kOutput, calls=%fused_computation.8 | convolution fusion | flops 3224895488 | bytes 9439232 | tf_op jit(solution)/shard_map/hca,da->hcd/dot_general | solution.py:774
  100.4 5.7 %add_convert_fusion.qkv_ref = bf16[2048,1152]{1,0:T(8,128)(2,1)S(1)} fusion(bf16[768,1152]{1,0:T(8,128)(2,1)S(1)} %bitcast.156, f32[1152]{0:T(1024)S(1)} %add.267, bf16[1024,768]{1,0:T(8,128)(2,1)} %collective-permute-done, bf16[1024,768]{1,0:T(8,128)(2,1)S(1)} %bitcast.190), kind=kOutput, calls=%fused_computation | convolution fusion | flops 3634888704 | bytes 9638400 | tf_op jit(solution)/shard_map/dot_general | solution.py:580
  106.1 75.5 %attend.1 = (bf16[2048,384]{1,0:T(8,128)(2,1)S(1)}, f32[2048,384]{1,0:T(8,128)S(1)}, f32[3,8,2048]{2,1,0:T(8,128)S(1)}) custom-call(s32[1]{0:T(128)} %bitcast.s_ref, s32[8]{0:T(128)S(1)} %and_select_fusion.5.nk_ref, s32[3,80]{1,0:T(4,128)S(1)} %add_add_fusion.items_ref, bf16[2048,1152]{1,0:T(8,128)(2,1)S(1)} %add_convert_fusion.qkv_ref, ...), custom_call_target="tpu_custom_call" | custom-call | flops 21474836480 | bytes 8388608 | tf_op jit(solution)/shard_map/attend/pallas_call | solution.py:198
  181.7 1.7 copy-done.1
  185.4 10.9 %collective-permute-done.2.refs_1_ = bf16[1024,384]{1,0:T(8,128)(2,1)} collective-permute-done((bf16[1024,384]{1,0:T(8,128)(2,1)S(1)}, bf16[1024,384]{1,0:T(8,128)(2,1)}, u32[]{:S(2)}, u32[]{:S(2)}) %collective-permute-start.2) | collective-permute-done | bytes 786464 | tf_op jit(solution)/shard_map/ppermute | solution.py:609
  196.3 51.1 %layer.1 = (bf16[1024,768]{1,0:T(8,128)(2,1)}, f32[1024,768]{1,0:T(8,128)}, bf16[1024,768]{1,0:T(8,128)(2,1)}, bf16[1024,768]{1,0:T(8,128)(2,1)}, bf16[1024,768]...) custom-call(s32[1]{0:T(128)} %bitcast.s_ref, ...), custom_call_target="tpu_custom_call" | custom-call | flops 21743271936 | bytes 37748736 | tf_op jit(solution)/shard_map/layer/pallas_call | solution.py:489
  247.4 1.5 broadcast_select_fusion.1
  250.1 21.9 %layer_weights.1 = (bf16[384,7936]{1,0:T(8,128)(2,1)}, bf16[16,6,4,24,128]{4,3,2,1,0:T(8,128)(2,1)}, bf16[16,6,4,24,128]{4,3,2,1,0:T(8,128)(2,1)}) custom-call(s32[1]{0:T(128)} %bitcast.s_ref, s32[16]{0:T(128)} %get-tuple-element.107.place_ref, f32[16,768]{1,0:T(8,128)} %get-tuple-element.61.vsum_ref, bf16[1024,768]{1,0:T(8,128)(2,1)} %get-tuple-element.62.att_ref, ...), custom_call_target="tpu_custom_call" | custom-call | flops 10871635968 | bytes 33554432 | tf_op jit(solution)/shard_map/layer_weights/pallas_call | solution.py:563
  272.0 1.3 pad_maximum_fusion.4.grad_ref
  276.7 60.7 %attend_back.2 = (bf16[2048,768]{1,0:T(8,128)(2,1)}, bf16[16,2,2,224,128]{4,3,2,1,0:T(8,128)(2,1)}) custom-call(s32[1]{0:T(128)} %bitcast.s_ref, s32[3,80]{1,0:T(4,128)} %copy-done.5, bf16[2048,1152]{1,0:T(8,128)(2,1)} %copy-done, bf16[2048,384]{1,0:T(8,128)(2,1)} %pad_maximum_fusion.4.grad_ref, f32[2048,384]{1,0:T(8,128)} %copy-done.1, ...), custom_call_target="tpu_custom_call" | custom-call | flops 8388608 | bytes 1048576 | tf_op jit(solution)/shard_map/attend_back/pallas_call | solution.py:347
  337.5 2.4 add_convert_fusion.2
  340.3 1.6 copy-done.11
  342.5 1.6 copy-done.30
  344.1 2.6 convolution_convert_fusion.1
  351.3 2.0 slice.314
  354.2 4.8 fusion.9
  359.0 32.9 %attend_back.3 = (bf16[2048,384]{1,0:T(8,128)(2,1)}, bf16[16,1,2,224,128]{4,3,2,1,0:T(8,128)(2,1)}) custom-call(s32[1]{0:T(128)} %bitcast.s_ref, s32[3,80]{1,0:T(4,128)} %copy-done.5, bf16[2048,1152]{1,0:T(8,128)(2,1)} %copy-done, bf16[2048,384]{1,0:T(8,128)(2,1)} %pad_maximum_fusion.4.grad_ref, f32[2048,384]{1,0:T(8,128)} %copy-done.1, ...), custom_call_target="tpu_custom_call" | custom-call | flops 4194304 | bytes 1048576 | tf_op jit(solution)/shard_map/attend_back/pallas_call | solution.py:347
  393.0 1.9 add_convert_fusion.3
  395.9 13.7 %collective-permute-start.11 = (bf16[2,1472,128]{2,1,0:T(8,128)(2,1)}, bf16[2,1472,128]{2,1,0:T(8,128)(2,1)}, u32[]{:S(2)}, u32[]{:S(2)}) collective-permute-start(bf16[2,1472,128]{2,1,0:T(8,128)(2,1)} %slice.316), channel_id=1, source_target_pairs={{0,4},{2,6},{4,0},{6,2},{8,12},{10,14},{12,8},{14,10},{1,5},{3,7},... | collective-permute-start | bytes 2261000 | tf_op jit(solution)/shard_map/ppermute | solution.py:613
  409.6 1.5 fusion.51
  411.2 1.6 collective-permute-start.18
  414.3 2.1 fusion.19
  416.3 2.5 collective-permute-done.18
  420.2 3.3 reshape.381
  423.5 3.8 copy.134
  427.4 4.0 reshape.382
  432.9 1.8 fusion.5
  434.8 1.7 collective-permute-start.14
  436.5 1.3 add_convert_fusion.4
  437.9 8.8 %collective-permute-done.14 = bf16[4,448,128]{2,1,0:T(8,128)(2,1)S(1)} collective-permute-done((bf16[4,448,128]{2,1,0:T(8,128)(2,1)S(1)}, bf16[4,448,128]{2,1,0:T(8,128)(2,1)S(1)}, u32[]{:S(2)}, u32[]{:S(2)}) %collective-permute-start.14) | collective-permute-done | bytes 458784 | tf_op jit(solution)/shard_map/ppermute | solution.py:613
  447.0 4.5 add_bitcast_fusion
  451.5 7.8 %collective-permute-done.15 = bf16[2,448,128]{2,1,0:T(8,128)(2,1)S(1)} collective-permute-done((bf16[2,448,128]{2,1,0:T(8,128)(2,1)S(1)}, bf16[2,448,128]{2,1,0:T(8,128)(2,1)S(1)}, u32[]{:S(2)}, u32[]{:S(2)}) %collective-permute-start.15) | collective-permute-done | bytes 229408 | tf_op jit(solution)/shard_map/ppermute | solution.py:613
  459.7 6.1 %collective-permute-done.16 = bf16[1,448,128]{2,1,0:T(8,128)(2,1)S(1)} collective-permute-done((bf16[1,448,128]{2,1,0:T(8,128)(2,1)S(1)}, bf16[1,448,128]{2,1,0:T(8,128)(2,1)S(1)}, u32[]{:S(2)}, u32[]{:S(2)}) %collective-permute-start.16) | collective-permute-done | bytes 114720 | tf_op jit(solution)/shard_map/ppermute | solution.py:613
  465.8 1.6 collective-permute-start.17
  468.1 3.2 collective-permute-done.17
  (211 shorter events, 42.2 us)
Async XLA Ops:
  7.2 13.5 %copy-start.22 = (bf16[96]{0:T(256)(128)(2,1)S(1)}, bf16[96]{0:T(256)(128)(2,1)}, u32[]{:S(2)}) copy-start(bf16[96]{0:T(256)(128)(2,1)} %param.36) | copy-start | bytes 580
  7.2 14.0 %copy-start.24 = (bf16[24]{0:T(256)(128)(2,1)S(1)}, bf16[24]{0:T(256)(128)(2,1)}, u32[]{:S(2)}) copy-start(bf16[24]{0:T(256)(128)(2,1)} %param.32) | copy-start | bytes 148
  7.2 14.1 %copy-start.25 = (bf16[24]{0:T(256)(128)(2,1)S(1)}, bf16[24]{0:T(256)(128)(2,1)}, u32[]{:S(2)}) copy-start(bf16[24]{0:T(256)(128)(2,1)} %param.33) | copy-start | bytes 148
  7.2 14.2 %copy-start.26 = (bf16[24]{0:T(256)(128)(2,1)S(1)}, bf16[24]{0:T(256)(128)(2,1)}, u32[]{:S(2)}) copy-start(bf16[24]{0:T(256)(128)(2,1)} %param.34) | copy-start | bytes 148
  7.2 14.3 %copy-start.27 = (bf16[24]{0:T(256)(128)(2,1)S(1)}, bf16[24]{0:T(256)(128)(2,1)}, u32[]{:S(2)}) copy-start(bf16[24]{0:T(256)(128)(2,1)} %param.38) | copy-start | bytes 148
  7.2 14.4 %copy-start.28 = (bf16[24]{0:T(256)(128)(2,1)S(1)}, bf16[24]{0:T(256)(128)(2,1)}, u32[]{:S(2)}) copy-start(bf16[24]{0:T(256)(128)(2,1)} %param.39) | copy-start | bytes 148
  7.3 14.5 %copy-start.29 = (bf16[24]{0:T(256)(128)(2,1)S(1)}, bf16[24]{0:T(256)(128)(2,1)}, u32[]{:S(2)}) copy-start(bf16[24]{0:T(256)(128)(2,1)} %param.40) | copy-start | bytes 148
  7.3 14.6 %copy-start.18 = (bf16[24,3072]{1,0:T(8,128)(2,1)S(1)}, bf16[24,3072]{1,0:T(8,128)(2,1)}, u32[]{:S(2)}) copy-start(bf16[24,3072]{1,0:T(8,128)(2,1)} %param.35) | copy-start | bytes 442372
  7.3 69.8 %all-gather.3.cloned.1.call-start = ((), (), s32[]{:S(2)}) async-start(), calls=%async_computation.1 | async-start | bytes 5292032 | tf_op jit(solution)/shard_map/all_gather | solution.py:738
  12.7 11.9 %copy-start.20 = (bf16[24,768]{1,0:T(8,128)(2,1)S(1)}, bf16[24,768]{1,0:T(8,128)(2,1)}, u32[]{:S(2)}) copy-start(bf16[24,768]{1,0:T(8,128)(2,1)} %param.31) | copy-start | bytes 110596
  12.8 11.9 %copy-start.19 = (bf16[96,768]{1,0:T(8,128)(2,1)S(1)}, bf16[96,768]{1,0:T(8,128)(2,1)}, u32[]{:S(2)}) copy-start(bf16[96,768]{1,0:T(8,128)(2,1)} %param.37) | copy-start | bytes 442372
  12.8 7.1 %collective-permute-start.1 = (bf16[608,128]{1,0:T(8,128)(2,1)S(1)}, bf16[608,128]{1,0:T(8,128)(2,1)S(1)}, u32[]{:S(2)}, u32[]{:S(2)}) collective-permute-start(bf16[608,128]{1,0:T(8,128)(2,1)S(1)} %dynamic-slice_bitcast_fusion.2), channel_id=1, source_target_pairs={{0,16},{16,0},{1,17},{17,1},{2,18},{18,2},{3,19},{19,3},{4,20},{20... | collective-permute-start | bytes 466952 | tf_op jit(solution)/shard_map/ppermute | solution.py:609
  20.7 175.6 %all-gather.5.cloned.1.call-start = ((), (), s32[]{:S(2)}) async-start(), calls=%async_computation.2 | async-start | bytes 11489280 | tf_op jit(solution)/shard_map/all_gather | solution.py:739
  23.1 15.3 %copy-start.21 = (s32[1,2048]{1,0:T(1,128)S(1)}, s32[1,2048]{1,0:T(1,128)}, u32[]{:S(2)}) copy-start(s32[1,2048]{1,0:T(1,128)} %param.25) | copy-start | bytes 24580
  24.7 9.2 %collective-permute-start.3 = (bf16[24,7040]{1,0:T(8,128)(2,1)S(1)}, bf16[24,7040]{1,0:T(8,128)(2,1)S(1)}, u32[]{:S(2)}, u32[]{:S(2)}) collective-permute-start(bf16[24,7040]{1,0:T(8,128)(2,1)S(1)} %constant_dynamic-update-slice_fusion), channel_id=1, source_target_pairs={{0,16},{16,0},{1,17},{17,1},{2,18},{18,2},{3,19},{19,3},{4,20},{20... | collective-permute-start | bytes 1013768 | tf_op jit(solution)/shard_map/ppermute | solution.py:609
  34.9 357.0 %reduce-scatter.2.cloned.1.call-start = ((), (), s32[]{:S(2)}) async-start(), calls=%async_computation.3 | async-start | bytes 6475776 | tf_op jit(solution)/shard_map/reduce_scatter | solution.py:808
  35.0 35.0 %collective-permute-start = (bf16[1024,768]{1,0:T(8,128)(2,1)}, bf16[1024,768]{1,0:T(8,128)(2,1)}, u32[]{:S(2)}, u32[]{:S(2)}) collective-permute-start(bf16[1024,768]{1,0:T(8,128)(2,1)} %bitcast.187), channel_id=1, source_target_pairs={{0,16},{16,0},{1,17},{17,1},{2,18},{18,2},{3,19},{19,3},{4,20},{20... | collective-permute-start | bytes 4718600 | tf_op jit(solution)/shard_map/ppermute | solution.py:609
  38.6 67.5 %copy-start.4 = (s32[2048]{0:T(1024)}, s32[2048]{0:T(1024)S(1)}, u32[]{:S(2)}) copy-start(s32[2048]{0:T(1024)S(1)} %select_reduce_fusion.1) | copy-start | bytes 24580
  41.3 64.9 %copy-start.5 = (s32[3,80]{1,0:T(4,128)}, s32[3,80]{1,0:T(4,128)S(1)}, u32[]{:S(2)}) copy-start(s32[3,80]{1,0:T(4,128)S(1)} %add_add_fusion.items_ref) | copy-start | bytes 2884
  78.7 4.1 copy-start.7
  92.2 8.3 %copy-start.10 = (bf16[96,8,9,128]{3,1,2,0:T(8,128)(2,1)S(1)}, bf16[96,8,9,128]{3,1,2,0:T(8,128)(2,1)}, u32[]{:S(2)}) copy-start(bf16[96,8,9,128]{3,1,2,0:T(8,128)(2,1)} %copy.147) | copy-start | bytes 5308420
  92.2 8.3 %copy-start.31 = (bf16[1,1024,768]{2,1,0:T(8,128)(2,1)S(1)}, bf16[1,1024,768]{2,1,0:T(8,128)(2,1)}, u32[]{:S(2)}) copy-start(bf16[1,1024,768]{2,1,0:T(8,128)(2,1)} %param.22) | copy-start | bytes 4718596
  106.1 75.6 %copy-start = (bf16[2048,1152]{1,0:T(8,128)(2,1)}, bf16[2048,1152]{1,0:T(8,128)(2,1)S(1)}, u32[]{:S(2)}) copy-start(bf16[2048,1152]{1,0:T(8,128)(2,1)S(1)} %add_convert_fusion.qkv_ref) | copy-start | bytes 14155780
  184.1 12.2 %copy-start.3 = (bf16[2048,384]{1,0:T(8,128)(2,1)}, bf16[2048,384]{1,0:T(8,128)(2,1)S(1)}, u32[]{:S(2)}) copy-start(bf16[2048,384]{1,0:T(8,128)(2,1)S(1)} %get-tuple-element.57.refs_0_) | copy-start | bytes 4718596
  184.2 12.2 %collective-permute-start.2 = (bf16[1024,384]{1,0:T(8,128)(2,1)S(1)}, bf16[1024,384]{1,0:T(8,128)(2,1)}, u32[]{:S(2)}, u32[]{:S(2)}) collective-permute-start(bf16[1024,384]{1,0:T(8,128)(2,1)S(1)} %slice.242), channel_id=1, source_target_pairs={{0,16},{16,0},{1,17},{17,1},{2,18},{18,2},{3,19},{19,3},{4,20},{20... | collective-permute-start | bytes 2359304 | tf_op jit(solution)/shard_map/ppermute | solution.py:609
  248.9 23.1 %collective-permute-start.4 = (bf16[1024,384]{1,0:T(8,128)(2,1)S(1)}, bf16[1024,384]{1,0:T(8,128)(2,1)S(1)}, u32[]{:S(2)}, u32[]{:S(2)}) collective-permute-start(bf16[1024,384]{1,0:T(8,128)(2,1)S(1)} %get-tuple-element.117), channel_id=1, source_target_pairs={{0,16},{16,0},{1,17},{17,1},{2,18},{18,2},{3,19},{19,3},{4,20},{20... | collective-permute-start | bytes 2359304 | tf_op jit(solution)/shard_map/ppermute | solution.py:609
  273.4 64.1 %collective-permute-start.5 = (bf16[16,6,4,24,128]{4,3,2,1,0:T(8,128)(2,1)}, bf16[16,6,4,24,128]{4,3,2,1,0:T(8,128)(2,1)}, u32[]{:S(2)}, u32[]{:S(2)}) collective-permute-start(bf16[16,6,4,24,128]{4,3,2,1,0:T(8,128)(2,1)} %get-tuple-element.78), channel_id=1, source_target_pairs={{0,16},{16,0},{1,17},{17,1},{2,18},{18,2},{3,19},{19,3},{4,20},{20... | collective-permute-start | bytes 7077896 | tf_op jit(solution)/shard_map/ppermute | solution.py:609
  276.7 60.8 %copy-start.14 = (bf16[16,6,4,24,128]{4,3,2,1,0:T(8,128)(2,1)S(1)}, bf16[16,6,4,24,128]{4,3,2,1,0:T(8,128)(2,1)}, u32[]{:S(2)}) copy-start(bf16[16,6,4,24,128]{4,3,2,1,0:T(8,128)(2,1)} %get-tuple-element.81) | copy-start | bytes 7077892
  342.5 5.5 %collective-permute-start.6 = (bf16[8,1472,128]{2,1,0:T(8,128)(2,1)S(1)}, bf16[8,1472,128]{2,1,0:T(8,128)(2,1)S(1)}, u32[]{:S(2)}, u32[]{:S(2)}) collective-permute-start(bf16[8,1472,128]{2,1,0:T(8,128)(2,1)S(1)} %pad_maximum_fusion.1), channel_id=1, source_target_pairs={{0,1},{1,0},{2,3},{3,2},{4,5},{5,4},{6,7},{7,6},{8,9},{9,8},{10,11... | collective-permute-start | bytes 9043976 | tf_op jit(solution)/shard_map/ppermute | solution.py:613
  348.8 44.2 %collective-permute-start.8 = (bf16[1024,768]{1,0:T(8,128)(2,1)}, bf16[1024,768]{1,0:T(8,128)(2,1)}, u32[]{:S(2)}, u32[]{:S(2)}) collective-permute-start(bf16[1024,768]{1,0:T(8,128)(2,1)} %convolution_convert_fusion.1), channel_id=1, source_target_pairs={{0,16},{16,0},{1,17},{17,1},{2,18},{18,2},{3,19},{19,3},{4,20},{20... | collective-permute-start | bytes 4718600 | tf_op jit(solution)/shard_map/ppermute | solution.py:609
  351.3 41.7 %collective-permute-start.7 = (bf16[4,1472,128]{2,1,0:T(8,128)(2,1)}, bf16[4,1472,128]{2,1,0:T(8,128)(2,1)}, u32[]{:S(2)}, u32[]{:S(2)}) collective-permute-start(bf16[4,1472,128]{2,1,0:T(8,128)(2,1)} %slice.264), channel_id=1, source_target_pairs={{0,2},{2,0},{4,6},{6,4},{8,10},{10,8},{12,14},{14,12},{1,3},{3,1},... | collective-permute-start | bytes 4521992 | tf_op jit(solution)/shard_map/ppermute | solution.py:613
  353.3 93.7 %collective-permute-start.10 = (bf16[768,384]{1,0:T(8,128)(2,1)}, bf16[768,384]{1,0:T(8,128)(2,1)}, u32[]{:S(2)}, u32[]{:S(2)}) collective-permute-start(bf16[768,384]{1,0:T(8,128)(2,1)} %slice.314), channel_id=1, source_target_pairs={{0,16},{16,0},{1,17},{17,1},{2,18},{18,2},{3,19},{19,3},{4,20},{20... | collective-permute-start | bytes 1769480 | tf_op jit(solution)/shard_map/ppermute | solution.py:609
  393.0 16.6 %copy-start.15 = (bf16[16,1,2,224,128]{4,3,2,1,0:T(8,128)(2,1)S(1)}, bf16[16,1,2,224,128]{4,3,2,1,0:T(8,128)(2,1)}, u32[]{:S(2)}) copy-start(bf16[16,1,2,224,128]{4,3,2,1,0:T(8,128)(2,1)} %get-tuple-element.92) | copy-start | bytes 5505028
  394.9 16.3 %copy-start.8 = (bf16[4,1472,128]{2,1,0:T(8,128)(2,1)}, bf16[4,1472,128]{2,1,0:T(8,128)(2,1)S(1)}, u32[]{:S(2)}) copy-start(bf16[4,1472,128]{2,1,0:T(8,128)(2,1)S(1)} %add_convert_fusion.3) | copy-start | bytes 4521988
  394.9 17.8 %copy-start.17 = (bf16[2048,384]{1,0:T(8,128)(2,1)S(1)}, bf16[2048,384]{1,0:T(8,128)(2,1)}, u32[]{:S(2)}) copy-start(bf16[2048,384]{1,0:T(8,128)(2,1)} %get-tuple-element.89) | copy-start | bytes 4718596
  395.9 40.6 %collective-permute-start.11 = (bf16[2,1472,128]{2,1,0:T(8,128)(2,1)}, bf16[2,1472,128]{2,1,0:T(8,128)(2,1)}, u32[]{:S(2)}, u32[]{:S(2)}) collective-permute-start(bf16[2,1472,128]{2,1,0:T(8,128)(2,1)} %slice.316), channel_id=1, source_target_pairs={{0,4},{2,6},{4,0},{6,2},{8,12},{10,14},{12,8},{14,10},{1,5},{3,7},... | collective-permute-start | bytes 2261000 | tf_op jit(solution)/shard_map/ppermute | solution.py:613
  411.1 21.7 %collective-permute-start.13 = (bf16[8,448,128]{2,1,0:T(8,128)(2,1)}, bf16[8,448,128]{2,1,0:T(8,128)(2,1)}, u32[]{:S(2)}, u32[]{:S(2)}) collective-permute-start(bf16[8,448,128]{2,1,0:T(8,128)(2,1)} %bitcast.51), channel_id=1, source_target_pairs={{0,1},{1,0},{2,3},{3,2},{4,5},{5,4},{6,7},{7,6},{8,9},{9,8},{10,11... | collective-permute-start | bytes 2752520 | tf_op jit(solution)/shard_map/ppermute | solution.py:613
  411.2 7.6 %collective-permute-start.18 = (bf16[24,3968]{1,0:T(8,128)(2,1)S(1)}, bf16[24,3968]{1,0:T(8,128)(2,1)S(1)}, u32[]{:S(2)}, u32[]{:S(2)}) collective-permute-start(bf16[24,3968]{1,0:T(8,128)(2,1)S(1)} %dynamic-slice_bitcast_fusion.1), channel_id=1, source_target_pairs={{0,16},{16,0},{1,17},{17,1},{2,18},{18,2},{3,19},{19,3},{4,20},{20... | collective-permute-start | bytes 571400 | tf_op jit(solution)/shard_map/ppermute | solution.py:609
  413.7 33.2 %collective-permute-start.9 = (bf16[1024,384]{1,0:T(8,128)(2,1)}, bf16[1024,384]{1,0:T(8,128)(2,1)}, u32[]{:S(2)}, u32[]{:S(2)}) collective-permute-start(bf16[1024,384]{1,0:T(8,128)(2,1)} %slice.267), channel_id=1, source_target_pairs={{0,16},{16,0},{1,17},{17,1},{2,18},{18,2},{3,19},{19,3},{4,20},{20... | collective-permute-start | bytes 2359304 | tf_op jit(solution)/shard_map/ppermute | solution.py:609
  432.1 4.4 copy-start.9
  432.9 14.1 %copy-start.13 = (f32[1024,768]{1,0:T(8,128)S(1)}, f32[1024,768]{1,0:T(8,128)}, u32[]{:S(2)}) copy-start(f32[1024,768]{1,0:T(8,128)} %fusion.9) | copy-start | bytes 9437188
  434.7 12.3 %copy-start.12 = (f32[1024,768]{1,0:T(8,128)S(1)}, f32[1024,768]{1,0:T(8,128)}, u32[]{:S(2)}) copy-start(f32[1024,768]{1,0:T(8,128)} %get-tuple-element.60) | copy-start | bytes 9437188
  434.8 11.9 %collective-permute-start.14 = (bf16[4,448,128]{2,1,0:T(8,128)(2,1)S(1)}, bf16[4,448,128]{2,1,0:T(8,128)(2,1)S(1)}, u32[]{:S(2)}, u32[]{:S(2)}) collective-permute-start(bf16[4,448,128]{2,1,0:T(8,128)(2,1)S(1)} %slice.321), channel_id=1, source_target_pairs={{0,2},{2,0},{4,6},{6,4},{8,10},{10,8},{12,14},{14,12},{1,3},{3,1},... | collective-permute-start | bytes 1376264 | tf_op jit(solution)/shard_map/ppermute | solution.py:613
  437.8 21.7 %collective-permute-start.12 = (bf16[1,1472,128]{2,1,0:T(8,128)(2,1)S(1)}, bf16[1,1472,128]{2,1,0:T(8,128)(2,1)S(1)}, u32[]{:S(2)}, u32[]{:S(2)}) collective-permute-start(bf16[1,1472,128]{2,1,0:T(8,128)(2,1)S(1)} %slice.318), channel_id=1, source_target_pairs={{0,8},{2,10},{4,12},{6,14},{8,0},{10,2},{12,4},{14,6},{1,9},{3,11}... | collective-permute-start | bytes 1130504 | tf_op jit(solution)/shard_map/ppermute | solution.py:613
  446.9 12.5 %collective-permute-start.15 = (bf16[2,448,128]{2,1,0:T(8,128)(2,1)S(1)}, bf16[2,448,128]{2,1,0:T(8,128)(2,1)S(1)}, u32[]{:S(2)}, u32[]{:S(2)}) collective-permute-start(bf16[2,448,128]{2,1,0:T(8,128)(2,1)S(1)} %slice.323), channel_id=1, source_target_pairs={{0,4},{2,6},{4,0},{6,2},{8,12},{10,14},{12,8},{14,10},{1,5},{3,7},... | collective-permute-start | bytes 688136 | tf_op jit(solution)/shard_map/ppermute | solution.py:613
  459.4 6.3 %collective-permute-start.16 = (bf16[1,448,128]{2,1,0:T(8,128)(2,1)S(1)}, bf16[1,448,128]{2,1,0:T(8,128)(2,1)S(1)}, u32[]{:S(2)}, u32[]{:S(2)}) collective-permute-start(bf16[1,448,128]{2,1,0:T(8,128)(2,1)S(1)} %slice.325), channel_id=1, source_target_pairs={{0,8},{2,10},{4,12},{6,14},{8,0},{10,2},{12,4},{14,6},{1,9},{3,11}... | collective-permute-start | bytes 344072 | tf_op jit(solution)/shard_map/ppermute | solution.py:613
  465.8 5.5 %collective-permute-start.17 = (bf16[3,224,128]{2,1,0:T(8,128)(2,1)S(1)}, bf16[3,224,128]{2,1,0:T(8,128)(2,1)S(1)}, u32[]{:S(2)}, u32[]{:S(2)}) collective-permute-start(bf16[3,224,128]{2,1,0:T(8,128)(2,1)S(1)} %fusion.25), channel_id=1, source_target_pairs={{0,16},{16,0},{1,17},{17,1},{2,18},{18,2},{3,19},{19,3},{4,20},{20... | collective-permute-start | bytes 516104 | tf_op jit(solution)/shard_map/ppermute | solution.py:609
  471.3 3.9 copy-start.16
  (6 other events, 12.8 us)
Sparse Core Ops, SparseCore 0:
  20.8 56.2 all-gather.2
  79.9 88.5 all-gather.4
  273.5 89.3 reduce-scatter.1
